TPU v7x, 32 devices: a whole 2x2x4 slice. The times are simulated.
32 devices in a mesh: grp: 2 (over core), blk: 16 (over z, y, x).
Axes of the slice: x: 2, y: 2, z: 4, core: 2. Of those that a mesh axis runs over, the one named last changes fastest.
Arguments:
- src_feats: bfloat16 [2, 4096, 512], P('grp', 'blk')
- tgt_feats: bfloat16 [2, 4096, 512], P('grp', 'blk')
- proj_weight: bfloat16 [512, 512], replicated, may hold values from -0.25 to 0.25
- match_blocks: int32 [2, 32, 4], P('grp', 'blk'), may hold values from 0 to 31, as said below
- match_count: int32 [2, 32], P('grp', 'blk'), may hold values from 1 to 4
- pair_src: int32 [2, 32, 4, 128], P('grp', 'blk'), may hold values from 0 to 127
- pair_tgt: int32 [2, 32, 4, 128], P('grp', 'blk'), may hold values from 0 to 127
Outputs:
- weight_grad: float32 [512, 512], replicated
- covariance: float32 [2, 512, 512], P('grp')
Inputs may be any that keep to these rules, and one draw needn't show every extreme that they name: `match_blocks`: each row lists 4 different target blocks; for source block s each listed block t has t // 2 at most 1 away from s // 2 along the loop of 16 runs (taken mod 16); unused slots follow the same rule.
All inputs are finite; a program needn't handle non-finite values.
Results may differ from a plain program's by a relative error of at most 0.0052.
Values may be sent and summed in bfloat16 or wider, within the bound.
No kernel may reach another device: no remote copies, remote signals or barrier semaphores. Data moves between devices by JAX's collectives and lax.ppermute only.
A program may use at most 64 MiB of HBM per device.

v0:
```python
import jax
import jax.numpy as jnp
from jax import lax
from jax.sharding import PartitionSpec as P

sharpness_divisor = 0.4
logit_bound = 2.5
norm_eps = 1e-06


def from_behind(shard, axis, by):
    count = lax.axis_size(axis)
    return lax.ppermute(shard, axis, [(i, (i + by) % count) for i in range(count)])


def project(features, weight_mat):
    projected = jnp.dot(features, weight_mat, preferred_element_type=jnp.float32)
    inv_norm = lax.rsqrt(jnp.sum(projected * projected, axis=1, keepdims=True) + norm_eps)
    unit_rows = projected * inv_norm
    return (unit_rows, inv_norm, unit_rows.astype(jnp.bfloat16))


def back_norm(unit_rows, inv_norm, grad_rows):
    inner = jnp.sum(unit_rows * grad_rows, axis=1, keepdims=True)
    return ((grad_rows - unit_rows * inner) * inv_norm).astype(jnp.bfloat16)


def pair_weights(anchor_stack, candidate_stack, onehot, matched):
    similarity_table = (
        jnp.einsum(
            "smd,skd->smk", anchor_stack, candidate_stack, preferred_element_type=jnp.float32
        )
        / sharpness_divisor
    )
    exp_terms = jnp.exp(similarity_table - logit_bound)
    shares = exp_terms / jnp.sum(exp_terms, axis=2, keepdims=True)
    linear_weights = (shares - onehot).astype(jnp.bfloat16)
    return linear_weights * matched.astype(jnp.bfloat16)[:, None, None]


def spread_blocks(target_total, linear_weights, anchor_stack, local_blocks, blocks_dev):
    slot_pieces = (
        jnp.einsum("smk,smd->skd", linear_weights, anchor_stack, preferred_element_type=jnp.float32)
        / sharpness_divisor
    )
    choice_mask = (
        local_blocks[:, None] == jnp.arange(blocks_dev, dtype=jnp.int32)[None, :]
    ).astype(jnp.float32)
    return target_total + jnp.einsum(
        "qm,qoi->moi", choice_mask, slot_pieces, precision=lax.Precision.HIGHEST
    )


def body(src_feats, tgt_feats, proj_weight, match_blocks, match_count, pair_src, pair_tgt):
    src_rows = src_feats[0]
    tgt_rows = tgt_feats[0]
    src_unit, source_inverse_norm, src_half = project(src_rows, proj_weight)
    tgt_unit, tgt_inv, tgt_half = project(tgt_rows, proj_weight)
    local_points = src_rows.shape[0]
    feature_width = src_rows.shape[1]
    blocks_dev = match_blocks.shape[1]
    slot_count = match_blocks.shape[2]
    matched_pair_count = pair_src.shape[3]
    block_points = local_points // blocks_dev
    slot_total = blocks_dev * slot_count
    runs = lax.axis_size("blk")
    reach_runs = runs // 16
    owning_run_index = lax.axis_index("blk")
    src_blocks = src_half.reshape(blocks_dev, block_points, feature_width)
    tgt_blocks = tgt_half.reshape(blocks_dev, block_points, feature_width)
    slot_index = jnp.arange(slot_count, dtype=jnp.int32)
    listed_flat = match_blocks[0].reshape(-1)
    live_flat = (slot_index[None, :] < match_count[0][:, None]).reshape(-1)
    block_base = (jnp.arange(blocks_dev, dtype=jnp.int32) * block_points)[:, None, None]
    row_index = (block_base + pair_src[0]).reshape(-1)
    tgt_table = pair_tgt[0].reshape(slot_total, matched_pair_count)
    query_stack = jnp.take(src_half, row_index, axis=0).reshape(
        slot_total, matched_pair_count, feature_width
    )
    columns = jnp.arange(block_points, dtype=jnp.int32)
    source_onehot = (tgt_table[:, :, None] == columns[None, None, :]).astype(jnp.float32)
    local_listed = listed_flat % blocks_dev
    query_zeros = jnp.zeros((slot_total * matched_pair_count, feature_width), jnp.float32)
    block_zeros = jnp.zeros((blocks_dev, block_points, feature_width), jnp.float32)

    def source_slots(held_tgt, run_id, query_total, target_total):
        matched = (listed_flat // blocks_dev == run_id) & live_flat
        candidate_stack = jnp.take(held_tgt, local_listed, axis=0)
        linear_weights = pair_weights(query_stack, candidate_stack, source_onehot, matched)
        query_part = (
            jnp.einsum(
                "smk,skd->smd", linear_weights, candidate_stack, preferred_element_type=jnp.float32
            )
            / sharpness_divisor
        )
        query_total = query_total + query_part.reshape(
            slot_total * matched_pair_count, feature_width
        )
        return (query_total, target_total)

    pair_table = jnp.concatenate(
        [pair_src[0].reshape(slot_total, matched_pair_count), tgt_table], axis=1
    )
    head_table = jnp.stack([listed_flat, live_flat.astype(jnp.int32)], axis=1)
    owner_base = (jnp.arange(slot_total, dtype=jnp.int32) // slot_count * block_points)[:, None]

    def target_slots(kept_source_rows, pair_rows, list_heads, target_total):
        target_blocks = list_heads[:, 0]
        matched = (target_blocks // blocks_dev == owning_run_index) & (list_heads[:, 1] > 0)
        their_src = pair_rows[:, :matched_pair_count]
        their_tgt = pair_rows[:, matched_pair_count:]
        gather_rows = (owner_base + their_src).reshape(-1)
        anchor_stack = jnp.take(
            kept_source_rows.reshape(local_points, feature_width), gather_rows, axis=0
        ).reshape(slot_total, matched_pair_count, feature_width)
        local_blocks = target_blocks % blocks_dev
        candidate_stack = jnp.take(tgt_blocks, local_blocks, axis=0)
        onehot = (their_tgt[:, :, None] == columns[None, None, :]).astype(jnp.float32)
        linear_weights = pair_weights(anchor_stack, candidate_stack, onehot, matched)
        return spread_blocks(target_total, linear_weights, anchor_stack, local_blocks, blocks_dev)

    def visit_run(held, run_id, totals):
        held_pair, pair_rows, list_heads = held
        query_total, target_total = totals
        query_total, _ = source_slots(held_pair[1], run_id, query_total, block_zeros)
        target_total = target_slots(held_pair[0], pair_rows, list_heads, target_total)
        return (query_total, target_total)

    own_held = (jnp.stack([src_blocks, tgt_blocks]), pair_table, head_table)
    totals = visit_run(own_held, owning_run_index, (query_zeros, block_zeros))

    def advance(offset, loop_state):
        ahead_held, behind_held, running = loop_state
        ahead_held = from_behind((ahead_held[0], ahead_held[1], ahead_held[2]), "blk", 1)
        behind_held = from_behind((behind_held[0], behind_held[1], behind_held[2]), "blk", -1)
        running = visit_run(ahead_held, (owning_run_index - offset) % runs, running)
        running = visit_run(behind_held, (owning_run_index + offset) % runs, running)
        return (ahead_held, behind_held, running)

    _, _, (anchor_loss_slope, grad_target) = lax.fori_loop(
        1, reach_runs + 1, advance, (own_held, own_held, totals)
    )
    grad_source = jax.ops.segment_sum(anchor_loss_slope, row_index, num_segments=local_points)
    src_grad = back_norm(src_unit, source_inverse_norm, grad_source)
    tgt_grad = back_norm(tgt_unit, tgt_inv, grad_target.reshape(local_points, feature_width))
    weight_part = lax.dot_general(
        src_rows, src_grad, (((0,), (0,)), ((), ())), preferred_element_type=jnp.float32
    )
    weight_part = weight_part + lax.dot_general(
        tgt_rows, tgt_grad, (((0,), (0,)), ((), ())), preferred_element_type=jnp.float32
    )
    weight_grad = lax.psum(weight_part, ("grp", "blk"))
    moment = lax.dot_general(
        src_half, src_half, (((0,), (0,)), ((), ())), preferred_element_type=jnp.float32
    )
    moment = moment + lax.dot_general(
        tgt_half, tgt_half, (((0,), (0,)), ((), ())), preferred_element_type=jnp.float32
    )
    moment = moment * (feature_width / (2.0 * local_points * runs))
    covariance = lax.psum(moment, "blk")
    return (weight_grad, covariance[None])


def solution(mesh):
    placed = (
        P("grp", "blk", None),
        P("grp", "blk", None),
        P(),
        P("grp", "blk", None),
        P("grp", "blk"),
        P("grp", "blk", None, None),
        P("grp", "blk", None, None),
    )
    return jax.shard_map(
        body, mesh=mesh, in_specs=placed, out_specs=(P(), P("grp", None, None)), check_vma=False
    )
```

profile of v0, /device:TPU:0, one launch (start us, length us, event | category | flops | bytes accessed | tf_op | source)
XLA Modules:
  0.0 379.4 jit_solution(14157346822565561980)
XLA Ops:
  7.2 0.8 reshape_squeeze.10
  8.0 0.7 fusion.129
  8.9 7.0 %collective-permute-start.4 = (s32[8,2]{0,1:T(2,128)S(1)}, s32[8,2]{0,1:T(2,128)S(1)}, u32[]{:S(2)}, u32[]{:S(2)}) collective-permute-start(s32[8,2]{0,1:T(2,128)S(1)} %pad_add_fusion.1), channel_id=1, source_target_pairs={{0,15},{1,0},{2,1},{3,2},{4,3},{5,4},{6,5},{7,6},{8,7},{9,8},{10,9... | collective-permute-start | bytes 200 | tf_op jit(solution)/shard_map/while/body/eval_jaxpr/ppermute | solution.py:13
  15.9 0.7 pad_add_fusion
  16.6 5.6 %collective-permute-start.5 = (s32[8,256]{1,0:T(8,128)S(1)}, s32[8,256]{1,0:T(8,128)S(1)}, u32[]{:S(2)}, u32[]{:S(2)}) collective-permute-start(s32[8,256]{1,0:T(8,128)S(1)} %pad_add_fusion), channel_id=1, source_target_pairs={{0,15},{1,0},{2,1},{3,2},{4,3},{5,4},{6,5},{7,6},{8,7},{9,8},{10,9... | collective-permute-start | bytes 24584 | tf_op jit(solution)/shard_map/while/body/eval_jaxpr/ppermute | solution.py:13
  22.2 1.3 multiply_reduce_fusion.2
  23.6 1.3 multiply_reduce_fusion.1
  25.1 0.9 pad_maximum_fusion
  26.0 5.6 %collective-permute-start.1 = (bf16[2,2,128,512]{3,2,1,0:T(8,128)(2,1)}, bf16[2,2,128,512]{3,2,1,0:T(8,128)(2,1)}, u32[]{:S(2)}, u32[]{:S(2)}) collective-permute-start(bf16[2,2,128,512]{3,2,1,0:T(8,128)(2,1)} %pad_maximum_fusion), channel_id=1, source_target_pairs={{0,15},{1,0},{2,1},{3,2},{4,3},{5,4},{6,5},{7,6},{8,7},{9,8},{10,9... | collective-permute-start | bytes 1572872 | tf_op jit(solution)/shard_map/while/body/eval_jaxpr/ppermute | solution.py:13
  31.9 1.6 gather_fusion.1
  33.6 1.6 gather_fusion.8
  35.2 1.6 gather_fusion.6
  36.9 4.0 %gather_fusion.4 = bf16[1024,512]{1,0:T(8,128)(2,1)S(1)} fusion(bf16[256,512]{1,0:T(8,128)(2,1)S(1)} %multiply_convert_fusion.2, s32[1024]{0:T(1024)S(1)} %get-tuple-element.77), kind=kCustom, calls=%fused_computation.2.clone | custom fusion | bytes 2101248 | tf_op jit(solution)/shard_map/jit(_take)/gather | solution.py:113
  40.9 5.1 %gather_fusion = bf16[1024,512]{1,0:T(8,128)(2,1)} fusion(bf16[256,512]{1,0:T(8,128)(2,1)S(1)} %multiply_convert_fusion.2, s32[1024]{0:T(1024)S(1)} %get-tuple-element.78), kind=kCustom, calls=%fused_computation.clone | custom fusion | bytes 2101248 | tf_op jit(solution)/shard_map/jit(_take)/gather | solution.py:77
  46.1 2.7 broadcast_select_fusion.5
  48.8 1.3 fusion.32
  50.1 0.5 copy-done.6
  50.6 3.1 fusion.52
  53.7 2.5 fusion.38
  56.2 3.3 convolution_multiply_fusion.2
  59.5 1.1 fusion.130
  60.6 5.1 %gather_fusion.5 = bf16[1024,512]{1,0:T(8,128)(2,1)} fusion(bf16[256,512]{1,0:T(8,128)(2,1)S(1)} %bitcast.154, s32[1024]{0:T(1024)S(1)} %get-tuple-element.86), kind=kCustom, calls=%fused_computation.3.clone | custom fusion | bytes 2101248 | tf_op jit(solution)/shard_map/while/body/eval_jaxpr/jit(_take)/gather | solution.py:113
  65.7 2.4 broadcast_select_fusion.4
  68.1 1.1 fusion.131
  69.1 5.1 %gather_fusion.7 = bf16[1024,512]{1,0:T(8,128)(2,1)} fusion(bf16[256,512]{1,0:T(8,128)(2,1)S(1)} %bitcast.153, s32[1024]{0:T(1024)S(1)} %get-tuple-element.87), kind=kCustom, calls=%fused_computation.4.clone | custom fusion | bytes 2101248 | tf_op jit(solution)/shard_map/while/body/eval_jaxpr/jit(_take)/gather | solution.py:113
  74.2 1.5 broadcast_select_fusion.3
  75.8 0.5 fusion.42
  76.3 0.4 copy-done.9
  76.7 3.1 convolution_multiply_fusion
  79.8 3.9 %fusion.6 = f32[2,128,512]{2,0,1:T(2,128)S(1)} fusion(f32[8,128,512]{2,1,0:T(8,128)} %convolution_multiply_fusion, s32[8]{0:T(128)S(1)} %fusion.117), kind=kOutput, calls=%fused_computation.16 | convolution fusion | flops 12582928 | bytes 2621472 | tf_op jit(solution)/shard_map/while/body/eval_jaxpr/qm,qoi->moi/dot_general | solution.py:49
  83.7 1.3 fusion.40
  85.0 3.3 convolution_multiply_fusion.1
  88.4 3.9 %fusion.8 = f32[2,128,512]{2,0,1:T(2,128)S(1)} fusion(f32[8,128,512]{2,1,0:T(8,128)} %convolution_multiply_fusion.1, s32[8]{0:T(128)S(1)} %fusion.116), kind=kOutput, calls=%fused_computation.18 | convolution fusion | flops 12582928 | bytes 2621472 | tf_op jit(solution)/shard_map/while/body/eval_jaxpr/qm,qoi->moi/dot_general | solution.py:49
  92.3 2.5 fusion.24
  95.3 1.6 gather_fusion.2
  96.9 2.8 fusion.34
  99.7 1.6 gather_fusion.3
  101.3 2.0 fusion.36
  103.3 3.5 fusion.50
  106.8 4.2 %add_multiply_fusion = f32[8,128,512]{2,1,0:T(8,128)} fusion(f32[8,128,512]{2,1,0:T(8,128)} %fusion.52, f32[8,128,512]{2,1,0:T(8,128)} %fusion.50, f32[8,128,128]{1,2,0:T(8,128)S(1)} %fusion.36, bf16[8,128,512]{2,1,0:T(8,128)(2,1)S(1)} %copy-done.1, pred[8]{0:T(512)(128)(4,1)S(1)} %get-tuple-element.90, s32[8,128]{1,0:T(8,128)S(1)} %bitcast.180, ...), kind=kOutput, calls=%fused_computation.22 | convolution fusion | flops 137495680 | bytes 7868440 | tf_op jit(solution)/shard_map/while/body/eval_jaxpr/smk,skd->smd/dot_general | solution.py:91
  111.0 7.6 %scatter_custom_fusion = f32[256,512]{1,0:T(8,128)S(1)} fusion(s32[1024]{0:T(1024)S(1)} %bitcast.181, f32[1024,512]{1,0:T(8,128)} %bitcast.159, f32[]{:T(128)} %constant.155.clone.1), kind=kCustom, calls=%fused_computation.124 | custom fusion | flops 524288 | bytes 524800 | tf_op jit(solution)/shard_map/scatter-add | solution.py:143
  118.8 1.4 fusion.66
  120.2 1.3 fusion.14
  121.9 1.3 fusion.13
  123.3 130.5 %all-reduce.3.cloned.1.call-done = f32[512,512]{0,1:T(8,128)} async-done(((f32[512,512]{0,1:T(8,128)}), f32[512,512]{0,1:T(8,128)}) %all-reduce.3.cloned.1.call-update) | async-done | bytes 1048592 | tf_op jit(solution)/shard_map/psum | solution.py:152
  253.7 2.5 copy.16
  256.3 114.1 %all-reduce.5.cloned.1.call-done = f32[1,512,512]{2,1,0:T(8,128)} async-done(((f32[1,512,512]{2,1,0:T(8,128)}), f32[1,512,512]{2,1,0:T(8,128)}) %all-reduce.5.cloned.1.call-update) | async-done | bytes 1048592 | tf_op jit(solution)/shard_map/psum | solution.py:160
  370.3 2.3 copy.32
  (76 shorter events, 2.0 us)
Async XLA Ops:
  7.2 15.0 %copy-start = (bf16[512,512]{1,0:T(8,128)(2,1)S(1)}, bf16[512,512]{1,0:T(8,128)(2,1)}, u32[]{:S(2)}) copy-start(bf16[512,512]{1,0:T(8,128)(2,1)} %param.13) | copy-start | bytes 1572868
  7.2 246.5 %all-reduce.3.cloned.1.call-start = ((), (), s32[]{:S(2)}) async-start(), calls=%async_computation | async-start | bytes 2097152 | tf_op jit(solution)/shard_map/psum | solution.py:152
  8.9 24.7 %collective-permute-start.4 = (s32[8,2]{0,1:T(2,128)S(1)}, s32[8,2]{0,1:T(2,128)S(1)}, u32[]{:S(2)}, u32[]{:S(2)}) collective-permute-start(s32[8,2]{0,1:T(2,128)S(1)} %pad_add_fusion.1), channel_id=1, source_target_pairs={{0,15},{1,0},{2,1},{3,2},{4,3},{5,4},{6,5},{7,6},{8,7},{9,8},{10,9... | collective-permute-start | bytes 200 | tf_op jit(solution)/shard_map/while/body/eval_jaxpr/ppermute | solution.py:13
  15.9 17.7 %collective-permute-start.2 = (s32[8,2]{0,1:T(2,128)S(1)}, s32[8,2]{0,1:T(2,128)S(1)}, u32[]{:S(2)}, u32[]{:S(2)}) collective-permute-start(s32[8,2]{0,1:T(2,128)S(1)} %pad_add_fusion.1), channel_id=1, source_target_pairs={{0,1},{1,2},{2,3},{3,4},{4,5},{5,6},{6,7},{7,8},{8,9},{9,10},{10,1... | collective-permute-start | bytes 200 | tf_op jit(solution)/shard_map/while/body/eval_jaxpr/ppermute | solution.py:13
  16.6 20.3 %collective-permute-start.5 = (s32[8,256]{1,0:T(8,128)S(1)}, s32[8,256]{1,0:T(8,128)S(1)}, u32[]{:S(2)}, u32[]{:S(2)}) collective-permute-start(s32[8,256]{1,0:T(8,128)S(1)} %pad_add_fusion), channel_id=1, source_target_pairs={{0,15},{1,0},{2,1},{3,2},{4,3},{5,4},{6,5},{7,6},{8,7},{9,8},{10,9... | collective-permute-start | bytes 24584 | tf_op jit(solution)/shard_map/while/body/eval_jaxpr/ppermute | solution.py:13
  22.2 14.7 %collective-permute-start.3 = (s32[8,256]{1,0:T(8,128)S(1)}, s32[8,256]{1,0:T(8,128)S(1)}, u32[]{:S(2)}, u32[]{:S(2)}) collective-permute-start(s32[8,256]{1,0:T(8,128)S(1)} %pad_add_fusion), channel_id=1, source_target_pairs={{0,1},{1,2},{2,3},{3,4},{4,5},{5,6},{6,7},{7,8},{8,9},{9,10},{10,1... | collective-permute-start | bytes 24584 | tf_op jit(solution)/shard_map/while/body/eval_jaxpr/ppermute | solution.py:13
  23.5 8.1 %copy-start.15 = (s32[1,2,4]{2,1,0:T(2,128)S(1)}, s32[1,2,4]{2,1,0:T(2,128)}, u32[]{:S(2)}) copy-start(s32[1,2,4]{2,1,0:T(2,128)} %param.14) | copy-start | bytes 100
  23.5 8.4 %copy-start.11 = (s32[1,2,4,128]{3,2,1,0:T(4,128)S(1)}, s32[1,2,4,128]{3,2,1,0:T(4,128)}, u32[]{:S(2)}) copy-start(s32[1,2,4,128]{3,2,1,0:T(4,128)} %param.16) | copy-start | bytes 12292
  26.0 42.1 %collective-permute-start.1 = (bf16[2,2,128,512]{3,2,1,0:T(8,128)(2,1)}, bf16[2,2,128,512]{3,2,1,0:T(8,128)(2,1)}, u32[]{:S(2)}, u32[]{:S(2)}) collective-permute-start(bf16[2,2,128,512]{3,2,1,0:T(8,128)(2,1)} %pad_maximum_fusion), channel_id=1, source_target_pairs={{0,15},{1,0},{2,1},{3,2},{4,3},{5,4},{6,5},{7,6},{8,7},{9,8},{10,9... | collective-permute-start | bytes 1572872 | tf_op jit(solution)/shard_map/while/body/eval_jaxpr/ppermute | solution.py:13
  33.5 26.0 %collective-permute-start = (bf16[2,2,128,512]{3,2,1,0:T(8,128)(2,1)}, bf16[2,2,128,512]{3,2,1,0:T(8,128)(2,1)}, u32[]{:S(2)}, u32[]{:S(2)}) collective-permute-start(bf16[2,2,128,512]{3,2,1,0:T(8,128)(2,1)} %pad_maximum_fusion), channel_id=1, source_target_pairs={{0,1},{1,2},{2,3},{3,4},{4,5},{5,6},{6,7},{7,8},{8,9},{9,10},{10,1... | collective-permute-start | bytes 1572872 | tf_op jit(solution)/shard_map/while/body/eval_jaxpr/ppermute | solution.py:13
  36.9 22.7 %copy-start.12 = (s32[8,256]{1,0:T(8,128)}, s32[8,256]{1,0:T(8,128)S(1)}, u32[]{:S(2)}) copy-start(s32[8,256]{1,0:T(8,128)S(1)} %collective-permute-done.5) | copy-start | bytes 24580
  36.9 22.7 %copy-start.13 = (s32[8,256]{1,0:T(8,128)}, s32[8,256]{1,0:T(8,128)S(1)}, u32[]{:S(2)}) copy-start(s32[8,256]{1,0:T(8,128)S(1)} %collective-permute-done.3) | copy-start | bytes 24580
  46.1 2.7 copy-start.5
  48.8 1.3 copy-start.10
  48.8 1.8 copy-start.6
  48.8 1.8 copy-start.14
  74.2 1.5 copy-start.4
  75.7 1.0 copy-start.9
  75.8 1.0 slice-start
  79.8 3.9 %copy-start.3 = (bf16[8,128,512]{2,1,0:T(8,128)(2,1)S(1)}, bf16[8,128,512]{2,1,0:T(8,128)(2,1)}, u32[]{:S(2)}) copy-start(bf16[8,128,512]{2,1,0:T(8,128)(2,1)} %gather_fusion.6) | copy-start | bytes 3145732
  79.8 3.9 %copy-start.8 = (bf16[1024,512]{1,0:T(8,128)(2,1)S(1)}, bf16[1024,512]{1,0:T(8,128)(2,1)}, u32[]{:S(2)}) copy-start(bf16[1024,512]{1,0:T(8,128)(2,1)} %broadcast_select_fusion.4) | copy-start | bytes 3145732
  83.7 1.3 slice-start.1
  88.4 3.9 %copy-start.2 = (f32[8,128,512]{2,1,0:T(8,128)S(1)}, f32[8,128,512]{2,1,0:T(8,128)}, u32[]{:S(2)}) copy-start(f32[8,128,512]{2,1,0:T(8,128)} %convolution_multiply_fusion.2) | copy-start | bytes 6291460
  103.3 3.5 copy-start.1
  111.0 9.2 %copy-start.7 = (bf16[1,256,512]{2,1,0:T(8,128)(2,1)S(1)}, bf16[1,256,512]{2,1,0:T(8,128)(2,1)}, u32[]{:S(2)}) copy-start(bf16[1,256,512]{2,1,0:T(8,128)(2,1)} %param.12) | copy-start | bytes 786436
  121.5 248.8 %all-reduce.5.cloned.1.call-start = ((), (), s32[]{:S(2)}) async-start(), calls=%async_computation.1 | async-start | bytes 2097152 | tf_op jit(solution)/shard_map/psum | solution.py:160
Sparse Core Ops, SparseCore 0:
  121.7 132.0 all-reduce.2
  259.0 111.2 all-reduce.4
where the time goes:
time: 380 us; the launch traced here: 379 us
  waiting for transfers between devices  245 us (64%)
  matrix products  48.3 us (13%)
  local copies, waits for them, and re-layouts  36.3 us (10%)
  starting transfers between devices  18.3 us (5%)
  other arithmetic  17.5 us (5%)
  between operations  14.4 us (4%)
    psum x1, waiting for transfers between devices, body(): weight_grad = lax.psum(weight_part, ('grp', 'blk'))  130 us
    psum x1, waiting for transfers between devices, body(): covariance = lax.psum(moment, 'blk')  114 us
    ppermute x6, starting transfers between devices, from_behind(): lax.ppermute(shard, axis, [(i, (i + by) % count) for i in range(count)])  18.2 us
    gather x3, local copies, waits for them, and re-layouts, target_slots(): jnp.take(kept_source_rows.reshape(local_points, feature_width), gather_ro...  14.1 us
    dot_general x3, matrix products, source_slots(): jnp.einsum('smk,skd->smd', linear_weights, candidate_stack, preferred_ele...  10.8 us
    dot_general x6, matrix products, pair_weights(): jnp.einsum('smd,skd->smk', anchor_stack, candidate_stack, preferred_eleme...  10.5 us
    dot_general x3, matrix products, spread_blocks(): jnp.einsum('qm,qoi->moi', choice_mask, slot_pieces, precision=lax.Precisi...  10.3 us
    dot_general x3, matrix products, spread_blocks(): jnp.einsum('smk,smd->skd', linear_weights, anchor_stack, preferred_elemen...  9.73 us
  transfers between devices with their start and end apart: 8, of which 2 were waited for; matrix products, arithmetic and copies ran while one was open for 12% of the time, Pallas kernels for 0%

commit v1 on v0

v1 whole, which is shorter than its diff:
```python
import functools
import jax
import jax.numpy as jnp
from jax import lax
from jax.experimental import pallas as pl
from jax.experimental.pallas import tpu as pltpu
from jax.sharding import PartitionSpec as P

inverse_sharpness = 2.5
logit_bound = 2.5
norm_eps = 1e-06
lane = 128

f32 = jnp.float32
bf16 = jnp.bfloat16


def dot_nn(a, b):
    return lax.dot_general(a, b, (((1,), (0,)), ((), ())), preferred_element_type=f32)


def dot_nt(a, b):
    return lax.dot_general(a, b, (((1,), (1,)), ((), ())), preferred_element_type=f32)


def dot_tn(a, b):
    return lax.dot_general(a, b, (((0,), (0,)), ((), ())), preferred_element_type=f32)


def project(rows, weight):
    projected = dot_nn(rows, weight)
    inv_norm = lax.rsqrt(jnp.sum(projected * projected, axis=1, keepdims=True) + norm_eps)
    return projected * inv_norm, inv_norm


def back_norm(unit, inv_norm, grad):
    inner = jnp.sum(unit * grad, axis=1, keepdims=True)
    return ((grad - unit * inner) * inv_norm).astype(bf16)


def pair_weights(anchors, candidates, counts, block):
    logits = dot_nt(anchors, candidates)
    terms = jnp.exp(logits * inverse_sharpness - logit_bound)
    parts = []
    for first in range(0, candidates.shape[0], block):
        part = terms[:, first : first + block]
        count = counts[:, first : first + block].astype(f32)
        pairs = jnp.sum(count, axis=1, keepdims=True)
        total = jnp.sum(part, axis=1, keepdims=True)
        parts.append((part * (pairs / total) - count).astype(bf16))
    return jnp.concatenate(parts, axis=1)


def pair_counts(src_ref, key_ref, blocks, slots, block, candidates):
    pairs = src_ref.shape[1]
    point = lax.broadcasted_iota(jnp.int32, (block, pairs), 0)
    place = lax.broadcasted_iota(jnp.int32, (candidates * block, pairs), 0)
    rows = []
    for b in range(blocks):
        left = []
        right = []
        for s in range(b * slots, (b + 1) * slots):
            left.append(jnp.where(src_ref[s : s + 1, :] == point, 1.0, 0.0).astype(bf16))
            right.append(jnp.where(key_ref[s : s + 1, :] == place, 1.0, 0.0).astype(bf16))
        rows.append(dot_nt(jnp.concatenate(left, axis=1), jnp.concatenate(right, axis=1)))
    return jnp.concatenate(rows, axis=0)


def own_kernel(
    blocks, slots, block, candidates, scale,
    xs_ref, xt_ref, w_ref, src_ref, key_ref,
    moment_ref, unit_ref, inv_ref, count_ref, grad_ref, part_ref,
):
    weight = w_ref[...]
    src_unit, src_inv = project(xs_ref[...], weight)
    tgt_unit, tgt_inv = project(xt_ref[...], weight)
    zs = src_unit.astype(bf16)
    zt = tgt_unit.astype(bf16)
    unit_ref[...] = src_unit
    inv_ref[...] = jnp.broadcast_to(src_inv, inv_ref.shape)
    moment = (dot_tn(zs, zs) + dot_tn(zt, zt)) * scale
    at = 0
    for r in range(0, moment.shape[0], lane):
        for c in range(r, moment.shape[1], lane):
            moment_ref[at : at + lane, :] = moment[r : r + lane, c : c + lane].astype(bf16)
            at += lane
    counts = pair_counts(src_ref, key_ref, blocks, slots, block, candidates)
    own = blocks * block
    count_ref[...] = counts[:, own:].astype(bf16)
    weights = pair_weights(zs, zt, counts[:, :own], block)
    grad_ref[...] = dot_nn(weights, zt)
    grad_zt = dot_tn(weights, zs) * inverse_sharpness
    part_ref[...] = dot_tn(xt_ref[...], back_norm(tgt_unit, tgt_inv, grad_zt))


def halo_kernel(
    nbrs, block, groups,
    grp_ref, xs_ref, w_ref, unit_ref, inv_ref, count_ref, grad_ref, part_ref, *refs,
):
    nbr_refs = refs[:nbrs]
    keep_ref, send_ref, total_ref = refs[nbrs:]
    weight = w_ref[...]
    rows = jnp.concatenate([r[...] for r in nbr_refs], axis=0)
    tgt_unit, tgt_inv = project(rows, weight)
    zt = tgt_unit.astype(bf16)
    src_unit = unit_ref[...]
    zs = src_unit.astype(bf16)
    weights = pair_weights(zs, zt, count_ref[...], block)
    grad_zs = (grad_ref[...] + dot_nn(weights, zt)) * inverse_sharpness
    grad_zt = dot_tn(weights, zs) * inverse_sharpness
    src_grad = back_norm(src_unit, inv_ref[:, :1], grad_zs)
    tgt_grad = back_norm(tgt_unit, tgt_inv, grad_zt)
    total_ref[...] = part_ref[...] + dot_tn(xs_ref[...], src_grad) + dot_tn(rows, tgt_grad)
    chunk = total_ref.shape[0] // groups
    me = grp_ref[0]
    keep_ref[...] = total_ref[pl.ds(pl.multiple_of(me * chunk, chunk), chunk), :]
    for k in range(1, groups):
        first = lax.rem(me + k, groups) * chunk
        send_ref[k - 1] = total_ref[pl.ds(pl.multiple_of(first, chunk), chunk), :].astype(bf16)


def unpack_kernel(packed_ref, out_ref):
    at = 0
    for r in range(0, out_ref.shape[0], lane):
        for c in range(r, out_ref.shape[1], lane):
            tile = packed_ref[at : at + lane, :].astype(f32)
            out_ref[r : r + lane, c : c + lane] = tile
            if c > r:
                out_ref[c : c + lane, r : r + lane] = tile.T
            at += lane


def body(src_feats, tgt_feats, proj_weight, match_blocks, match_count, pair_src, pair_tgt):
    xs = src_feats[0]
    xt = tgt_feats[0]
    points, width = xs.shape
    blocks, slots, pairs = pair_src.shape[1:]
    block = points // blocks
    runs = lax.axis_size("blk")
    groups = lax.axis_size("grp")
    reach = runs // 16
    run = lax.axis_index("blk")
    grp = lax.axis_index("grp")

    nbrs = []
    for k in range(1, reach + 1):
        nbrs.append(lax.ppermute(xt, "blk", [(i, (i - k) % runs) for i in range(runs)]))
        nbrs.append(lax.ppermute(xt, "blk", [(i, (i + k) % runs) for i in range(runs)]))

    listed = match_blocks[0]
    offset = (listed // blocks - run + reach) % runs - reach
    order = jnp.where(offset > 0, 2 * offset - 1, -2 * offset)
    live = jnp.arange(slots, dtype=jnp.int32)[None, :] < match_count[0][:, None]
    first = (order * blocks + listed % blocks) * block
    keys = jnp.where(live[:, :, None], first[:, :, None] + pair_tgt[0], -1)
    keys = keys.reshape(blocks * slots, pairs)
    sources = pair_src[0].reshape(blocks * slots, pairs)

    candidates = (2 * reach + 1) * blocks
    tiles = width // lane
    packed_rows = tiles * (tiles + 1) // 2 * lane
    chunk = width // groups
    scale = width / (2.0 * points * runs)
    vmem = pl.BlockSpec(memory_space=pltpu.VMEM)
    smem = pl.BlockSpec(memory_space=pltpu.SMEM)

    packed, unit, inv, counts, grad, part = pl.pallas_call(
        functools.partial(own_kernel, blocks, slots, block, candidates, scale),
        out_shape=(
            jax.ShapeDtypeStruct((packed_rows, lane), bf16),
            jax.ShapeDtypeStruct((points, width), f32),
            jax.ShapeDtypeStruct((points, lane), f32),
            jax.ShapeDtypeStruct((points, (candidates - blocks) * block), bf16),
            jax.ShapeDtypeStruct((points, width), f32),
            jax.ShapeDtypeStruct((width, width), f32),
        ),
        in_specs=[vmem] * 5,
        out_specs=(vmem,) * 6,
        name="own",
    )(xs, xt, proj_weight, sources, keys)

    moved = lax.all_to_all(packed.reshape(runs, packed_rows // runs, lane), "blk", 0, 0)
    keep, send = pl.pallas_call(
        functools.partial(halo_kernel, 2 * reach, block, groups),
        out_shape=(
            jax.ShapeDtypeStruct((chunk, width), f32),
            jax.ShapeDtypeStruct((groups - 1, chunk, width), bf16),
        ),
        in_specs=[smem] + [vmem] * (7 + 2 * reach),
        out_specs=(vmem, vmem),
        scratch_shapes=[pltpu.VMEM((width, width), f32)],
        name="halo",
    )(grp.reshape(1), xs, proj_weight, unit, inv, counts, grad, part, *nbrs)

    total = keep
    for k in range(1, groups):
        got = lax.ppermute(send[k - 1], "grp", [(i, (i + k) % groups) for i in range(groups)])
        total = total + got.astype(f32)
    piece = chunk // runs
    spread = lax.all_to_all(total.astype(bf16).reshape(runs, piece, width), "blk", 0, 0)
    mine = jnp.sum(spread.astype(f32), axis=0).astype(bf16)
    whole = lax.all_to_all(jnp.broadcast_to(mine, (runs, piece, width)), "blk", 0, 0)
    half = whole.reshape(chunk, width)
    parts = [half]
    for k in range(1, groups):
        parts.append(lax.ppermute(half, "grp", [(i, (i - k) % groups) for i in range(groups)]))
    if groups == 2:
        low = jnp.where(grp == 0, parts[0], parts[1])
        high = jnp.where(grp == 0, parts[1], parts[0])
        weight_grad = jnp.concatenate([low, high], axis=0).astype(f32)
    else:
        stacked = jnp.stack(parts)
        place = (jnp.arange(groups, dtype=jnp.int32) - grp) % groups
        weight_grad = jnp.take(stacked, place, axis=0).reshape(width, width).astype(f32)

    mine_c = jnp.sum(moved.astype(f32), axis=0).astype(bf16)
    packed_all = lax.all_to_all(
        jnp.broadcast_to(mine_c, (runs, packed_rows // runs, lane)), "blk", 0, 0
    )
    covariance = pl.pallas_call(
        unpack_kernel,
        out_shape=jax.ShapeDtypeStruct((width, width), f32),
        in_specs=[vmem],
        out_specs=vmem,
        name="unpack",
    )(packed_all.reshape(packed_rows, lane))
    return (weight_grad, covariance[None])


def solution(mesh):
    placed = (
        P("grp", "blk", None),
        P("grp", "blk", None),
        P(),
        P("grp", "blk", None),
        P("grp", "blk"),
        P("grp", "blk", None, None),
        P("grp", "blk", None, None),
    )
    return jax.shard_map(
        body, mesh=mesh, in_specs=placed, out_specs=(P(), P("grp", None, None)), check_vma=False
    )
```

time: 380 us -> 88.5 us (0.23)
  waiting for transfers between devices: 245 us -> 36 us
  matrix products: 48.3 us -> 0 us
  local copies, waits for them, and re-layouts: 36.3 us -> 5.14 us
  other arithmetic: 17.5 us -> 3.12 us
  between operations: 14.4 us -> 0.7 us
  blocking collectives: 0 us -> 13.6 us
  Pallas kernels: 0 us -> 11.6 us
    psum x2 -> x0, waiting for transfers between devices: 245 us -> none  [the longest x1 130 us: body(): weight_grad = lax.psum(weight_part, ('grp', 'blk'))]
    dot_general x21 -> x0, matrix products: 48.3 us -> none  [the longest x3 10.8 us: source_slots(): jnp.einsum('smk,skd->smd', linear_weights, candidate_stack, preferred_ele...]
    all_to_all x0 -> x3, waiting for transfers between devices: none -> 30.2 us  [the longest x1 10.8 us: body(): lax.all_to_all(packed.reshape(runs, packed_rows // runs, lane), 'blk', 0, 0)]
    gather x9 -> x0, local copies, waits for them, and re-layouts: 27.2 us -> none  [the longest x3 14.1 us: target_slots(): jnp.take(kept_source_rows.reshape(local_points, feature_width), gather_ro...]
    all_to_all x0 -> x1, blocking collectives: none -> 13.6 us  [body(): lax.all_to_all(total.astype(bf16).reshape(runs, piece, width), 'blk', 0, 0)]
    pallas_call x0 -> x3, Pallas kernels: none -> 11.6 us  [the longest x1 4.94 us: body(): pl.pallas_call(functools.partial(halo_kernel, 2 * reach, block, groups),...]
    ppermute x6 -> x4, starting transfers between devices: 18.2 us -> 7.09 us  [the longest x1 7.01 us: body(): lax.ppermute(xt, 'blk', [(i, (i - k) % runs) for i in range(runs)])]
    all_to_all x0 -> x3, starting transfers between devices: none -> 10.6 us  [the longest x1 3.55 us: body(): lax.all_to_all(packed.reshape(runs, packed_rows // runs, lane), 'blk', 0, 0)]
  transfers between devices with their start and end apart: 8 -> 7, of which waited for: 2 -> 5; matrix products, arithmetic and copies ran while one was open for 12% -> 1% of each run, Pallas kernels for 0% -> 8%
where the time goes in v1:
time: 88.5 us; the launch traced here: 87.9 us
  waiting for transfers between devices  36 us (41%)
  starting transfers between devices  17.7 us (20%)
  blocking collectives  13.6 us (15%)
  Pallas kernels  11.6 us (13%)
  local copies, waits for them, and re-layouts  5.14 us (6%)
  other arithmetic  3.12 us (4%)
    all_to_all x1, blocking collectives, body(): lax.all_to_all(total.astype(bf16).reshape(runs, piece, width), 'blk', 0, 0)  13.6 us
    all_to_all x1, waiting for transfers between devices, body(): lax.all_to_all(packed.reshape(runs, packed_rows // runs, lane), 'blk', 0, 0)  10.8 us
    all_to_all x1, waiting for transfers between devices, body(): lax.all_to_all(jnp.broadcast_to(mine_c, (runs, packed_rows // runs, lane)...  10.5 us
    all_to_all x1, waiting for transfers between devices, body(): lax.all_to_all(jnp.broadcast_to(mine, (runs, piece, width)), 'blk', 0, 0)  8.96 us
    ppermute x1, starting transfers between devices, body(): lax.ppermute(xt, 'blk', [(i, (i - k) % runs) for i in range(runs)])  7.01 us
    pallas_call x1, Pallas kernels, body(): pl.pallas_call(functools.partial(halo_kernel, 2 * reach, block, groups),...  4.94 us
    pallas_call x1, Pallas kernels, body(): pl.pallas_call(functools.partial(own_kernel, blocks, slots, block, candid...  4.57 us
    ppermute x1, waiting for transfers between devices, body(): lax.ppermute(xt, 'blk', [(i, (i + k) % runs) for i in range(runs)])  4.06 us
  transfers between devices with their start and end apart: 7, of which 5 were waited for; matrix products, arithmetic and copies ran while one was open for 1% of the time, Pallas kernels for 8%

profile of v1, /device:TPU:0, one launch (start us, length us, event | category | flops | bytes accessed | tf_op | source)
XLA Modules:
  0.0 87.9 jit_solution(16424651377347350243)
XLA Ops:
  0.6 7.0 %collective-permute-start = (bf16[256,512]{1,0:T(8,128)(2,1)}, bf16[256,512]{1,0:T(8,128)(2,1)S(1)}, u32[]{:S(2)}, u32[]{:S(2)}) collective-permute-start(bf16[256,512]{1,0:T(8,128)(2,1)} %bitcast.20), channel_id=1, source_target_pairs={{0,15},{1,0},{2,1},{3,2},{4,3},{5,4},{6,5},{7,6},{8,7},{9,8},{10,9... | collective-permute-start | bytes 786440 | tf_op jit(solution)/shard_map/ppermute | solution.py:147
  7.6 0.0 collective-permute-start.1
  7.6 0.0 copy-start.4
  7.6 0.7 copy-done.4
  8.3 0.1 squeeze.17
  8.4 0.0 copy-start.5
  8.4 0.7 copy-done.5
  9.1 0.1 iota_compare_fusion
  9.2 0.1 lt.36
  9.2 0.0 copy-start.3
  9.2 0.7 copy-done.3
  9.9 0.6 add_select_fusion.key_ref
  10.6 4.6 %own.1 = (bf16[1280,128]{1,0:T(8,128)(2,1)}, f32[256,512]{1,0:T(8,128)}, f32[256,128]{1,0:T(8,128)}, bf16[256,512]{1,0:T(8,128)(2,1)}, f32[256,512]{1,0:T(8,128)}, /*index=5*/f32[512,512]{1,0:T(8,128)}) custom-call(bf16[256,512]{1,0:T(8,128)(2,1)} %bitcast.16, bf16[256,512]{1,0:T(8,128)(2,1)} %bitcast.22, bf16[512,512]{1,0:T(8,128)(2,1)} %w_ref.3, ...), custom_call_target="tpu_custom_call" | custom-call | tf_op jit(solution)/shard_map/own/pallas_call | solution.py:167
  15.2 0.0 collective-permute-done.refs_0_
  15.2 0.0 copy-start.1
  15.2 4.1 %collective-permute-done.1.refs_1_ = bf16[256,512]{1,0:T(8,128)(2,1)S(1)} collective-permute-done((bf16[256,512]{1,0:T(8,128)(2,1)}, bf16[256,512]{1,0:T(8,128)(2,1)S(1)}, u32[]{:S(2)}, u32[]{:S(2)}) %collective-permute-start.1) | collective-permute-done | bytes 262176 | tf_op jit(solution)/shard_map/ppermute | solution.py:148
  19.2 0.0 copy-start.2
  19.2 0.0 copy-done.1
  19.2 0.7 copy-done.2
  19.9 4.9 %halo.1 = (f32[256,512]{1,0:T(8,128)}, bf16[1,256,512]{2,1,0:T(8,128)(2,1)}) custom-call(s32[1]{0:T(128)} %bitcast.grp_ref, bf16[256,512]{1,0:T(8,128)(2,1)} %bitcast.17, bf16[512,512]{1,0:T(8,128)(2,1)} %w_ref.3, f32[256,512]{1,0:T(8,128)} %get-tuple-element.10.unit_ref, f32[256,128]{1,0:T(8,128)} %get-tuple-element.11.inv_ref, ...), custom_call_target="tpu_custom_call" | custom-call | tf_op jit(solution)/shard_map/halo/pallas_call | solution.py:183
  24.9 0.0 collective-permute-start.2
  24.9 1.7 %collective-permute-done.2 = bf16[256,512]{1,0:T(8,128)(2,1)S(1)} collective-permute-done((bf16[256,512]{1,0:T(8,128)(2,1)}, bf16[256,512]{1,0:T(8,128)(2,1)S(1)}, u32[]{:S(2)}, u32[]{:S(2)}) %collective-permute-start.2) | collective-permute-done | bytes 262176 | tf_op jit(solution)/shard_map/ppermute | solution.py:197
  26.6 1.1 %add_convert_fusion = bf16[256,512]{1,0:T(8,128)(2,1)S(1)} fusion(f32[256,512]{1,0:T(8,128)} %get-tuple-element.15, bf16[256,512]{1,0:T(8,128)(2,1)S(1)} %collective-permute-done.2), kind=kLoop, calls=%fused_computation.1 | loop fusion | flops 393216 | bytes 1048576 | tf_op jit(solution)/shard_map/convert_element_type | solution.py:200
  27.8 13.6 %all_to_all.20 = bf16[16,16,512]{2,1,0:T(8,128)(2,1)S(1)} all-to-all(bf16[16,16,512]{2,1,0:T(8,128)(2,1)S(1)} %bitcast.19), channel_id=1, replica_groups=mesh['grp'=2,'blk'=16] {'blk'}, dimensions={0} | all-to-all | bytes 524288 | tf_op jit(solution)/shard_map/all_to_all | solution.py:200
  41.3 3.5 %all-to-all-start.2 = ((bf16[16,80,128]{2,1,0:T(8,128)(2,1)}), bf16[16,80,128]{2,1,0:T(8,128)(2,1)S(1)}, u32[]{:S(2)}, u32[]{:S(2)}) async-start(bf16[16,80,128]{2,1,0:T(8,128)(2,1)} %bitcast.9), calls=%async_computation.2 | async-start | bytes 655360 | tf_op jit(solution)/shard_map/all_to_all | solution.py:182
  45.0 10.8 %all-to-all-done.2 = bf16[16,80,128]{2,1,0:T(8,128)(2,1)S(1)} async-done(((bf16[16,80,128]{2,1,0:T(8,128)(2,1)}), bf16[16,80,128]{2,1,0:T(8,128)(2,1)S(1)}, u32[]{:S(2)}, u32[]{:S(2)}) %all-to-all-start.2) | async-done | bytes 327712 | tf_op jit(solution)/shard_map/all_to_all | solution.py:182
  55.8 0.7 broadcast_in_dim.26
  56.5 3.5 %all-to-all-start.1 = ((bf16[16,16,512]{2,1,0:T(8,128)(2,1)}), bf16[16,16,512]{2,1,0:T(8,128)(2,1)S(1)}, u32[]{:S(2)}, u32[]{:S(2)}) async-start(bf16[16,16,512]{2,1,0:T(8,128)(2,1)} %broadcast_in_dim.26), calls=%async_computation.1 | async-start | bytes 524288 | tf_op jit(solution)/shard_map/all_to_all | solution.py:202
  60.0 0.1 reduce_sum.25
  60.1 9.0 %all-to-all-done.1 = bf16[16,16,512]{2,1,0:T(8,128)(2,1)S(1)} async-done(((bf16[16,16,512]{2,1,0:T(8,128)(2,1)}), bf16[16,16,512]{2,1,0:T(8,128)(2,1)S(1)}, u32[]{:S(2)}, u32[]{:S(2)}) %all-to-all-start.1) | async-done | bytes 262176 | tf_op jit(solution)/shard_map/all_to_all | solution.py:202
  69.1 0.8 broadcast_in_dim.27
  69.8 3.5 %all-to-all-start.3 = ((bf16[16,80,128]{2,1,0:T(8,128)(2,1)}), bf16[16,80,128]{2,1,0:T(8,128)(2,1)S(1)}, u32[]{:S(2)}, u32[]{:S(2)}) async-start(bf16[16,80,128]{2,1,0:T(8,128)(2,1)} %broadcast_in_dim.27), calls=%async_computation.3 | async-start | bytes 655360 | tf_op jit(solution)/shard_map/all_to_all | solution.py:217
  73.4 0.1 collective-permute-start.3
  73.5 10.5 %all-to-all-done.3 = bf16[16,80,128]{2,1,0:T(8,128)(2,1)S(1)} async-done(((bf16[16,80,128]{2,1,0:T(8,128)(2,1)}), bf16[16,80,128]{2,1,0:T(8,128)(2,1)S(1)}, u32[]{:S(2)}, u32[]{:S(2)}) %all-to-all-start.3) | async-done | bytes 327712 | tf_op jit(solution)/shard_map/all_to_all | solution.py:217
  83.9 0.0 copy-start
  83.9 0.7 copy-done
  84.7 2.1 %unpack.1 = f32[512,512]{1,0:T(8,128)} custom-call(bf16[1280,128]{1,0:T(8,128)(2,1)} %bitcast.14), custom_call_target="tpu_custom_call" | custom-call | tf_op jit(solution)/shard_map/unpack/pallas_call | solution.py:220
  86.7 0.0 collective-permute-done.3
  86.8 0.1 broadcast_select_fusion.1
  86.8 1.1 %maximum_convert_fusion = f32[512,512]{1,0:T(8,128)} fusion(bf16[256,512]{1,0:T(8,128)(2,1)S(1)} %get-tuple-element.19, bf16[256,512]{1,0:T(8,128)(2,1)S(1)} %get-tuple-element.18), kind=kLoop, calls=%fused_computation | loop fusion | flops 1048576 | bytes 1572864 | tf_op jit(solution)/shard_map/convert_element_type | solution.py:210
  (2 shorter events, 0.1 us)
Async XLA Ops:
  0.6 14.5 %collective-permute-start = (bf16[256,512]{1,0:T(8,128)(2,1)}, bf16[256,512]{1,0:T(8,128)(2,1)S(1)}, u32[]{:S(2)}, u32[]{:S(2)}) collective-permute-start(bf16[256,512]{1,0:T(8,128)(2,1)} %bitcast.20), channel_id=1, source_target_pairs={{0,15},{1,0},{2,1},{3,2},{4,3},{5,4},{6,5},{7,6},{8,7},{9,8},{10,9... | collective-permute-start | bytes 786440 | tf_op jit(solution)/shard_map/ppermute | solution.py:147
  7.6 11.6 %collective-permute-start.1 = (bf16[256,512]{1,0:T(8,128)(2,1)}, bf16[256,512]{1,0:T(8,128)(2,1)S(1)}, u32[]{:S(2)}, u32[]{:S(2)}) collective-permute-start(bf16[256,512]{1,0:T(8,128)(2,1)} %bitcast.21), channel_id=1, source_target_pairs={{0,1},{1,2},{2,3},{3,4},{4,5},{5,6},{6,7},{7,8},{8,9},{9,10},{10,1... | collective-permute-start | bytes 786440 | tf_op jit(solution)/shard_map/ppermute | solution.py:148
  7.6 0.7 copy-start.4
  8.4 0.7 copy-start.5
  9.2 0.7 copy-start.3
  15.2 4.1 %copy-start.1 = (bf16[256,512]{1,0:T(8,128)(2,1)}, bf16[256,512]{1,0:T(8,128)(2,1)S(1)}, u32[]{:S(2)}) copy-start(bf16[256,512]{1,0:T(8,128)(2,1)S(1)} %collective-permute-done.refs_0_) | copy-start | bytes 786436
  19.2 0.7 copy-start.2
  24.9 1.7 %collective-permute-start.2 = (bf16[256,512]{1,0:T(8,128)(2,1)}, bf16[256,512]{1,0:T(8,128)(2,1)S(1)}, u32[]{:S(2)}, u32[]{:S(2)}) collective-permute-start(bf16[256,512]{1,0:T(8,128)(2,1)} %bitcast.25), channel_id=1, source_target_pairs={{0,16},{16,0},{1,17},{17,1},{2,18},{18,2},{3,19},{19,3},{4,20},{20... | collective-permute-start | bytes 786440 | tf_op jit(solution)/shard_map/ppermute | solution.py:197
  41.3 14.4 %all-to-all-start.2 = ((bf16[16,80,128]{2,1,0:T(8,128)(2,1)}), bf16[16,80,128]{2,1,0:T(8,128)(2,1)S(1)}, u32[]{:S(2)}, u32[]{:S(2)}) async-start(bf16[16,80,128]{2,1,0:T(8,128)(2,1)} %bitcast.9), calls=%async_computation.2 | async-start | bytes 655360 | tf_op jit(solution)/shard_map/all_to_all | solution.py:182
  56.5 12.6 %all-to-all-start.1 = ((bf16[16,16,512]{2,1,0:T(8,128)(2,1)}), bf16[16,16,512]{2,1,0:T(8,128)(2,1)S(1)}, u32[]{:S(2)}, u32[]{:S(2)}) async-start(bf16[16,16,512]{2,1,0:T(8,128)(2,1)} %broadcast_in_dim.26), calls=%async_computation.1 | async-start | bytes 524288 | tf_op jit(solution)/shard_map/all_to_all | solution.py:202
  69.8 14.1 %all-to-all-start.3 = ((bf16[16,80,128]{2,1,0:T(8,128)(2,1)}), bf16[16,80,128]{2,1,0:T(8,128)(2,1)S(1)}, u32[]{:S(2)}, u32[]{:S(2)}) async-start(bf16[16,80,128]{2,1,0:T(8,128)(2,1)} %broadcast_in_dim.27), calls=%async_computation.3 | async-start | bytes 655360 | tf_op jit(solution)/shard_map/all_to_all | solution.py:217
  73.4 13.4 %collective-permute-start.3 = (bf16[256,512]{1,0:T(8,128)(2,1)S(1)}, bf16[256,512]{1,0:T(8,128)(2,1)S(1)}, u32[]{:S(2)}, u32[]{:S(2)}) collective-permute-start(bf16[256,512]{1,0:T(8,128)(2,1)S(1)} %bitcast.18), channel_id=1, source_target_pairs={{0,16},{16,0},{1,17},{17,1},{2,18},{18,2},{3,19},{19,3},{4,20},{20... | collective-permute-start | bytes 786440 | tf_op jit(solution)/shard_map/ppermute | solution.py:206
  83.9 0.7 copy-start

commit v2 on v1

--- a/solution.py
+++ b/solution.py
@@ -6,6 +6,7 @@
 from jax.experimental.pallas import tpu as pltpu
 from jax.sharding import PartitionSpec as P
 
+
 inverse_sharpness = 2.5
 logit_bound = 2.5
 norm_eps = 1e-06
@@ -25,6 +26,10 @@
 
 def dot_tn(a, b):
     return lax.dot_general(a, b, (((0,), (0,)), ((), ())), preferred_element_type=f32)
+
+
+def room(mebibytes):
+    return pltpu.CompilerParams(vmem_limit_bytes=mebibytes * 1024 * 1024)
 
 
 def project(rows, weight):
@@ -51,25 +56,47 @@
     return jnp.concatenate(parts, axis=1)
 
 
-def pair_counts(src_ref, key_ref, blocks, slots, block, candidates):
-    pairs = src_ref.shape[1]
+def slot_start(listed, blocks, block, run, runs, reach):
+    offset = lax.rem(lax.div(listed, blocks) - run + reach + runs, runs) - reach
+    order = jnp.where(offset > 0, 2 * offset - 1, -2 * offset)
+    return (order * blocks + lax.rem(listed, blocks)) * block
+
+
+def pair_counts(list_ref, live_ref, src_ref, tgt_ref, block, run, runs, reach):
+    blocks, slots, pairs = src_ref.shape
+    candidates = (2 * reach + 1) * blocks
     point = lax.broadcasted_iota(jnp.int32, (block, pairs), 0)
     place = lax.broadcasted_iota(jnp.int32, (candidates * block, pairs), 0)
     rows = []
     for b in range(blocks):
         left = []
         right = []
-        for s in range(b * slots, (b + 1) * slots):
-            left.append(jnp.where(src_ref[s : s + 1, :] == point, 1.0, 0.0).astype(bf16))
-            right.append(jnp.where(key_ref[s : s + 1, :] == place, 1.0, 0.0).astype(bf16))
+        for s in range(slots):
+            first = slot_start(list_ref[b, s], blocks, block, run, runs, reach)
+            first = jnp.where(s < live_ref[0, b], first, -block)
+            key = tgt_ref[b, s : s + 1, :] + first
+            left.append(jnp.where(src_ref[b, s : s + 1, :] == point, 1.0, 0.0).astype(bf16))
+            right.append(jnp.where(key == place, 1.0, 0.0).astype(bf16))
         rows.append(dot_nt(jnp.concatenate(left, axis=1), jnp.concatenate(right, axis=1)))
     return jnp.concatenate(rows, axis=0)
 
 
+def moment_kernel(scale, xs_ref, xt_ref, w_ref, moment_ref):
+    weight = w_ref[...]
+    zs = project(xs_ref[...], weight)[0].astype(bf16)
+    zt = project(xt_ref[...], weight)[0].astype(bf16)
+    moment = (dot_tn(zs, zs) + dot_tn(zt, zt)) * scale
+    at = 0
+    for r in range(0, moment.shape[0], lane):
+        for c in range(r, moment.shape[1], lane):
+            moment_ref[at : at + lane, :] = moment[r : r + lane, c : c + lane].astype(bf16)
+            at += lane
+
+
 def own_kernel(
-    blocks, slots, block, candidates, scale,
-    xs_ref, xt_ref, w_ref, src_ref, key_ref,
-    moment_ref, unit_ref, inv_ref, count_ref, grad_ref, part_ref,
+    runs, reach,
+    run_ref, list_ref, live_ref, xs_ref, xt_ref, w_ref, src_ref, tgt_ref,
+    unit_ref, inv_ref, count_ref, grad_ref, part_ref,
 ):
     weight = w_ref[...]
     src_unit, src_inv = project(xs_ref[...], weight)
@@ -78,14 +105,11 @@
     zt = tgt_unit.astype(bf16)
     unit_ref[...] = src_unit
     inv_ref[...] = jnp.broadcast_to(src_inv, inv_ref.shape)
-    moment = (dot_tn(zs, zs) + dot_tn(zt, zt)) * scale
-    at = 0
-    for r in range(0, moment.shape[0], lane):
-        for c in range(r, moment.shape[1], lane):
-            moment_ref[at : at + lane, :] = moment[r : r + lane, c : c + lane].astype(bf16)
-            at += lane
-    counts = pair_counts(src_ref, key_ref, blocks, slots, block, candidates)
-    own = blocks * block
+    own = xs_ref.shape[0]
+    block = own // src_ref.shape[0]
+    counts = pair_counts(
+        list_ref, live_ref, src_ref, tgt_ref, block, run_ref[0], runs, reach
+    )
     count_ref[...] = counts[:, own:].astype(bf16)
     weights = pair_weights(zs, zt, counts[:, :own], block)
     grad_ref[...] = dot_nn(weights, zt)
@@ -119,7 +143,7 @@
         send_ref[k - 1] = total_ref[pl.ds(pl.multiple_of(first, chunk), chunk), :].astype(bf16)
 
 
-def unpack_kernel(packed_ref, out_ref):
+def unpack_ordered_kernel(packed_ref, out_ref):
     at = 0
     for r in range(0, out_ref.shape[0], lane):
         for c in range(r, out_ref.shape[1], lane):
@@ -130,11 +154,60 @@
             at += lane
 
 
+def unpack_kernel(run_ref, *refs):
+    column_refs = refs[:-2]
+    out_ref, packed_ref = refs[-2:]
+    low = len(column_refs)
+    rows = column_refs[0].shape[1]
+    for m, ref in enumerate(column_refs):
+        for k in range(ref.shape[0]):
+            owner = lax.bitwise_xor(run_ref[0], k * low + m)
+            packed_ref[pl.ds(pl.multiple_of(owner * rows, 16), rows), :] = ref[k]
+    unpack_ordered_kernel(packed_ref, out_ref)
+
+
+def sum_kernel(moved_ref, out_ref):
+    total = moved_ref[0].astype(f32)
+    for i in range(1, moved_ref.shape[0]):
+        total = total + moved_ref[i].astype(f32)
+    total = total.astype(bf16)
+    for i in range(out_ref.shape[0]):
+        out_ref[i] = total
+
+
+def sum_pieces(moved, repeats):
+    vmem = pl.BlockSpec(memory_space=pltpu.VMEM)
+    return pl.pallas_call(
+        sum_kernel,
+        out_shape=jax.ShapeDtypeStruct((repeats,) + moved.shape[1:], moved.dtype),
+        in_specs=[vmem],
+        out_specs=vmem,
+        compiler_params=room(8),
+    )(moved)
+
+
+def join_kernel(*refs):
+    out_ref = refs[-1]
+    for i, ref in enumerate(refs[:-1]):
+        out_ref[i] = ref[0]
+
+
+def join(pieces):
+    vmem = pl.BlockSpec(memory_space=pltpu.VMEM)
+    return pl.pallas_call(
+        join_kernel,
+        out_shape=jax.ShapeDtypeStruct((len(pieces),) + pieces[0].shape[1:], pieces[0].dtype),
+        in_specs=[vmem] * len(pieces),
+        out_specs=vmem,
+        compiler_params=room(8),
+    )(*pieces)
+
+
 def body(src_feats, tgt_feats, proj_weight, match_blocks, match_count, pair_src, pair_tgt):
     xs = src_feats[0]
     xt = tgt_feats[0]
     points, width = xs.shape
-    blocks, slots, pairs = pair_src.shape[1:]
+    blocks = pair_src.shape[1]
     block = points // blocks
     runs = lax.axis_size("blk")
     groups = lax.axis_size("grp")
@@ -147,16 +220,6 @@
         nbrs.append(lax.ppermute(xt, "blk", [(i, (i - k) % runs) for i in range(runs)]))
         nbrs.append(lax.ppermute(xt, "blk", [(i, (i + k) % runs) for i in range(runs)]))
 
-    listed = match_blocks[0]
-    offset = (listed // blocks - run + reach) % runs - reach
-    order = jnp.where(offset > 0, 2 * offset - 1, -2 * offset)
-    live = jnp.arange(slots, dtype=jnp.int32)[None, :] < match_count[0][:, None]
-    first = (order * blocks + listed % blocks) * block
-    keys = jnp.where(live[:, :, None], first[:, :, None] + pair_tgt[0], -1)
-    keys = keys.reshape(blocks * slots, pairs)
-    sources = pair_src[0].reshape(blocks * slots, pairs)
-
-    candidates = (2 * reach + 1) * blocks
     tiles = width // lane
     packed_rows = tiles * (tiles + 1) // 2 * lane
     chunk = width // groups
@@ -164,22 +227,32 @@
     vmem = pl.BlockSpec(memory_space=pltpu.VMEM)
     smem = pl.BlockSpec(memory_space=pltpu.SMEM)
 
-    packed, unit, inv, counts, grad, part = pl.pallas_call(
-        functools.partial(own_kernel, blocks, slots, block, candidates, scale),
+    packed = pl.pallas_call(
+        functools.partial(moment_kernel, scale),
+        out_shape=jax.ShapeDtypeStruct((packed_rows, lane), bf16),
+        in_specs=[vmem] * 3,
+        out_specs=vmem,
+        compiler_params=room(16),
+        name="moment",
+    )(xs, xt, proj_weight)
+    moved = lax.all_to_all(packed.reshape(runs, packed_rows // runs, lane), "blk", 0, 0)
+    unit, inv, counts, grad, part = pl.pallas_call(
+        functools.partial(own_kernel, runs, reach),
         out_shape=(
-            jax.ShapeDtypeStruct((packed_rows, lane), bf16),
             jax.ShapeDtypeStruct((points, width), f32),
             jax.ShapeDtypeStruct((points, lane), f32),
-            jax.ShapeDtypeStruct((points, (candidates - blocks) * block), bf16),
+            jax.ShapeDtypeStruct((points, 2 * reach * points), bf16),
             jax.ShapeDtypeStruct((points, width), f32),
             jax.ShapeDtypeStruct((width, width), f32),
         ),
-        in_specs=[vmem] * 5,
-        out_specs=(vmem,) * 6,
+        in_specs=[smem] * 3 + [vmem] * 5,
+        out_specs=(vmem,) * 5,
+        compiler_params=room(16 + 4 * reach),
         name="own",
-    )(xs, xt, proj_weight, sources, keys)
-
-    moved = lax.all_to_all(packed.reshape(runs, packed_rows // runs, lane), "blk", 0, 0)
+    )(
+        run.reshape(1), match_blocks[0], match_count, xs, xt, proj_weight,
+        pair_src[0], pair_tgt[0],
+    )
     keep, send = pl.pallas_call(
         functools.partial(halo_kernel, 2 * reach, block, groups),
         out_shape=(
@@ -189,6 +262,7 @@
         in_specs=[smem] + [vmem] * (7 + 2 * reach),
         out_specs=(vmem, vmem),
         scratch_shapes=[pltpu.VMEM((width, width), f32)],
+        compiler_params=room(16 + 8 * reach),
         name="halo",
     )(grp.reshape(1), xs, proj_weight, unit, inv, counts, grad, part, *nbrs)
 
@@ -196,10 +270,42 @@
     for k in range(1, groups):
         got = lax.ppermute(send[k - 1], "grp", [(i, (i + k) % groups) for i in range(groups)])
         total = total + got.astype(f32)
-    piece = chunk // runs
-    spread = lax.all_to_all(total.astype(bf16).reshape(runs, piece, width), "blk", 0, 0)
-    mine = jnp.sum(spread.astype(f32), axis=0).astype(bf16)
-    whole = lax.all_to_all(jnp.broadcast_to(mine, (runs, piece, width)), "blk", 0, 0)
+    spread = lax.all_to_all(total.astype(bf16).reshape(runs, chunk // runs, width), "blk", 0, 0)
+    low = 1 << (runs.bit_length() // 2)
+    mine = sum_pieces(moved, 1)
+    pieces = [mine] + [
+        lax.ppermute(mine, "blk", [(i, i ^ (k * low)) for i in range(runs)])
+        for k in range(1, runs // low)
+    ]
+    column = join(pieces)
+    mine = sum_pieces(spread, runs)
+    whole = lax.all_to_all(mine, "blk", 0, 0)
+    columns = [column] + [
+        lax.ppermute(column, "blk", [(i, i ^ k) for i in range(runs)]) for k in range(1, low)
+    ]
+    rows = packed_rows // runs
+    if rows % 16 == 0:
+        covariance = pl.pallas_call(
+            unpack_kernel,
+            out_shape=jax.ShapeDtypeStruct((width, width), f32),
+            in_specs=[smem] + [vmem] * low,
+            out_specs=vmem,
+            scratch_shapes=[pltpu.VMEM((packed_rows, lane), bf16)],
+            compiler_params=room(12),
+            name="unpack",
+        )(run.reshape(1), *columns)
+    else:
+        owner = jnp.arange(runs, dtype=jnp.int32) ^ run
+        found = jnp.stack(columns, axis=1).reshape(runs, rows, lane)
+        ordered = jnp.take(found, owner, axis=0).reshape(packed_rows, lane)
+        covariance = pl.pallas_call(
+            unpack_ordered_kernel,
+            out_shape=jax.ShapeDtypeStruct((width, width), f32),
+            in_specs=[vmem],
+            out_specs=vmem,
+            compiler_params=room(12),
+            name="unpack",
+        )(ordered)
     half = whole.reshape(chunk, width)
     parts = [half]
     for k in range(1, groups):
@@ -212,18 +318,6 @@
         stacked = jnp.stack(parts)
         place = (jnp.arange(groups, dtype=jnp.int32) - grp) % groups
         weight_grad = jnp.take(stacked, place, axis=0).reshape(width, width).astype(f32)
-
-    mine_c = jnp.sum(moved.astype(f32), axis=0).astype(bf16)
-    packed_all = lax.all_to_all(
-        jnp.broadcast_to(mine_c, (runs, packed_rows // runs, lane)), "blk", 0, 0
-    )
-    covariance = pl.pallas_call(
-        unpack_kernel,
-        out_shape=jax.ShapeDtypeStruct((width, width), f32),
-        in_specs=[vmem],
-        out_specs=vmem,
-        name="unpack",
-    )(packed_all.reshape(packed_rows, lane))
     return (weight_grad, covariance[None])
 
 

time: 88.5 us -> 82.3 us (0.930)
  starting transfers between devices: 17.7 us -> 22.3 us
  waiting for transfers between devices: 36 us -> 32.1 us
  Pallas kernels: 11.6 us -> 8.16 us
  other arithmetic: 3.12 us -> 1.23 us
  local copies, waits for them, and re-layouts: 5.14 us -> 3.66 us
    all_to_all x2 -> x1, waiting for transfers between devices: 19.4 us -> 7.68 us  [body(): whole = lax.all_to_all(mine, 'blk', 0, 0)]
    ppermute x0 -> x6, starting transfers between devices: none -> 7.94 us  [the longest x3 4.45 us: body(): lax.ppermute(mine, 'blk', [(i, i ^ k * low) for i in range(runs)])]
    ppermute x0 -> x6, waiting for transfers between devices: none -> 6.85 us  [the longest x3 3.43 us: body(): lax.ppermute(mine, 'blk', [(i, i ^ k * low) for i in range(runs)])]
    all_to_all x2 -> x1, starting transfers between devices: 7.08 us -> 3.68 us  [body(): whole = lax.all_to_all(mine, 'blk', 0, 0)]
    pallas_call x1, Pallas kernels: 4.94 us -> 2.03 us  [body(): pl.pallas_call(functools.partial(halo_kernel, 2 * reach, block, groups),...]
    broadcast_in_dim x2 -> x0, local copies, waits for them, and re-layouts: 1.5 us -> none  [the longest x1 0.77 us: body(): jnp.broadcast_to(mine_c, (runs, packed_rows // runs, lane))]
    ppermute x1, waiting for transfers between devices: 4.06 us -> 5.46 us  [body(): lax.ppermute(xt, 'blk', [(i, (i + k) % runs) for i in range(runs)])]
    convert_element_type x1, other arithmetic: 1.12 us -> 0.07 us  [body(): total.astype(bf16).reshape(runs, chunk // runs, width)]
  transfers between devices with their start and end apart: 7 -> 12, of which waited for: 5 -> 9; matrix products, arithmetic and copies ran while one was open for 1% -> 0% of each run, Pallas kernels for 8% -> 7%
where the time goes in v2:
time: 82.3 us; the launch traced here: 81.9 us
  waiting for transfers between devices  32.1 us (39%)
  starting transfers between devices  22.3 us (27%)
  blocking collectives  13.6 us (17%)
  Pallas kernels  8.16 us (10%)
  local copies, waits for them, and re-layouts  3.66 us (4%)
  other arithmetic  1.23 us (1%)
    all_to_all x1, blocking collectives, body(): lax.all_to_all(total.astype(bf16).reshape(runs, chunk // runs, width), 'b...  13.6 us
    all_to_all x1, waiting for transfers between devices, body(): lax.all_to_all(packed.reshape(runs, packed_rows // runs, lane), 'blk', 0, 0)  10.6 us
    all_to_all x1, waiting for transfers between devices, body(): whole = lax.all_to_all(mine, 'blk', 0, 0)  7.68 us
    ppermute x1, starting transfers between devices, body(): lax.ppermute(xt, 'blk', [(i, (i - k) % runs) for i in range(runs)])  7.01 us
    ppermute x1, waiting for transfers between devices, body(): lax.ppermute(xt, 'blk', [(i, (i + k) % runs) for i in range(runs)])  5.46 us
    ppermute x3, starting transfers between devices, body(): lax.ppermute(mine, 'blk', [(i, i ^ k * low) for i in range(runs)])  4.45 us
    all_to_all x1, starting transfers between devices, body(): whole = lax.all_to_all(mine, 'blk', 0, 0)  3.68 us
    unnamed x20, local copies, waits for them, and re-layouts  3.66 us
  transfers between devices with their start and end apart: 12, of which 9 were waited for; matrix products, arithmetic and copies ran while one was open for 0% of the time, Pallas kernels for 7%

profile of v2, /device:TPU:0, one launch (start us, length us, event | category | flops | bytes accessed | tf_op | source)
XLA Modules:
  0.0 81.9 jit_solution(13338491816679456595)
XLA Ops:
  0.6 7.0 %collective-permute-start = (bf16[256,512]{1,0:T(8,128)(2,1)}, bf16[256,512]{1,0:T(8,128)(2,1)S(1)}, u32[]{:S(2)}, u32[]{:S(2)}) collective-permute-start(bf16[256,512]{1,0:T(8,128)(2,1)} %bitcast.17), channel_id=1, source_target_pairs={{0,15},{1,0},{2,1},{3,2},{4,3},{5,4},{6,5},{7,6},{8,7},{9,8},{10,9... | collective-permute-start | bytes 786440 | tf_op jit(solution)/shard_map/ppermute | solution.py:220
  7.6 0.0 collective-permute-start.1
  7.6 0.0 copy-start.9
  7.7 0.0 copy-start.7
  7.7 0.0 copy-start.6
  7.7 0.0 copy-start.8
  7.7 0.6 copy-done.9
  8.3 0.0 copy-done.7
  8.4 0.0 copy-done.6
  8.4 0.0 copy-done.8
  8.4 0.0 copy-start
  8.4 1.0 %copy-done = bf16[512,512]{1,0:T(8,128)(2,1)S(1)} copy-done((bf16[512,512]{1,0:T(8,128)(2,1)S(1)}, bf16[512,512]{1,0:T(8,128)(2,1)}, u32[]{:S(2)}) %copy-start) | copy-done | bytes 524312
  9.4 0.9 %copy-done.2 = bf16[1,256,512]{2,1,0:T(8,128)(2,1)S(1)} copy-done((bf16[1,256,512]{2,1,0:T(8,128)(2,1)S(1)}, bf16[1,256,512]{2,1,0:T(8,128)(2,1)}, u32[]{:S(2)}) %copy-start.2) | copy-done | bytes 262168
  10.4 0.9 %copy-done.4 = bf16[1,256,512]{2,1,0:T(8,128)(2,1)S(1)} copy-done((bf16[1,256,512]{2,1,0:T(8,128)(2,1)S(1)}, bf16[1,256,512]{2,1,0:T(8,128)(2,1)}, u32[]{:S(2)}) %copy-start.4) | copy-done | bytes 262168
  11.3 2.4 %own.1 = (f32[256,512]{1,0:T(8,128)S(1)}, f32[256,128]{1,0:T(8,128)S(1)}, bf16[256,512]{1,0:T(8,128)(2,1)S(1)}, f32[256,512]{1,0:T(8,128)S(1)}, f32[512,512]{1,0:T(8,128)S(1)}) custom-call(s32[1]{0:T(128)} %bitcast.2.run_ref, s32[2,4]{1,0:T(2,128)S(1)} %bitcast.23, s32[1,2]{1,0:T(1,128)S(1)} %copy-done.9, bf16[256,512]{1,0:T(8,128)(2,1)S(1)} %bitcast.14, ...), custom_call_target="tpu_custom_call" | custom-call | tf_op jit(solution)/shard_map/own/pallas_call | solution.py:239
  13.8 0.0 collective-permute-done.refs_0_
  13.8 5.5 %collective-permute-done.1.refs_1_ = bf16[256,512]{1,0:T(8,128)(2,1)S(1)} collective-permute-done((bf16[256,512]{1,0:T(8,128)(2,1)}, bf16[256,512]{1,0:T(8,128)(2,1)S(1)}, u32[]{:S(2)}, u32[]{:S(2)}) %collective-permute-start.1) | collective-permute-done | bytes 262176 | tf_op jit(solution)/shard_map/ppermute | solution.py:221
  19.2 0.0 copy-done.1
  19.2 0.0 copy-done.3
  19.2 2.0 %halo.1 = (f32[256,512]{1,0:T(8,128)S(1)}, bf16[1,256,512]{2,1,0:T(8,128)(2,1)S(1)}) custom-call(s32[1]{0:T(128)} %bitcast.grp_ref, bf16[256,512]{1,0:T(8,128)(2,1)S(1)} %bitcast.15, bf16[512,512]{1,0:T(8,128)(2,1)S(1)} %copy-done.1, f32[256,512]{1,0:T(8,128)S(1)} %get-tuple-element.9.unit_ref, f32[256,128]{1,0:T(8,128)S(1)} %get-tuple-element.10.inv_ref, ...), custom_call_target="tpu_custom_call" | custom-call | tf_op jit(solution)/shard_map/halo/pallas_call | solution.py:256
  21.3 0.1 collective-permute-start.2
  21.3 1.5 %collective-permute-done.2 = bf16[256,512]{1,0:T(8,128)(2,1)S(1)} collective-permute-done((bf16[256,512]{1,0:T(8,128)(2,1)S(1)}, bf16[256,512]{1,0:T(8,128)(2,1)S(1)}, u32[]{:S(2)}, u32[]{:S(2)}) %collective-permute-start.2) | collective-permute-done | bytes 262176 | tf_op jit(solution)/shard_map/ppermute | solution.py:271
  22.9 0.1 add_convert_fusion
  22.9 13.6 %all_to_all.15.moved_ref = bf16[16,16,512]{2,1,0:T(8,128)(2,1)S(1)} all-to-all(bf16[16,16,512]{2,1,0:T(8,128)(2,1)S(1)} %bitcast.27), channel_id=1, replica_groups=mesh['grp'=2,'blk'=16] {'blk'}, dimensions={0} | all-to-all | bytes 524288 | tf_op jit(solution)/shard_map/all_to_all | solution.py:273
  36.5 0.8 shard_map.86
  37.3 3.7 %all-to-all-start.1 = ((bf16[16,16,512]{2,1,0:T(8,128)(2,1)}), bf16[16,16,512]{2,1,0:T(8,128)(2,1)S(1)}, u32[]{:S(2)}, u32[]{:S(2)}) async-start(bf16[16,16,512]{2,1,0:T(8,128)(2,1)} %shard_map.86), calls=%async_computation.1 | async-start | bytes 524288 | tf_op jit(solution)/shard_map/all_to_all | solution.py:282
  41.0 0.0 copy-done.5
  41.0 1.7 %moment.1 = bf16[1280,128]{1,0:T(8,128)(2,1)} custom-call(bf16[256,512]{1,0:T(8,128)(2,1)S(1)} %bitcast.16, bf16[256,512]{1,0:T(8,128)(2,1)S(1)} %bitcast.20, bf16[512,512]{1,0:T(8,128)(2,1)S(1)} %copy-done.1), custom_call_target="tpu_custom_call" | custom-call | tf_op jit(solution)/shard_map/moment/pallas_call | solution.py:230
  42.7 7.7 %all-to-all-done.1 = bf16[16,16,512]{2,1,0:T(8,128)(2,1)S(1)} async-done(((bf16[16,16,512]{2,1,0:T(8,128)(2,1)}), bf16[16,16,512]{2,1,0:T(8,128)(2,1)S(1)}, u32[]{:S(2)}, u32[]{:S(2)}) %all-to-all-start.1) | async-done | bytes 262176 | tf_op jit(solution)/shard_map/all_to_all | solution.py:282
  50.4 3.6 %all-to-all-start.2 = ((bf16[16,80,128]{2,1,0:T(8,128)(2,1)}), bf16[16,80,128]{2,1,0:T(8,128)(2,1)S(1)}, u32[]{:S(2)}, u32[]{:S(2)}) async-start(bf16[16,80,128]{2,1,0:T(8,128)(2,1)} %bitcast.10), calls=%async_computation.2 | async-start | bytes 655360 | tf_op jit(solution)/shard_map/all_to_all | solution.py:238
  54.0 0.1 collective-permute-start.3
  54.1 10.6 %all-to-all-done.2.moved_ref = bf16[16,80,128]{2,1,0:T(8,128)(2,1)S(1)} async-done(((bf16[16,80,128]{2,1,0:T(8,128)(2,1)}), bf16[16,80,128]{2,1,0:T(8,128)(2,1)S(1)}, u32[]{:S(2)}, u32[]{:S(2)}) %all-to-all-start.2) | async-done | bytes 327712 | tf_op jit(solution)/shard_map/all_to_all | solution.py:238
  64.7 1.1 %collective-permute-start.4 = (bf16[1,80,128]{2,1,0:T(8,128)(2,1)S(1)}, bf16[1,80,128]{2,1,0:T(8,128)(2,1)S(1)}, u32[]{:S(2)}, u32[]{:S(2)}) collective-permute-start(bf16[1,80,128]{2,1,0:T(8,128)(2,1)S(1)} %shard_map.87.refs_0_), channel_id=1, source_target_pairs={{0,4},{1,5},{2,6},{3,7},{4,0},{5,1},{6,2},{7,3},{8,12},{9,13},{10,... | collective-permute-start | bytes 61448 | tf_op jit(solution)/shard_map/ppermute | solution.py:277
  65.8 1.2 %collective-permute-start.5 = (bf16[1,80,128]{2,1,0:T(8,128)(2,1)S(1)}, bf16[1,80,128]{2,1,0:T(8,128)(2,1)S(1)}, u32[]{:S(2)}, u32[]{:S(2)}) collective-permute-start(bf16[1,80,128]{2,1,0:T(8,128)(2,1)S(1)} %shard_map.87.refs_0_), channel_id=1, source_target_pairs={{0,8},{1,9},{2,10},{3,11},{4,12},{5,13},{6,14},{7,15},{8,0},{9,1},... | collective-permute-start | bytes 61448 | tf_op jit(solution)/shard_map/ppermute | solution.py:277
  67.0 2.1 %collective-permute-start.6 = (bf16[1,80,128]{2,1,0:T(8,128)(2,1)S(1)}, bf16[1,80,128]{2,1,0:T(8,128)(2,1)S(1)}, u32[]{:S(2)}, u32[]{:S(2)}) collective-permute-start(bf16[1,80,128]{2,1,0:T(8,128)(2,1)S(1)} %shard_map.87.refs_0_), channel_id=1, source_target_pairs={{0,12},{1,13},{2,14},{3,15},{4,8},{5,9},{6,10},{7,11},{8,4},{9,5},... | collective-permute-start | bytes 61448 | tf_op jit(solution)/shard_map/ppermute | solution.py:277
  69.2 0.0 collective-permute-done.4.refs_1_
  69.2 1.3 %collective-permute-done.5.refs_2_ = bf16[1,80,128]{2,1,0:T(8,128)(2,1)S(1)} collective-permute-done((bf16[1,80,128]{2,1,0:T(8,128)(2,1)S(1)}, bf16[1,80,128]{2,1,0:T(8,128)(2,1)S(1)}, u32[]{:S(2)}, u32[]{:S(2)}) %collective-permute-start.5) | collective-permute-done | bytes 20512 | tf_op jit(solution)/shard_map/ppermute | solution.py:277
  70.5 2.1 %collective-permute-done.6.refs_3_ = bf16[1,80,128]{2,1,0:T(8,128)(2,1)S(1)} collective-permute-done((bf16[1,80,128]{2,1,0:T(8,128)(2,1)S(1)}, bf16[1,80,128]{2,1,0:T(8,128)(2,1)S(1)}, u32[]{:S(2)}, u32[]{:S(2)}) %collective-permute-start.6) | collective-permute-done | bytes 20512 | tf_op jit(solution)/shard_map/ppermute | solution.py:277
  72.6 0.6 collective-permute-start.7
  73.2 1.0 %collective-permute-start.8 = (bf16[4,80,128]{2,1,0:T(8,128)(2,1)S(1)}, bf16[4,80,128]{2,1,0:T(8,128)(2,1)S(1)}, u32[]{:S(2)}, u32[]{:S(2)}) collective-permute-start(bf16[4,80,128]{2,1,0:T(8,128)(2,1)S(1)} %shard_map.88.refs_0_), channel_id=1, source_target_pairs={{0,2},{1,3},{2,0},{3,1},{4,6},{5,7},{6,4},{7,5},{8,10},{9,11},{10,... | collective-permute-start | bytes 245768 | tf_op jit(solution)/shard_map/ppermute | solution.py:284
  74.2 1.9 %collective-permute-start.9 = (bf16[4,80,128]{2,1,0:T(8,128)(2,1)S(1)}, bf16[4,80,128]{2,1,0:T(8,128)(2,1)S(1)}, u32[]{:S(2)}, u32[]{:S(2)}) collective-permute-start(bf16[4,80,128]{2,1,0:T(8,128)(2,1)S(1)} %shard_map.88.refs_0_), channel_id=1, source_target_pairs={{0,3},{1,2},{2,1},{3,0},{4,7},{5,6},{6,5},{7,4},{8,11},{9,10},{10,... | collective-permute-start | bytes 245768 | tf_op jit(solution)/shard_map/ppermute | solution.py:284
  76.1 1.0 %collective-permute-done.7.refs_1_ = bf16[4,80,128]{2,1,0:T(8,128)(2,1)S(1)} collective-permute-done((bf16[4,80,128]{2,1,0:T(8,128)(2,1)S(1)}, bf16[4,80,128]{2,1,0:T(8,128)(2,1)S(1)}, u32[]{:S(2)}, u32[]{:S(2)}) %collective-permute-start.7) | collective-permute-done | bytes 81952 | tf_op jit(solution)/shard_map/ppermute | solution.py:284
  77.1 0.6 collective-permute-done.8.refs_2_
  77.6 1.9 %collective-permute-done.9.refs_3_ = bf16[4,80,128]{2,1,0:T(8,128)(2,1)S(1)} collective-permute-done((bf16[4,80,128]{2,1,0:T(8,128)(2,1)S(1)}, bf16[4,80,128]{2,1,0:T(8,128)(2,1)S(1)}, u32[]{:S(2)}, u32[]{:S(2)}) %collective-permute-start.9) | collective-permute-done | bytes 81952 | tf_op jit(solution)/shard_map/ppermute | solution.py:284
  79.5 1.1 %unpack.1 = f32[512,512]{1,0:T(8,128)} custom-call(s32[1]{0:T(128)} %bitcast.2.run_ref, bf16[4,80,128]{2,1,0:T(8,128)(2,1)S(1)} %shard_map.88.refs_0_, bf16[4,80,128]{2,1,0:T(8,128)(2,1)S(1)} %collective-permute-done.7.refs_1_, bf16[4,80,128]{2,1,0:T(8,128)(2,1)S(1)} %collective-permute-done.8.refs_2_, bf16[4,80,128]{2,1,0:T(8,128)(2,1)S(1)} %collective-permute-done.9.refs_3_), custom_call_target="tpu_custom_call" | custom-call | tf_op jit(solution)/shard_map/unpack/pallas_call | solution.py:288
  80.7 0.0 collective-permute-done.3
  80.7 0.1 broadcast_select_fusion.1
  80.8 1.1 %maximum_convert_fusion = f32[512,512]{1,0:T(8,128)} fusion(bf16[256,512]{1,0:T(8,128)(2,1)S(1)} %get-tuple-element.17, bf16[256,512]{1,0:T(8,128)(2,1)S(1)} %get-tuple-element.16), kind=kLoop, calls=%fused_computation | loop fusion | flops 1048576 | bytes 1572864 | tf_op jit(solution)/shard_map/convert_element_type | solution.py:316
  (7 shorter events, 0.1 us)
Async XLA Ops:
  0.6 13.1 %collective-permute-start = (bf16[256,512]{1,0:T(8,128)(2,1)}, bf16[256,512]{1,0:T(8,128)(2,1)S(1)}, u32[]{:S(2)}, u32[]{:S(2)}) collective-permute-start(bf16[256,512]{1,0:T(8,128)(2,1)} %bitcast.17), channel_id=1, source_target_pairs={{0,15},{1,0},{2,1},{3,2},{4,3},{5,4},{6,5},{7,6},{8,7},{9,8},{10,9... | collective-permute-start | bytes 786440 | tf_op jit(solution)/shard_map/ppermute | solution.py:220
  7.6 11.6 %collective-permute-start.1 = (bf16[256,512]{1,0:T(8,128)(2,1)}, bf16[256,512]{1,0:T(8,128)(2,1)S(1)}, u32[]{:S(2)}, u32[]{:S(2)}) collective-permute-start(bf16[256,512]{1,0:T(8,128)(2,1)} %bitcast.18), channel_id=1, source_target_pairs={{0,1},{1,2},{2,3},{3,4},{4,5},{5,6},{6,7},{7,8},{8,9},{9,10},{10,1... | collective-permute-start | bytes 786440 | tf_op jit(solution)/shard_map/ppermute | solution.py:221
  7.6 0.7 copy-start.9
  7.7 0.7 copy-start.7
  7.7 0.7 copy-start.6
  7.7 0.7 copy-start.8
  8.4 1.0 %copy-start = (bf16[512,512]{1,0:T(8,128)(2,1)S(1)}, bf16[512,512]{1,0:T(8,128)(2,1)}, u32[]{:S(2)}) copy-start(bf16[512,512]{1,0:T(8,128)(2,1)} %w_ref.5) | copy-start | bytes 1572868
  9.4 0.9 %copy-start.2 = (bf16[1,256,512]{2,1,0:T(8,128)(2,1)S(1)}, bf16[1,256,512]{2,1,0:T(8,128)(2,1)}, u32[]{:S(2)}) copy-start(bf16[1,256,512]{2,1,0:T(8,128)(2,1)} %param.7) | copy-start | bytes 786436
  10.4 0.9 %copy-start.4 = (bf16[1,256,512]{2,1,0:T(8,128)(2,1)S(1)}, bf16[1,256,512]{2,1,0:T(8,128)(2,1)}, u32[]{:S(2)}) copy-start(bf16[1,256,512]{2,1,0:T(8,128)(2,1)} %param.8) | copy-start | bytes 786436
  11.3 7.9 %copy-start.1 = (bf16[512,512]{1,0:T(8,128)(2,1)S(1)}, bf16[512,512]{1,0:T(8,128)(2,1)}, u32[]{:S(2)}) copy-start(bf16[512,512]{1,0:T(8,128)(2,1)} %w_ref.5) | copy-start | bytes 1572868
  11.3 7.9 %copy-start.3 = (bf16[1,256,512]{2,1,0:T(8,128)(2,1)S(1)}, bf16[1,256,512]{2,1,0:T(8,128)(2,1)}, u32[]{:S(2)}) copy-start(bf16[1,256,512]{2,1,0:T(8,128)(2,1)} %param.7) | copy-start | bytes 786436
  21.3 1.6 %collective-permute-start.2 = (bf16[256,512]{1,0:T(8,128)(2,1)S(1)}, bf16[256,512]{1,0:T(8,128)(2,1)S(1)}, u32[]{:S(2)}, u32[]{:S(2)}) collective-permute-start(bf16[256,512]{1,0:T(8,128)(2,1)S(1)} %bitcast.24), channel_id=1, source_target_pairs={{0,16},{16,0},{1,17},{17,1},{2,18},{18,2},{3,19},{19,3},{4,20},{20... | collective-permute-start | bytes 786440 | tf_op jit(solution)/shard_map/ppermute | solution.py:271
  37.3 3.7 %copy-start.5 = (bf16[1,256,512]{2,1,0:T(8,128)(2,1)S(1)}, bf16[1,256,512]{2,1,0:T(8,128)(2,1)}, u32[]{:S(2)}) copy-start(bf16[1,256,512]{2,1,0:T(8,128)(2,1)} %param.8) | copy-start | bytes 786436
  37.3 13.1 %all-to-all-start.1 = ((bf16[16,16,512]{2,1,0:T(8,128)(2,1)}), bf16[16,16,512]{2,1,0:T(8,128)(2,1)S(1)}, u32[]{:S(2)}, u32[]{:S(2)}) async-start(bf16[16,16,512]{2,1,0:T(8,128)(2,1)} %shard_map.86), calls=%async_computation.1 | async-start | bytes 524288 | tf_op jit(solution)/shard_map/all_to_all | solution.py:282
  50.4 14.3 %all-to-all-start.2 = ((bf16[16,80,128]{2,1,0:T(8,128)(2,1)}), bf16[16,80,128]{2,1,0:T(8,128)(2,1)S(1)}, u32[]{:S(2)}, u32[]{:S(2)}) async-start(bf16[16,80,128]{2,1,0:T(8,128)(2,1)} %bitcast.10), calls=%async_computation.2 | async-start | bytes 655360 | tf_op jit(solution)/shard_map/all_to_all | solution.py:238
  54.0 26.7 %collective-permute-start.3 = (bf16[256,512]{1,0:T(8,128)(2,1)S(1)}, bf16[256,512]{1,0:T(8,128)(2,1)S(1)}, u32[]{:S(2)}, u32[]{:S(2)}) collective-permute-start(bf16[256,512]{1,0:T(8,128)(2,1)S(1)} %bitcast.26), channel_id=1, source_target_pairs={{0,16},{16,0},{1,17},{17,1},{2,18},{18,2},{3,19},{19,3},{4,20},{20... | collective-permute-start | bytes 786440 | tf_op jit(solution)/shard_map/ppermute | solution.py:312
  64.7 4.5 %collective-permute-start.4 = (bf16[1,80,128]{2,1,0:T(8,128)(2,1)S(1)}, bf16[1,80,128]{2,1,0:T(8,128)(2,1)S(1)}, u32[]{:S(2)}, u32[]{:S(2)}) collective-permute-start(bf16[1,80,128]{2,1,0:T(8,128)(2,1)S(1)} %shard_map.87.refs_0_), channel_id=1, source_target_pairs={{0,4},{1,5},{2,6},{3,7},{4,0},{5,1},{6,2},{7,3},{8,12},{9,13},{10,... | collective-permute-start | bytes 61448 | tf_op jit(solution)/shard_map/ppermute | solution.py:277
  65.8 4.7 %collective-permute-start.5 = (bf16[1,80,128]{2,1,0:T(8,128)(2,1)S(1)}, bf16[1,80,128]{2,1,0:T(8,128)(2,1)S(1)}, u32[]{:S(2)}, u32[]{:S(2)}) collective-permute-start(bf16[1,80,128]{2,1,0:T(8,128)(2,1)S(1)} %shard_map.87.refs_0_), channel_id=1, source_target_pairs={{0,8},{1,9},{2,10},{3,11},{4,12},{5,13},{6,14},{7,15},{8,0},{9,1},... | collective-permute-start | bytes 61448 | tf_op jit(solution)/shard_map/ppermute | solution.py:277
  67.0 5.6 %collective-permute-start.6 = (bf16[1,80,128]{2,1,0:T(8,128)(2,1)S(1)}, bf16[1,80,128]{2,1,0:T(8,128)(2,1)S(1)}, u32[]{:S(2)}, u32[]{:S(2)}) collective-permute-start(bf16[1,80,128]{2,1,0:T(8,128)(2,1)S(1)} %shard_map.87.refs_0_), channel_id=1, source_target_pairs={{0,12},{1,13},{2,14},{3,15},{4,8},{5,9},{6,10},{7,11},{8,4},{9,5},... | collective-permute-start | bytes 61448 | tf_op jit(solution)/shard_map/ppermute | solution.py:277
  72.6 4.4 %collective-permute-start.7 = (bf16[4,80,128]{2,1,0:T(8,128)(2,1)S(1)}, bf16[4,80,128]{2,1,0:T(8,128)(2,1)S(1)}, u32[]{:S(2)}, u32[]{:S(2)}) collective-permute-start(bf16[4,80,128]{2,1,0:T(8,128)(2,1)S(1)} %shard_map.88.refs_0_), channel_id=1, source_target_pairs={{0,1},{1,0},{2,3},{3,2},{4,5},{5,4},{6,7},{7,6},{8,9},{9,8},{10,11... | collective-permute-start | bytes 245768 | tf_op jit(solution)/shard_map/ppermute | solution.py:284
  73.2 4.4 %collective-permute-start.8 = (bf16[4,80,128]{2,1,0:T(8,128)(2,1)S(1)}, bf16[4,80,128]{2,1,0:T(8,128)(2,1)S(1)}, u32[]{:S(2)}, u32[]{:S(2)}) collective-permute-start(bf16[4,80,128]{2,1,0:T(8,128)(2,1)S(1)} %shard_map.88.refs_0_), channel_id=1, source_target_pairs={{0,2},{1,3},{2,0},{3,1},{4,6},{5,7},{6,4},{7,5},{8,10},{9,11},{10,... | collective-permute-start | bytes 245768 | tf_op jit(solution)/shard_map/ppermute | solution.py:284
  74.2 5.3 %collective-permute-start.9 = (bf16[4,80,128]{2,1,0:T(8,128)(2,1)S(1)}, bf16[4,80,128]{2,1,0:T(8,128)(2,1)S(1)}, u32[]{:S(2)}, u32[]{:S(2)}) collective-permute-start(bf16[4,80,128]{2,1,0:T(8,128)(2,1)S(1)} %shard_map.88.refs_0_), channel_id=1, source_target_pairs={{0,3},{1,2},{2,1},{3,0},{4,7},{5,6},{6,5},{7,4},{8,11},{9,10},{10,... | collective-permute-start | bytes 245768 | tf_op jit(solution)/shard_map/ppermute | solution.py:284

commit v3 on v2

--- a/solution.py
+++ b/solution.py
@@ -11,6 +11,7 @@
 logit_bound = 2.5
 norm_eps = 1e-06
 lane = 128
+
 
 f32 = jnp.float32
 bf16 = jnp.bfloat16
@@ -81,7 +82,18 @@
     return jnp.concatenate(rows, axis=0)
 
 
-def moment_kernel(scale, xs_ref, xt_ref, w_ref, moment_ref):
+def load(pairs, sem):
+    copies = [pltpu.make_async_copy(src, dst, sem.at[i]) for i, (src, dst) in enumerate(pairs)]
+    for copy in copies:
+        copy.start()
+    return copies
+
+
+def moment_kernel(far, near, scale, run_ref, xs_hbm, xt_hbm, w_hbm, *refs):
+    out_refs = refs[:far]
+    xs_ref, xt_ref, w_ref, packed_ref, sem = refs[far:]
+    for copy in load(((w_hbm, w_ref), (xs_hbm, xs_ref), (xt_hbm, xt_ref)), sem):
+        copy.wait()
     weight = w_ref[...]
     zs = project(xs_ref[...], weight)[0].astype(bf16)
     zt = project(xt_ref[...], weight)[0].astype(bf16)
@@ -89,8 +101,15 @@
     at = 0
     for r in range(0, moment.shape[0], lane):
         for c in range(r, moment.shape[1], lane):
-            moment_ref[at : at + lane, :] = moment[r : r + lane, c : c + lane].astype(bf16)
+            packed_ref[at : at + lane, :] = moment[r : r + lane, c : c + lane].astype(bf16)
             at += lane
+    if at < packed_ref.shape[0]:
+        packed_ref[at:, :] = jnp.zeros((packed_ref.shape[0] - at, lane), bf16)
+    rows = packed_ref.shape[0] // far
+    place = lax.div(run_ref[0], near)
+    for k in range(far):
+        first = lax.bitwise_xor(place, k) * rows
+        out_refs[k][...] = packed_ref[pl.ds(pl.multiple_of(first, 16), rows), :]
 
 
 def own_kernel(
@@ -118,13 +137,13 @@
 
 
 def halo_kernel(
-    nbrs, block, groups,
+    reach, block, groups,
     grp_ref, xs_ref, w_ref, unit_ref, inv_ref, count_ref, grad_ref, part_ref, *refs,
 ):
-    nbr_refs = refs[:nbrs]
-    keep_ref, send_ref, total_ref = refs[nbrs:]
+    nbr_refs = refs[: 2 * reach]
+    keep_ref, send_ref, total_ref = refs[2 * reach :]
     weight = w_ref[...]
-    rows = jnp.concatenate([r[...] for r in nbr_refs], axis=0)
+    rows = jnp.concatenate([ref[...] for ref in nbr_refs], axis=0)
     tgt_unit, tgt_inv = project(rows, weight)
     zt = tgt_unit.astype(bf16)
     src_unit = unit_ref[...]
@@ -143,7 +162,64 @@
         send_ref[k - 1] = total_ref[pl.ds(pl.multiple_of(first, chunk), chunk), :].astype(bf16)
 
 
-def unpack_ordered_kernel(packed_ref, out_ref):
+def tree(parts):
+    while len(parts) > 1:
+        parts = [parts[i] + parts[i + 1] for i in range(0, len(parts), 2)]
+    return parts[0]
+
+
+def deal_kernel(near, groups, run_ref, *refs):
+    keep_ref, *got_refs = refs[:groups]
+    total_ref, sum_ref = refs[-2:]
+    out_refs = refs[-2 - near : -2]
+    piece_refs = refs[groups : -2 - near]
+    total = keep_ref[...]
+    for ref in got_refs:
+        total = total + ref[...].astype(f32)
+    total_ref[...] = total
+    sum_ref[...] = tree([ref[...].astype(f32) for ref in piece_refs]).astype(bf16)
+    place = lax.rem(run_ref[0], near)
+    rows = total_ref.shape[0] // near
+    below = sum_ref.shape[0] // near
+    for k in range(near):
+        owner = lax.bitwise_xor(place, k)
+        part = total_ref[pl.ds(pl.multiple_of(owner * rows, rows), rows), :].astype(bf16)
+        at = 0
+        for c in range(0, total_ref.shape[1], lane):
+            out_refs[k][at : at + rows, :] = part[:, c : c + lane]
+            at += rows
+        first = pl.multiple_of(owner * below, 16)
+        out_refs[k][at : at + below, :] = sum_ref[pl.ds(first, below), :]
+
+
+def near_kernel(*refs):
+    refs[-1][...] = tree([ref[...].astype(f32) for ref in refs[:-1]]).astype(bf16)
+
+
+def far_kernel(rows, *refs):
+    out_ref = refs[-1]
+    out_ref[:rows, :] = tree([ref[:rows, :].astype(f32) for ref in refs[:-1]]).astype(bf16)
+    below = refs[0].shape[0] - rows
+    for i, ref in enumerate(refs[:-1]):
+        at = rows + i * below
+        out_ref[at : at + below, :] = ref[rows:, :]
+
+
+def gather_kernel(rows, *refs):
+    out_ref = refs[-1]
+    for i, ref in enumerate(refs[:-1]):
+        out_ref[i * rows : (i + 1) * rows, :] = ref[:rows, :]
+
+
+def unpack_kernel(near, far, skip, run_ref, *refs):
+    column_refs = refs[:near]
+    out_ref, packed_ref = refs[near:]
+    rows = (column_refs[0].shape[0] - skip) // far
+    for m, ref in enumerate(column_refs):
+        for k in range(far):
+            owner = lax.bitwise_xor(run_ref[0], k * near + m)
+            at = skip + k * rows
+            packed_ref[pl.ds(pl.multiple_of(owner * rows, 16), rows), :] = ref[at : at + rows, :]
     at = 0
     for r in range(0, out_ref.shape[0], lane):
         for c in range(r, out_ref.shape[1], lane):
@@ -154,53 +230,37 @@
             at += lane
 
 
-def unpack_kernel(run_ref, *refs):
-    column_refs = refs[:-2]
-    out_ref, packed_ref = refs[-2:]
-    low = len(column_refs)
-    rows = column_refs[0].shape[1]
-    for m, ref in enumerate(column_refs):
-        for k in range(ref.shape[0]):
-            owner = lax.bitwise_xor(run_ref[0], k * low + m)
-            packed_ref[pl.ds(pl.multiple_of(owner * rows, 16), rows), :] = ref[k]
-    unpack_ordered_kernel(packed_ref, out_ref)
-
-
-def sum_kernel(moved_ref, out_ref):
-    total = moved_ref[0].astype(f32)
-    for i in range(1, moved_ref.shape[0]):
-        total = total + moved_ref[i].astype(f32)
-    total = total.astype(bf16)
-    for i in range(out_ref.shape[0]):
-        out_ref[i] = total
-
-
-def sum_pieces(moved, repeats):
+def place_kernel(near, run_ref, grp_ref, *refs):
+    out_ref = refs[-1]
+    groups = len(refs) - 1
+    chunk = out_ref.shape[0] // groups
+    rows = chunk // near
+    place = lax.rem(run_ref[0], near)
+    for j, ref in enumerate(refs[:-1]):
+        base = lax.rem(grp_ref[0] + j, groups) * chunk
+        at = 0
+        for m in range(near):
+            first = pl.multiple_of(base + lax.bitwise_xor(place, m) * rows, rows)
+            for c in range(0, out_ref.shape[1], lane):
+                out_ref[pl.ds(first, rows), c : c + lane] = ref[at : at + rows, :].astype(f32)
+                at += rows
+
+
+def swap(array, bits, runs):
+    return lax.ppermute(array, "blk", [(i, i ^ bits) for i in range(runs)])
+
+
+def small_call(kernel, shapes, specs, scratch=()):
     vmem = pl.BlockSpec(memory_space=pltpu.VMEM)
+    many = isinstance(shapes, tuple)
     return pl.pallas_call(
-        sum_kernel,
-        out_shape=jax.ShapeDtypeStruct((repeats,) + moved.shape[1:], moved.dtype),
-        in_specs=[vmem],
-        out_specs=vmem,
-        compiler_params=room(8),
-    )(moved)
-
-
-def join_kernel(*refs):
-    out_ref = refs[-1]
-    for i, ref in enumerate(refs[:-1]):
-        out_ref[i] = ref[0]
-
-
-def join(pieces):
-    vmem = pl.BlockSpec(memory_space=pltpu.VMEM)
-    return pl.pallas_call(
-        join_kernel,
-        out_shape=jax.ShapeDtypeStruct((len(pieces),) + pieces[0].shape[1:], pieces[0].dtype),
-        in_specs=[vmem] * len(pieces),
-        out_specs=vmem,
-        compiler_params=room(8),
-    )(*pieces)
+        kernel,
+        out_shape=shapes,
+        in_specs=specs,
+        out_specs=(vmem,) * len(shapes) if many else vmem,
+        scratch_shapes=scratch,
+        compiler_params=room(12),
+    )
 
 
 def body(src_feats, tgt_feats, proj_weight, match_blocks, match_count, pair_src, pair_tgt):
@@ -221,21 +281,35 @@
         nbrs.append(lax.ppermute(xt, "blk", [(i, (i + k) % runs) for i in range(runs)]))
 
     tiles = width // lane
-    packed_rows = tiles * (tiles + 1) // 2 * lane
+    near = 1 << (runs.bit_length() // 2)
+    far = runs // near
+    piece_rows = -(-tiles * (tiles + 1) // 2 * lane // (16 * runs)) * 16
+    column_rows = near * piece_rows
     chunk = width // groups
+    grad_rows = chunk // near * tiles
     scale = width / (2.0 * points * runs)
     vmem = pl.BlockSpec(memory_space=pltpu.VMEM)
     smem = pl.BlockSpec(memory_space=pltpu.SMEM)
-
-    packed = pl.pallas_call(
-        functools.partial(moment_kernel, scale),
-        out_shape=jax.ShapeDtypeStruct((packed_rows, lane), bf16),
-        in_specs=[vmem] * 3,
-        out_specs=vmem,
+    hbm = pl.BlockSpec(memory_space=pltpu.HBM)
+    run_id = run.reshape(1)
+    grp_id = grp.reshape(1)
+
+    pieces = pl.pallas_call(
+        functools.partial(moment_kernel, far, near, scale),
+        out_shape=(jax.ShapeDtypeStruct((column_rows, lane), bf16),) * far,
+        in_specs=[smem] + [hbm] * 3,
+        out_specs=(vmem,) * far,
+        scratch_shapes=[
+            pltpu.VMEM((points, width), bf16),
+            pltpu.VMEM((points, width), bf16),
+            pltpu.VMEM((width, width), bf16),
+            pltpu.VMEM((far * column_rows, lane), bf16),
+            pltpu.SemaphoreType.DMA((3,)),
+        ],
         compiler_params=room(16),
         name="moment",
-    )(xs, xt, proj_weight)
-    moved = lax.all_to_all(packed.reshape(runs, packed_rows // runs, lane), "blk", 0, 0)
+    )(run_id, *(pltpu.with_memory_space_constraint(a, pltpu.HBM) for a in (xs, xt, proj_weight)))
+    pieces = [pieces[0]] + [swap(pieces[k], k * near, runs) for k in range(1, far)]
     unit, inv, counts, grad, part = pl.pallas_call(
         functools.partial(own_kernel, runs, reach),
         out_shape=(
@@ -250,11 +324,11 @@
         compiler_params=room(16 + 4 * reach),
         name="own",
     )(
-        run.reshape(1), match_blocks[0], match_count, xs, xt, proj_weight,
+        run_id, match_blocks[0], match_count, xs, xt, proj_weight,
         pair_src[0], pair_tgt[0],
     )
     keep, send = pl.pallas_call(
-        functools.partial(halo_kernel, 2 * reach, block, groups),
+        functools.partial(halo_kernel, reach, block, groups),
         out_shape=(
             jax.ShapeDtypeStruct((chunk, width), f32),
             jax.ShapeDtypeStruct((groups - 1, chunk, width), bf16),
@@ -264,60 +338,48 @@
         scratch_shapes=[pltpu.VMEM((width, width), f32)],
         compiler_params=room(16 + 8 * reach),
         name="halo",
-    )(grp.reshape(1), xs, proj_weight, unit, inv, counts, grad, part, *nbrs)
-
-    total = keep
-    for k in range(1, groups):
-        got = lax.ppermute(send[k - 1], "grp", [(i, (i + k) % groups) for i in range(groups)])
-        total = total + got.astype(f32)
-    spread = lax.all_to_all(total.astype(bf16).reshape(runs, chunk // runs, width), "blk", 0, 0)
-    low = 1 << (runs.bit_length() // 2)
-    mine = sum_pieces(moved, 1)
-    pieces = [mine] + [
-        lax.ppermute(mine, "blk", [(i, i ^ (k * low)) for i in range(runs)])
-        for k in range(1, runs // low)
+    )(grp_id, xs, proj_weight, unit, inv, counts, grad, part, *nbrs)
+
+    got = [
+        lax.ppermute(send[k - 1], "grp", [(i, (i + k) % groups) for i in range(groups)])
+        for k in range(1, groups)
     ]
-    column = join(pieces)
-    mine = sum_pieces(spread, runs)
-    whole = lax.all_to_all(mine, "blk", 0, 0)
-    columns = [column] + [
-        lax.ppermute(column, "blk", [(i, i ^ k) for i in range(runs)]) for k in range(1, low)
+    part_shape = jax.ShapeDtypeStruct((grad_rows + piece_rows, lane), bf16)
+    parts = small_call(
+        functools.partial(deal_kernel, near, groups),
+        (part_shape,) * near,
+        [smem] + [vmem] * (groups + far),
+        [pltpu.VMEM((chunk, width), f32), pltpu.VMEM((column_rows, lane), bf16)],
+    )(run_id, keep, *got, *pieces)
+    parts = [parts[0]] + [swap(parts[k], k, runs) for k in range(1, near)]
+    part = small_call(near_kernel, part_shape, [vmem] * near)(*parts)
+    parts = [part] + [swap(part, k * near, runs) for k in range(1, far)]
+    part = small_call(
+        functools.partial(far_kernel, grad_rows),
+        jax.ShapeDtypeStruct((grad_rows + far * piece_rows, lane), bf16),
+        [vmem] * far,
+    )(*parts)
+    columns = [part] + [swap(part, k, runs) for k in range(1, near)]
+    half = small_call(
+        functools.partial(gather_kernel, grad_rows),
+        jax.ShapeDtypeStruct((near * grad_rows, lane), bf16),
+        [vmem] * near,
+    )(*columns)
+    halves = [half] + [
+        lax.ppermute(half, "grp", [(i, (i - k) % groups) for i in range(groups)])
+        for k in range(1, groups)
     ]
-    rows = packed_rows // runs
-    if rows % 16 == 0:
-        covariance = pl.pallas_call(
-            unpack_kernel,
-            out_shape=jax.ShapeDtypeStruct((width, width), f32),
-            in_specs=[smem] + [vmem] * low,
-            out_specs=vmem,
-            scratch_shapes=[pltpu.VMEM((packed_rows, lane), bf16)],
-            compiler_params=room(12),
-            name="unpack",
-        )(run.reshape(1), *columns)
-    else:
-        owner = jnp.arange(runs, dtype=jnp.int32) ^ run
-        found = jnp.stack(columns, axis=1).reshape(runs, rows, lane)
-        ordered = jnp.take(found, owner, axis=0).reshape(packed_rows, lane)
-        covariance = pl.pallas_call(
-            unpack_ordered_kernel,
-            out_shape=jax.ShapeDtypeStruct((width, width), f32),
-            in_specs=[vmem],
-            out_specs=vmem,
-            compiler_params=room(12),
-            name="unpack",
-        )(ordered)
-    half = whole.reshape(chunk, width)
-    parts = [half]
-    for k in range(1, groups):
-        parts.append(lax.ppermute(half, "grp", [(i, (i - k) % groups) for i in range(groups)]))
-    if groups == 2:
-        low = jnp.where(grp == 0, parts[0], parts[1])
-        high = jnp.where(grp == 0, parts[1], parts[0])
-        weight_grad = jnp.concatenate([low, high], axis=0).astype(f32)
-    else:
-        stacked = jnp.stack(parts)
-        place = (jnp.arange(groups, dtype=jnp.int32) - grp) % groups
-        weight_grad = jnp.take(stacked, place, axis=0).reshape(width, width).astype(f32)
+    covariance = small_call(
+        functools.partial(unpack_kernel, near, far, grad_rows),
+        jax.ShapeDtypeStruct((width, width), f32),
+        [smem] + [vmem] * near,
+        [pltpu.VMEM((far * column_rows, lane), bf16)],
+    )(run_id, *columns)
+    weight_grad = small_call(
+        functools.partial(place_kernel, near),
+        jax.ShapeDtypeStruct((width, width), f32),
+        [smem] * 2 + [vmem] * groups,
+    )(run_id, grp_id, *halves)
     return (weight_grad, covariance[None])
 
 

time: 82.3 us -> 61.6 us (0.75)
  blocking collectives: 13.6 us -> 0 us
  waiting for transfers between devices: 32.1 us -> 24.9 us
  other arithmetic: 1.23 us -> 0 us
  Pallas kernels: 8.16 us -> 9.17 us
    all_to_all x2 -> x0, waiting for transfers between devices: 18.3 us -> none  [the longest x1 10.6 us: body(): lax.all_to_all(packed.reshape(runs, packed_rows // runs, lane), 'blk', 0, 0)]
    all_to_all x1 -> x0, blocking collectives: 13.6 us -> none  [body(): lax.all_to_all(total.astype(bf16).reshape(runs, chunk // runs, width), 'b...]
    ppermute x6 -> x12, waiting for transfers between devices: 6.85 us -> 19.1 us  [swap(): return lax.ppermute(array, 'blk', [(i, i ^ bits) for i in range(runs)])]
    ppermute x6 -> x12, starting transfers between devices: 7.94 us -> 15.7 us  [swap(): return lax.ppermute(array, 'blk', [(i, i ^ bits) for i in range(runs)])]
    all_to_all x2 -> x0, starting transfers between devices: 7.23 us -> none  [the longest x1 3.68 us: body(): whole = lax.all_to_all(mine, 'blk', 0, 0)]
    ppermute x1, waiting for transfers between devices: 1.52 us -> 0.01 us  [body(): lax.ppermute(send[k - 1], 'grp', [(i, (i + k) % groups) for i in range(gr...]
    convert_element_type x2 -> x0, other arithmetic: 1.18 us -> none  [the longest x1 1.1 us: body(): weight_grad = jnp.concatenate([low, high], axis=0).astype(f32)]
    pallas_call x6 -> x8, Pallas kernels: 5.74 us -> 6.74 us  [the longest x1 2.25 us: body(): pl.pallas_call(functools.partial(moment_kernel, far, near, scale), out_sh...]
  transfers between devices with their start and end apart: 12 -> 16, of which waited for: 9 -> 13; matrix products, arithmetic and copies ran while one was open for 0% -> 0% of each run, Pallas kernels for 7% -> 10%
where the time goes in v3:
time: 61.6 us; the launch traced here: 61.3 us
  waiting for transfers between devices  24.9 us (40%)
  starting transfers between devices  22.9 us (37%)
  Pallas kernels  9.17 us (15%)
  local copies, waits for them, and re-layouts  3.66 us (6%)
  between operations  0.73 us (1%)
    ppermute x12, waiting for transfers between devices, swap(): return lax.ppermute(array, 'blk', [(i, i ^ bits) for i in range(runs)])  19.1 us
    ppermute x12, starting transfers between devices, swap(): return lax.ppermute(array, 'blk', [(i, i ^ bits) for i in range(runs)])  15.7 us
    ppermute x1, starting transfers between devices, body(): lax.ppermute(xt, 'blk', [(i, (i - k) % runs) for i in range(runs)])  7.01 us
    ppermute x1, waiting for transfers between devices, body(): lax.ppermute(xt, 'blk', [(i, (i + k) % runs) for i in range(runs)])  5.45 us
    unnamed x18, local copies, waits for them, and re-layouts  3.66 us
    pallas_call x1, Pallas kernels, body(): pl.pallas_call(functools.partial(own_kernel, runs, reach), out_shape=(jax...  2.43 us
    pallas_call x1, Pallas kernels, body(): pl.pallas_call(functools.partial(moment_kernel, far, near, scale), out_sh...  2.25 us
    pallas_call x1, Pallas kernels, body(): pl.pallas_call(functools.partial(halo_kernel, reach, block, groups), out_...  2.04 us
  transfers between devices with their start and end apart: 16, of which 13 were waited for; matrix products, arithmetic and copies ran while one was open for 0% of the time, Pallas kernels for 10%

profile of v3, /device:TPU:0, one launch (start us, length us, event | category | flops | bytes accessed | tf_op | source)
XLA Modules:
  0.0 61.3 jit_solution(6882354757155758971)
XLA Ops:
  0.6 7.0 %collective-permute-start = (bf16[256,512]{1,0:T(8,128)(2,1)}, bf16[256,512]{1,0:T(8,128)(2,1)S(1)}, u32[]{:S(2)}, u32[]{:S(2)}) collective-permute-start(bf16[256,512]{1,0:T(8,128)(2,1)} %bitcast.12), channel_id=1, source_target_pairs={{0,15},{1,0},{2,1},{3,2},{4,3},{5,4},{6,5},{7,6},{8,7},{9,8},{10,9... | collective-permute-start | bytes 786440 | tf_op jit(solution)/shard_map/ppermute | solution.py:280
  7.6 0.0 collective-permute-start.1
  7.7 0.0 copy-start.7
  7.7 0.6 %copy-done.8 = s32[1,2]{1,0:T(1,128)S(1)} copy-done((s32[1,2]{1,0:T(1,128)S(1)}, s32[1,2]{1,0:T(1,128)}, u32[]{:S(2)}) %copy-start.8) | copy-done | bytes 32
  8.3 0.0 copy-done.6
  8.4 0.0 copy-done.5
  8.4 0.0 copy-done.7
  8.4 1.0 %copy-done = bf16[512,512]{1,0:T(8,128)(2,1)S(1)} copy-done((bf16[512,512]{1,0:T(8,128)(2,1)S(1)}, bf16[512,512]{1,0:T(8,128)(2,1)}, u32[]{:S(2)}) %copy-start) | copy-done | bytes 524312
  9.4 0.9 %copy-done.2 = bf16[1,256,512]{2,1,0:T(8,128)(2,1)S(1)} copy-done((bf16[1,256,512]{2,1,0:T(8,128)(2,1)S(1)}, bf16[1,256,512]{2,1,0:T(8,128)(2,1)}, u32[]{:S(2)}) %copy-start.2) | copy-done | bytes 262168
  10.4 0.9 %copy-done.4 = bf16[1,256,512]{2,1,0:T(8,128)(2,1)S(1)} copy-done((bf16[1,256,512]{2,1,0:T(8,128)(2,1)S(1)}, bf16[1,256,512]{2,1,0:T(8,128)(2,1)}, u32[]{:S(2)}) %copy-start.4) | copy-done | bytes 262168
  11.3 2.4 %own.1 = (f32[256,512]{1,0:T(8,128)S(1)}, f32[256,128]{1,0:T(8,128)S(1)}, bf16[256,512]{1,0:T(8,128)(2,1)S(1)}, f32[256,512]{1,0:T(8,128)S(1)}, f32[512,512]{1,0:T(8,128)S(1)}) custom-call(s32[1]{0:T(128)} %bitcast.run_ref, s32[2,4]{1,0:T(2,128)S(1)} %bitcast.18, s32[1,2]{1,0:T(1,128)S(1)} %copy-done.8, bf16[256,512]{1,0:T(8,128)(2,1)S(1)} %bitcast.10, ...), custom_call_target="tpu_custom_call" | custom-call | tf_op jit(solution)/shard_map/own/pallas_call | solution.py:313
  13.8 0.0 collective-permute-done.refs_0_
  13.8 5.5 %collective-permute-done.1.refs_1_ = bf16[256,512]{1,0:T(8,128)(2,1)S(1)} collective-permute-done((bf16[256,512]{1,0:T(8,128)(2,1)}, bf16[256,512]{1,0:T(8,128)(2,1)S(1)}, u32[]{:S(2)}, u32[]{:S(2)}) %collective-permute-start.1) | collective-permute-done | bytes 262176 | tf_op jit(solution)/shard_map/ppermute | solution.py:281
  19.2 0.0 copy-done.1
  19.2 0.0 copy-done.3
  19.2 2.0 %halo.1 = (f32[256,512]{1,0:T(8,128)S(1)}, bf16[1,256,512]{2,1,0:T(8,128)(2,1)S(1)}) custom-call(s32[1]{0:T(128)} %bitcast.1.grp_ref, bf16[256,512]{1,0:T(8,128)(2,1)S(1)} %bitcast.11, bf16[512,512]{1,0:T(8,128)(2,1)S(1)} %copy-done.1, f32[256,512]{1,0:T(8,128)S(1)} %get-tuple-element.17.unit_ref, f32[256,128]{1,0:T(8,128)S(1)} %get-tuple-element.18.inv_ref, ...), custom_call_target="tpu_custom_call" | custom-call | tf_op jit(solution)/shard_map/halo/pallas_call | solution.py:330
  21.3 0.1 collective-permute-start.2
  21.3 2.3 %moment.1 = (bf16[320,128]{1,0:T(8,128)(2,1)S(1)}, bf16[320,128]{1,0:T(8,128)(2,1)S(1)}, bf16[320,128]{1,0:T(8,128)(2,1)S(1)}, bf16[320,128]{1,0:T(8,128)(2,1)S(1)}) custom-call(s32[1]{0:T(128)} %bitcast.run_ref, bf16[256,512]{1,0:T(8,128)(2,1)} %bitcast.9, bf16[256,512]{1,0:T(8,128)(2,1)} %bitcast.14, bf16[512,512]{1,0:T(8,128)(2,1)} %w_hbm.1), custom_call_target="tpu_custom_call" | custom-call | tf_op jit(solution)/shard_map/moment/pallas_call | solution.py:297
  23.6 0.1 collective-permute-start.3
  23.7 1.0 %collective-permute-start.4 = (bf16[320,128]{1,0:T(8,128)(2,1)S(1)}, bf16[320,128]{1,0:T(8,128)(2,1)S(1)}, u32[]{:S(2)}, u32[]{:S(2)}) collective-permute-start(bf16[320,128]{1,0:T(8,128)(2,1)S(1)} %get-tuple-element.26), channel_id=1, source_target_pairs={{0,8},{1,9},{2,10},{3,11},{4,12},{5,13},{6,14},{7,15},{8,0},{9,1},... | collective-permute-start | bytes 245768 | tf_op jit(solution)/shard_map/ppermute | solution.py:250
  24.6 3.4 %collective-permute-start.5 = (bf16[320,128]{1,0:T(8,128)(2,1)S(1)}, bf16[320,128]{1,0:T(8,128)(2,1)S(1)}, u32[]{:S(2)}, u32[]{:S(2)}) collective-permute-start(bf16[320,128]{1,0:T(8,128)(2,1)S(1)} %get-tuple-element.27), channel_id=1, source_target_pairs={{0,12},{1,13},{2,14},{3,15},{4,8},{5,9},{6,10},{7,11},{8,4},{9,5},... | collective-permute-start | bytes 245768 | tf_op jit(solution)/shard_map/ppermute | solution.py:250
  28.1 1.6 %collective-permute-done.3.refs_3_ = bf16[320,128]{1,0:T(8,128)(2,1)S(1)} collective-permute-done((bf16[320,128]{1,0:T(8,128)(2,1)S(1)}, bf16[320,128]{1,0:T(8,128)(2,1)S(1)}, u32[]{:S(2)}, u32[]{:S(2)}) %collective-permute-start.3) | collective-permute-done | bytes 81952 | tf_op jit(solution)/shard_map/ppermute | solution.py:250
  29.7 3.9 %collective-permute-done.4.refs_4_ = bf16[320,128]{1,0:T(8,128)(2,1)S(1)} collective-permute-done((bf16[320,128]{1,0:T(8,128)(2,1)S(1)}, bf16[320,128]{1,0:T(8,128)(2,1)S(1)}, u32[]{:S(2)}, u32[]{:S(2)}) %collective-permute-start.4) | collective-permute-done | bytes 81952 | tf_op jit(solution)/shard_map/ppermute | solution.py:250
  33.5 0.0 collective-permute-done.5.refs_5_
  33.5 0.0 collective-permute-done.2.refs_1_
  33.5 0.1 shard_map.86
  33.7 0.6 collective-permute-start.6
  34.3 0.5 collective-permute-start.7
  34.8 2.5 %collective-permute-start.8 = (bf16[336,128]{1,0:T(8,128)(2,1)S(1)}, bf16[336,128]{1,0:T(8,128)(2,1)S(1)}, u32[]{:S(2)}, u32[]{:S(2)}) collective-permute-start(bf16[336,128]{1,0:T(8,128)(2,1)S(1)} %get-tuple-element.31), channel_id=1, source_target_pairs={{0,3},{1,2},{2,1},{3,0},{4,7},{5,6},{6,5},{7,4},{8,11},{9,10},{10,... | collective-permute-start | bytes 258056 | tf_op jit(solution)/shard_map/ppermute | solution.py:250
  37.2 1.4 %collective-permute-done.6.refs_1_ = bf16[336,128]{1,0:T(8,128)(2,1)S(1)} collective-permute-done((bf16[336,128]{1,0:T(8,128)(2,1)S(1)}, bf16[336,128]{1,0:T(8,128)(2,1)S(1)}, u32[]{:S(2)}, u32[]{:S(2)}) %collective-permute-start.6) | collective-permute-done | bytes 86048 | tf_op jit(solution)/shard_map/ppermute | solution.py:250
  38.6 0.5 collective-permute-done.7.refs_2_
  39.1 1.1 %collective-permute-done.8.refs_3_ = bf16[336,128]{1,0:T(8,128)(2,1)S(1)} collective-permute-done((bf16[336,128]{1,0:T(8,128)(2,1)S(1)}, bf16[336,128]{1,0:T(8,128)(2,1)S(1)}, u32[]{:S(2)}, u32[]{:S(2)}) %collective-permute-start.8) | collective-permute-done | bytes 86048 | tf_op jit(solution)/shard_map/ppermute | solution.py:250
  40.2 2.9 %collective-permute-start.10 = (bf16[336,128]{1,0:T(8,128)(2,1)S(1)}, bf16[336,128]{1,0:T(8,128)(2,1)S(1)}, u32[]{:S(2)}, u32[]{:S(2)}) collective-permute-start(bf16[336,128]{1,0:T(8,128)(2,1)S(1)} %shard_map.87.refs_0_), channel_id=1, source_target_pairs={{0,8},{1,9},{2,10},{3,11},{4,12},{5,13},{6,14},{7,15},{8,0},{9,1},... | collective-permute-start | bytes 258056 | tf_op jit(solution)/shard_map/ppermute | solution.py:250
  43.1 1.3 %collective-permute-start.11 = (bf16[336,128]{1,0:T(8,128)(2,1)S(1)}, bf16[336,128]{1,0:T(8,128)(2,1)S(1)}, u32[]{:S(2)}, u32[]{:S(2)}) collective-permute-start(bf16[336,128]{1,0:T(8,128)(2,1)S(1)} %shard_map.87.refs_0_), channel_id=1, source_target_pairs={{0,12},{1,13},{2,14},{3,15},{4,8},{5,9},{6,10},{7,11},{8,4},{9,5},... | collective-permute-start | bytes 258056 | tf_op jit(solution)/shard_map/ppermute | solution.py:250
  44.4 0.0 collective-permute-start.9
  44.4 2.9 %collective-permute-done.10.refs_2_ = bf16[336,128]{1,0:T(8,128)(2,1)S(1)} collective-permute-done((bf16[336,128]{1,0:T(8,128)(2,1)S(1)}, bf16[336,128]{1,0:T(8,128)(2,1)S(1)}, u32[]{:S(2)}, u32[]{:S(2)}) %collective-permute-start.10) | collective-permute-done | bytes 86048 | tf_op jit(solution)/shard_map/ppermute | solution.py:250
  47.3 2.2 %collective-permute-done.11.refs_3_ = bf16[336,128]{1,0:T(8,128)(2,1)S(1)} collective-permute-done((bf16[336,128]{1,0:T(8,128)(2,1)S(1)}, bf16[336,128]{1,0:T(8,128)(2,1)S(1)}, u32[]{:S(2)}, u32[]{:S(2)}) %collective-permute-start.11) | collective-permute-done | bytes 86048 | tf_op jit(solution)/shard_map/ppermute | solution.py:250
  49.5 0.3 collective-permute-done.9.refs_1_
  49.8 1.2 %collective-permute-start.12 = (bf16[576,128]{1,0:T(8,128)(2,1)S(1)}, bf16[576,128]{1,0:T(8,128)(2,1)S(1)}, u32[]{:S(2)}, u32[]{:S(2)}) collective-permute-start(bf16[576,128]{1,0:T(8,128)(2,1)S(1)} %shard_map.88.refs_0_), channel_id=1, source_target_pairs={{0,1},{1,0},{2,3},{3,2},{4,5},{5,4},{6,7},{7,6},{8,9},{9,8},{10,11... | collective-permute-start | bytes 442376 | tf_op jit(solution)/shard_map/ppermute | solution.py:250
  51.0 1.6 %collective-permute-start.13 = (bf16[576,128]{1,0:T(8,128)(2,1)S(1)}, bf16[576,128]{1,0:T(8,128)(2,1)S(1)}, u32[]{:S(2)}, u32[]{:S(2)}) collective-permute-start(bf16[576,128]{1,0:T(8,128)(2,1)S(1)} %shard_map.88.refs_0_), channel_id=1, source_target_pairs={{0,2},{1,3},{2,0},{3,1},{4,6},{5,7},{6,4},{7,5},{8,10},{9,11},{10,... | collective-permute-start | bytes 442376 | tf_op jit(solution)/shard_map/ppermute | solution.py:250
  52.6 0.8 %collective-permute-start.14 = (bf16[576,128]{1,0:T(8,128)(2,1)S(1)}, bf16[576,128]{1,0:T(8,128)(2,1)S(1)}, u32[]{:S(2)}, u32[]{:S(2)}) collective-permute-start(bf16[576,128]{1,0:T(8,128)(2,1)S(1)} %shard_map.88.refs_0_), channel_id=1, source_target_pairs={{0,3},{1,2},{2,1},{3,0},{4,7},{5,6},{6,5},{7,4},{8,11},{9,10},{10,... | collective-permute-start | bytes 442376 | tf_op jit(solution)/shard_map/ppermute | solution.py:250
  53.4 1.9 %collective-permute-done.12.refs_1_ = bf16[576,128]{1,0:T(8,128)(2,1)S(1)} collective-permute-done((bf16[576,128]{1,0:T(8,128)(2,1)S(1)}, bf16[576,128]{1,0:T(8,128)(2,1)S(1)}, u32[]{:S(2)}, u32[]{:S(2)}) %collective-permute-start.12) | collective-permute-done | bytes 147488 | tf_op jit(solution)/shard_map/ppermute | solution.py:250
  55.3 1.6 %collective-permute-done.13.refs_2_ = bf16[576,128]{1,0:T(8,128)(2,1)S(1)} collective-permute-done((bf16[576,128]{1,0:T(8,128)(2,1)S(1)}, bf16[576,128]{1,0:T(8,128)(2,1)S(1)}, u32[]{:S(2)}, u32[]{:S(2)}) %collective-permute-start.13) | collective-permute-done | bytes 147488 | tf_op jit(solution)/shard_map/ppermute | solution.py:250
  56.9 1.8 %collective-permute-done.14.refs_3_ = bf16[576,128]{1,0:T(8,128)(2,1)S(1)} collective-permute-done((bf16[576,128]{1,0:T(8,128)(2,1)S(1)}, bf16[576,128]{1,0:T(8,128)(2,1)S(1)}, u32[]{:S(2)}, u32[]{:S(2)}) %collective-permute-start.14) | collective-permute-done | bytes 147488 | tf_op jit(solution)/shard_map/ppermute | solution.py:250
  58.7 0.1 collective-permute-start.15
  58.8 1.2 %shard_map.91 = f32[512,512]{1,0:T(8,128)} custom-call(s32[1]{0:T(128)} %bitcast.run_ref, bf16[576,128]{1,0:T(8,128)(2,1)S(1)} %shard_map.88.refs_0_, bf16[576,128]{1,0:T(8,128)(2,1)S(1)} %collective-permute-done.12.refs_1_, bf16[576,128]{1,0:T(8,128)(2,1)S(1)} %collective-permute-done.13.refs_2_, bf16[576,128]{1,0:T(8,128)(2,1)S(1)} %collective-permute-done.14.refs_3_), custom_call_target="tpu_custom_call" | custom-call | tf_op jit(solution)/shard_map/pallas_call | solution.py:372
  59.9 0.4 collective-permute-done.15.refs_1_
  60.3 1.0 %shard_map.90 = f32[512,512]{1,0:T(8,128)} custom-call(s32[1]{0:T(128)} %bitcast.run_ref, s32[1]{0:T(128)} %bitcast.1.grp_ref, bf16[1024,128]{1,0:T(8,128)(2,1)S(1)} %shard_map.89.refs_0_, bf16[1024,128]{1,0:T(8,128)(2,1)S(1)} %collective-permute-done.15.refs_1_), custom_call_target="tpu_custom_call" | custom-call | tf_op jit(solution)/shard_map/pallas_call | solution.py:378
  (11 shorter events, 0.1 us)
Async XLA Ops:
  0.6 13.1 %collective-permute-start = (bf16[256,512]{1,0:T(8,128)(2,1)}, bf16[256,512]{1,0:T(8,128)(2,1)S(1)}, u32[]{:S(2)}, u32[]{:S(2)}) collective-permute-start(bf16[256,512]{1,0:T(8,128)(2,1)} %bitcast.12), channel_id=1, source_target_pairs={{0,15},{1,0},{2,1},{3,2},{4,3},{5,4},{6,5},{7,6},{8,7},{9,8},{10,9... | collective-permute-start | bytes 786440 | tf_op jit(solution)/shard_map/ppermute | solution.py:280
  7.6 11.6 %collective-permute-start.1 = (bf16[256,512]{1,0:T(8,128)(2,1)}, bf16[256,512]{1,0:T(8,128)(2,1)S(1)}, u32[]{:S(2)}, u32[]{:S(2)}) collective-permute-start(bf16[256,512]{1,0:T(8,128)(2,1)} %bitcast.13), channel_id=1, source_target_pairs={{0,1},{1,2},{2,3},{3,4},{4,5},{5,6},{6,7},{7,8},{8,9},{9,10},{10,1... | collective-permute-start | bytes 786440 | tf_op jit(solution)/shard_map/ppermute | solution.py:281
  7.6 0.7 %copy-start.8 = (s32[1,2]{1,0:T(1,128)S(1)}, s32[1,2]{1,0:T(1,128)}, u32[]{:S(2)}) copy-start(s32[1,2]{1,0:T(1,128)} %live_ref.1) | copy-start | bytes 28
  7.6 0.7 %copy-start.6 = (s32[1,2,4,128]{3,2,1,0:T(4,128)S(1)}, s32[1,2,4,128]{3,2,1,0:T(4,128)}, u32[]{:S(2)}) copy-start(s32[1,2,4,128]{3,2,1,0:T(4,128)} %param.13) | copy-start | bytes 12292
  7.7 0.7 %copy-start.5 = (s32[1,2,4,128]{3,2,1,0:T(4,128)S(1)}, s32[1,2,4,128]{3,2,1,0:T(4,128)}, u32[]{:S(2)}) copy-start(s32[1,2,4,128]{3,2,1,0:T(4,128)} %param.12) | copy-start | bytes 12292
  7.7 0.7 %copy-start.7 = (s32[1,2,4]{2,1,0:T(2,128)S(1)}, s32[1,2,4]{2,1,0:T(2,128)}, u32[]{:S(2)}) copy-start(s32[1,2,4]{2,1,0:T(2,128)} %param.10) | copy-start | bytes 100
  8.4 1.0 %copy-start = (bf16[512,512]{1,0:T(8,128)(2,1)S(1)}, bf16[512,512]{1,0:T(8,128)(2,1)}, u32[]{:S(2)}) copy-start(bf16[512,512]{1,0:T(8,128)(2,1)} %w_hbm.1) | copy-start | bytes 1572868
  9.4 0.9 %copy-start.2 = (bf16[1,256,512]{2,1,0:T(8,128)(2,1)S(1)}, bf16[1,256,512]{2,1,0:T(8,128)(2,1)}, u32[]{:S(2)}) copy-start(bf16[1,256,512]{2,1,0:T(8,128)(2,1)} %param.7) | copy-start | bytes 786436
  10.4 0.9 %copy-start.4 = (bf16[1,256,512]{2,1,0:T(8,128)(2,1)S(1)}, bf16[1,256,512]{2,1,0:T(8,128)(2,1)}, u32[]{:S(2)}) copy-start(bf16[1,256,512]{2,1,0:T(8,128)(2,1)} %param.8) | copy-start | bytes 786436
  11.3 7.9 %copy-start.1 = (bf16[512,512]{1,0:T(8,128)(2,1)S(1)}, bf16[512,512]{1,0:T(8,128)(2,1)}, u32[]{:S(2)}) copy-start(bf16[512,512]{1,0:T(8,128)(2,1)} %w_hbm.1) | copy-start | bytes 1572868
  11.3 7.9 %copy-start.3 = (bf16[1,256,512]{2,1,0:T(8,128)(2,1)S(1)}, bf16[1,256,512]{2,1,0:T(8,128)(2,1)}, u32[]{:S(2)}) copy-start(bf16[1,256,512]{2,1,0:T(8,128)(2,1)} %param.7) | copy-start | bytes 786436
  21.3 12.3 %collective-permute-start.2 = (bf16[256,512]{1,0:T(8,128)(2,1)S(1)}, bf16[256,512]{1,0:T(8,128)(2,1)S(1)}, u32[]{:S(2)}, u32[]{:S(2)}) collective-permute-start(bf16[256,512]{1,0:T(8,128)(2,1)S(1)} %bitcast.19), channel_id=1, source_target_pairs={{0,16},{16,0},{1,17},{17,1},{2,18},{18,2},{3,19},{19,3},{4,20},{20... | collective-permute-start | bytes 786440 | tf_op jit(solution)/shard_map/ppermute | solution.py:344
  23.6 6.1 %collective-permute-start.3 = (bf16[320,128]{1,0:T(8,128)(2,1)S(1)}, bf16[320,128]{1,0:T(8,128)(2,1)S(1)}, u32[]{:S(2)}, u32[]{:S(2)}) collective-permute-start(bf16[320,128]{1,0:T(8,128)(2,1)S(1)} %get-tuple-element.25), channel_id=1, source_target_pairs={{0,4},{1,5},{2,6},{3,7},{4,0},{5,1},{6,2},{7,3},{8,12},{9,13},{10,... | collective-permute-start | bytes 245768 | tf_op jit(solution)/shard_map/ppermute | solution.py:250
  23.7 9.8 %collective-permute-start.4 = (bf16[320,128]{1,0:T(8,128)(2,1)S(1)}, bf16[320,128]{1,0:T(8,128)(2,1)S(1)}, u32[]{:S(2)}, u32[]{:S(2)}) collective-permute-start(bf16[320,128]{1,0:T(8,128)(2,1)S(1)} %get-tuple-element.26), channel_id=1, source_target_pairs={{0,8},{1,9},{2,10},{3,11},{4,12},{5,13},{6,14},{7,15},{8,0},{9,1},... | collective-permute-start | bytes 245768 | tf_op jit(solution)/shard_map/ppermute | solution.py:250
  24.6 8.9 %collective-permute-start.5 = (bf16[320,128]{1,0:T(8,128)(2,1)S(1)}, bf16[320,128]{1,0:T(8,128)(2,1)S(1)}, u32[]{:S(2)}, u32[]{:S(2)}) collective-permute-start(bf16[320,128]{1,0:T(8,128)(2,1)S(1)} %get-tuple-element.27), channel_id=1, source_target_pairs={{0,12},{1,13},{2,14},{3,15},{4,8},{5,9},{6,10},{7,11},{8,4},{9,5},... | collective-permute-start | bytes 245768 | tf_op jit(solution)/shard_map/ppermute | solution.py:250
  33.7 4.9 %collective-permute-start.6 = (bf16[336,128]{1,0:T(8,128)(2,1)S(1)}, bf16[336,128]{1,0:T(8,128)(2,1)S(1)}, u32[]{:S(2)}, u32[]{:S(2)}) collective-permute-start(bf16[336,128]{1,0:T(8,128)(2,1)S(1)} %get-tuple-element.29), channel_id=1, source_target_pairs={{0,1},{1,0},{2,3},{3,2},{4,5},{5,4},{6,7},{7,6},{8,9},{9,8},{10,11... | collective-permute-start | bytes 258056 | tf_op jit(solution)/shard_map/ppermute | solution.py:250
  34.3 4.8 %collective-permute-start.7 = (bf16[336,128]{1,0:T(8,128)(2,1)S(1)}, bf16[336,128]{1,0:T(8,128)(2,1)S(1)}, u32[]{:S(2)}, u32[]{:S(2)}) collective-permute-start(bf16[336,128]{1,0:T(8,128)(2,1)S(1)} %get-tuple-element.30), channel_id=1, source_target_pairs={{0,2},{1,3},{2,0},{3,1},{4,6},{5,7},{6,4},{7,5},{8,10},{9,11},{10,... | collective-permute-start | bytes 258056 | tf_op jit(solution)/shard_map/ppermute | solution.py:250
  34.8 5.4 %collective-permute-start.8 = (bf16[336,128]{1,0:T(8,128)(2,1)S(1)}, bf16[336,128]{1,0:T(8,128)(2,1)S(1)}, u32[]{:S(2)}, u32[]{:S(2)}) collective-permute-start(bf16[336,128]{1,0:T(8,128)(2,1)S(1)} %get-tuple-element.31), channel_id=1, source_target_pairs={{0,3},{1,2},{2,1},{3,0},{4,7},{5,6},{6,5},{7,4},{8,11},{9,10},{10,... | collective-permute-start | bytes 258056 | tf_op jit(solution)/shard_map/ppermute | solution.py:250
  40.2 7.1 %collective-permute-start.10 = (bf16[336,128]{1,0:T(8,128)(2,1)S(1)}, bf16[336,128]{1,0:T(8,128)(2,1)S(1)}, u32[]{:S(2)}, u32[]{:S(2)}) collective-permute-start(bf16[336,128]{1,0:T(8,128)(2,1)S(1)} %shard_map.87.refs_0_), channel_id=1, source_target_pairs={{0,8},{1,9},{2,10},{3,11},{4,12},{5,13},{6,14},{7,15},{8,0},{9,1},... | collective-permute-start | bytes 258056 | tf_op jit(solution)/shard_map/ppermute | solution.py:250
  43.1 6.4 %collective-permute-start.11 = (bf16[336,128]{1,0:T(8,128)(2,1)S(1)}, bf16[336,128]{1,0:T(8,128)(2,1)S(1)}, u32[]{:S(2)}, u32[]{:S(2)}) collective-permute-start(bf16[336,128]{1,0:T(8,128)(2,1)S(1)} %shard_map.87.refs_0_), channel_id=1, source_target_pairs={{0,12},{1,13},{2,14},{3,15},{4,8},{5,9},{6,10},{7,11},{8,4},{9,5},... | collective-permute-start | bytes 258056 | tf_op jit(solution)/shard_map/ppermute | solution.py:250
  44.4 5.4 %collective-permute-start.9 = (bf16[336,128]{1,0:T(8,128)(2,1)S(1)}, bf16[336,128]{1,0:T(8,128)(2,1)S(1)}, u32[]{:S(2)}, u32[]{:S(2)}) collective-permute-start(bf16[336,128]{1,0:T(8,128)(2,1)S(1)} %shard_map.87.refs_0_), channel_id=1, source_target_pairs={{0,4},{1,5},{2,6},{3,7},{4,0},{5,1},{6,2},{7,3},{8,12},{9,13},{10,... | collective-permute-start | bytes 258056 | tf_op jit(solution)/shard_map/ppermute | solution.py:250
  49.8 5.5 %collective-permute-start.12 = (bf16[576,128]{1,0:T(8,128)(2,1)S(1)}, bf16[576,128]{1,0:T(8,128)(2,1)S(1)}, u32[]{:S(2)}, u32[]{:S(2)}) collective-permute-start(bf16[576,128]{1,0:T(8,128)(2,1)S(1)} %shard_map.88.refs_0_), channel_id=1, source_target_pairs={{0,1},{1,0},{2,3},{3,2},{4,5},{5,4},{6,7},{7,6},{8,9},{9,8},{10,11... | collective-permute-start | bytes 442376 | tf_op jit(solution)/shard_map/ppermute | solution.py:250
  51.0 5.9 %collective-permute-start.13 = (bf16[576,128]{1,0:T(8,128)(2,1)S(1)}, bf16[576,128]{1,0:T(8,128)(2,1)S(1)}, u32[]{:S(2)}, u32[]{:S(2)}) collective-permute-start(bf16[576,128]{1,0:T(8,128)(2,1)S(1)} %shard_map.88.refs_0_), channel_id=1, source_target_pairs={{0,2},{1,3},{2,0},{3,1},{4,6},{5,7},{6,4},{7,5},{8,10},{9,11},{10,... | collective-permute-start | bytes 442376 | tf_op jit(solution)/shard_map/ppermute | solution.py:250
  52.6 6.0 %collective-permute-start.14 = (bf16[576,128]{1,0:T(8,128)(2,1)S(1)}, bf16[576,128]{1,0:T(8,128)(2,1)S(1)}, u32[]{:S(2)}, u32[]{:S(2)}) collective-permute-start(bf16[576,128]{1,0:T(8,128)(2,1)S(1)} %shard_map.88.refs_0_), channel_id=1, source_target_pairs={{0,3},{1,2},{2,1},{3,0},{4,7},{5,6},{6,5},{7,4},{8,11},{9,10},{10,... | collective-permute-start | bytes 442376 | tf_op jit(solution)/shard_map/ppermute | solution.py:250
  58.7 1.6 %collective-permute-start.15 = (bf16[1024,128]{1,0:T(8,128)(2,1)S(1)}, bf16[1024,128]{1,0:T(8,128)(2,1)S(1)}, u32[]{:S(2)}, u32[]{:S(2)}) collective-permute-start(bf16[1024,128]{1,0:T(8,128)(2,1)S(1)} %shard_map.89.refs_0_), channel_id=1, source_target_pairs={{0,16},{16,0},{1,17},{17,1},{2,18},{18,2},{3,19},{19,3},{4,20},{20... | collective-permute-start | bytes 786440 | tf_op jit(solution)/shard_map/ppermute | solution.py:369

commit v4 on v3

--- a/solution.py
+++ b/solution.py
@@ -57,9 +57,22 @@
     return jnp.concatenate(parts, axis=1)
 
 
+def turn(k):
+    return (k & -k).bit_length() - 1
+
+
+def partners(k, odd, runs):
+    pairs = [(i, (i + k) % runs) for i in range(runs) if (i >> turn(k)) % 2 == odd]
+    return pairs + [(j, i) for i, j in pairs]
+
+
 def slot_start(listed, blocks, block, run, runs, reach):
     offset = lax.rem(lax.div(listed, blocks) - run + reach + runs, runs) - reach
-    order = jnp.where(offset > 0, 2 * offset - 1, -2 * offset)
+    order = 0
+    for k in range(1, reach + 1):
+        odd = lax.rem(lax.shift_right_logical(run, turn(k)), 2)
+        order = jnp.where(offset == k, k + reach * odd, order)
+        order = jnp.where(offset == -k, k + reach * (1 - odd), order)
     return (order * blocks + lax.rem(listed, blocks)) * block
 
 
@@ -89,14 +102,34 @@
     return copies
 
 
-def moment_kernel(far, near, scale, run_ref, xs_hbm, xt_hbm, w_hbm, *refs):
+def moment_kernel(
+    far, near, scale, run_ref, xs_hbm, xt_hbm, w_hbm, src_hbm, tgt_hbm, *refs
+):
     out_refs = refs[:far]
-    xs_ref, xt_ref, w_ref, packed_ref, sem = refs[far:]
-    for copy in load(((w_hbm, w_ref), (xs_hbm, xs_ref), (xt_hbm, xt_ref)), sem):
-        copy.wait()
+    src_unit_ref, src_inv_ref, tgt_unit_ref, tgt_inv_ref, src_ref, tgt_ref = refs[far : far + 6]
+    xs_ref, xt_ref, w_ref, packed_ref, sem = refs[far + 6 :]
+    copies = load(
+        (
+            (w_hbm, w_ref),
+            (xs_hbm, xs_ref),
+            (xt_hbm, xt_ref),
+            (src_hbm, src_ref),
+            (tgt_hbm, tgt_ref),
+        ),
+        sem,
+    )
+    copies[0].wait()
+    copies[1].wait()
     weight = w_ref[...]
-    zs = project(xs_ref[...], weight)[0].astype(bf16)
-    zt = project(xt_ref[...], weight)[0].astype(bf16)
+    unit, inv_norm = project(xs_ref[...], weight)
+    src_unit_ref[...] = unit
+    src_inv_ref[...] = jnp.broadcast_to(inv_norm, src_inv_ref.shape)
+    zs = unit.astype(bf16)
+    copies[2].wait()
+    unit, inv_norm = project(xt_ref[...], weight)
+    tgt_unit_ref[...] = unit
+    tgt_inv_ref[...] = jnp.broadcast_to(inv_norm, tgt_inv_ref.shape)
+    zt = unit.astype(bf16)
     moment = (dot_tn(zs, zs) + dot_tn(zt, zt)) * scale
     at = 0
     for r in range(0, moment.shape[0], lane):
@@ -110,50 +143,57 @@
     for k in range(far):
         first = lax.bitwise_xor(place, k) * rows
         out_refs[k][...] = packed_ref[pl.ds(pl.multiple_of(first, 16), rows), :]
+    copies[3].wait()
+    copies[4].wait()
 
 
 def own_kernel(
     runs, reach,
-    run_ref, list_ref, live_ref, xs_ref, xt_ref, w_ref, src_ref, tgt_ref,
-    unit_ref, inv_ref, count_ref, grad_ref, part_ref,
+    run_ref, list_ref, live_ref, xt_ref, src_unit_ref, tgt_unit_ref, tgt_inv_ref, src_ref, tgt_ref,
+    even_ref, odd_ref, grad_ref, part_ref,
 ):
-    weight = w_ref[...]
-    src_unit, src_inv = project(xs_ref[...], weight)
-    tgt_unit, tgt_inv = project(xt_ref[...], weight)
-    zs = src_unit.astype(bf16)
-    zt = tgt_unit.astype(bf16)
-    unit_ref[...] = src_unit
-    inv_ref[...] = jnp.broadcast_to(src_inv, inv_ref.shape)
-    own = xs_ref.shape[0]
+    zs = src_unit_ref[...].astype(bf16)
+    own = xt_ref.shape[0]
     block = own // src_ref.shape[0]
     counts = pair_counts(
         list_ref, live_ref, src_ref, tgt_ref, block, run_ref[0], runs, reach
     )
-    count_ref[...] = counts[:, own:].astype(bf16)
-    weights = pair_weights(zs, zt, counts[:, :own], block)
-    grad_ref[...] = dot_nn(weights, zt)
+    far = own * (1 + reach)
+    even_ref[...] = counts[:, own:far].astype(bf16)
+    odd_ref[...] = counts[:, far:].astype(bf16)
+    grad_ref[...], part_ref[...] = score(
+        xt_ref[...], tgt_unit_ref[...], tgt_inv_ref[:, :1], zs, counts[:, :own], block
+    )
+
+
+def score(rows, unit, inv_norm, zs, counts, block):
+    zt = unit.astype(bf16)
+    weights = pair_weights(zs, zt, counts, block)
     grad_zt = dot_tn(weights, zs) * inverse_sharpness
-    part_ref[...] = dot_tn(xt_ref[...], back_norm(tgt_unit, tgt_inv, grad_zt))
-
-
-def halo_kernel(
+    return dot_nn(weights, zt), dot_tn(rows, back_norm(unit, inv_norm, grad_zt))
+
+
+def even_kernel(reach, block, w_ref, unit_ref, count_ref, grad_ref, part_ref, *refs):
+    out_grad_ref, out_part_ref = refs[reach:]
+    rows = jnp.concatenate([ref[...] for ref in refs[:reach]], axis=0)
+    zs = unit_ref[...].astype(bf16)
+    grad, part = score(rows, *project(rows, w_ref[...]), zs, count_ref[...], block)
+    out_grad_ref[...] = grad_ref[...] + grad
+    out_part_ref[...] = part_ref[...] + part
+
+
+def odd_kernel(
     reach, block, groups,
     grp_ref, xs_ref, w_ref, unit_ref, inv_ref, count_ref, grad_ref, part_ref, *refs,
 ):
-    nbr_refs = refs[: 2 * reach]
-    keep_ref, send_ref, total_ref = refs[2 * reach :]
-    weight = w_ref[...]
-    rows = jnp.concatenate([ref[...] for ref in nbr_refs], axis=0)
-    tgt_unit, tgt_inv = project(rows, weight)
-    zt = tgt_unit.astype(bf16)
-    src_unit = unit_ref[...]
-    zs = src_unit.astype(bf16)
-    weights = pair_weights(zs, zt, count_ref[...], block)
-    grad_zs = (grad_ref[...] + dot_nn(weights, zt)) * inverse_sharpness
-    grad_zt = dot_tn(weights, zs) * inverse_sharpness
-    src_grad = back_norm(src_unit, inv_ref[:, :1], grad_zs)
-    tgt_grad = back_norm(tgt_unit, tgt_inv, grad_zt)
-    total_ref[...] = part_ref[...] + dot_tn(xs_ref[...], src_grad) + dot_tn(rows, tgt_grad)
+    keep_ref, send_ref, total_ref = refs[reach:]
+    rows = jnp.concatenate([ref[...] for ref in refs[:reach]], axis=0)
+    unit = unit_ref[...]
+    zs = unit.astype(bf16)
+    grad, part = score(rows, *project(rows, w_ref[...]), zs, count_ref[...], block)
+    grad_zs = (grad_ref[...] + grad) * inverse_sharpness
+    src_grad = back_norm(unit, inv_ref[:, :1], grad_zs)
+    total_ref[...] = part_ref[...] + part + dot_tn(xs_ref[...], src_grad)
     chunk = total_ref.shape[0] // groups
     me = grp_ref[0]
     keep_ref[...] = total_ref[pl.ds(pl.multiple_of(me * chunk, chunk), chunk), :]
@@ -275,10 +315,9 @@
     run = lax.axis_index("blk")
     grp = lax.axis_index("grp")
 
-    nbrs = []
-    for k in range(1, reach + 1):
-        nbrs.append(lax.ppermute(xt, "blk", [(i, (i - k) % runs) for i in range(runs)]))
-        nbrs.append(lax.ppermute(xt, "blk", [(i, (i + k) % runs) for i in range(runs)]))
+    hops = range(1, reach + 1)
+    odd = [lax.ppermute(xt, "blk", partners(k, 1, runs)) for k in hops]
+    even = [lax.ppermute(xt, "blk", partners(k, 0, runs)) for k in hops]
 
     tiles = width // lane
     near = 1 << (runs.bit_length() // 2)
@@ -294,51 +333,67 @@
     run_id = run.reshape(1)
     grp_id = grp.reshape(1)
 
-    pieces = pl.pallas_call(
+    far_away = [
+        pltpu.with_memory_space_constraint(array, pltpu.HBM)
+        for array in (xs, xt, proj_weight, pair_src[0], pair_tgt[0])
+    ]
+    *pieces, unit, inv, tgt_unit, tgt_inv, sources, targets = pl.pallas_call(
         functools.partial(moment_kernel, far, near, scale),
-        out_shape=(jax.ShapeDtypeStruct((column_rows, lane), bf16),) * far,
-        in_specs=[smem] + [hbm] * 3,
-        out_specs=(vmem,) * far,
+        out_shape=(jax.ShapeDtypeStruct((column_rows, lane), bf16),) * far
+        + (jax.ShapeDtypeStruct((points, width), f32), jax.ShapeDtypeStruct((points, lane), f32))
+        * 2
+        + (jax.ShapeDtypeStruct(pair_src.shape[1:], jnp.int32),) * 2,
+        in_specs=[smem] + [hbm] * 5,
+        out_specs=(vmem,) * (far + 6),
         scratch_shapes=[
             pltpu.VMEM((points, width), bf16),
             pltpu.VMEM((points, width), bf16),
             pltpu.VMEM((width, width), bf16),
             pltpu.VMEM((far * column_rows, lane), bf16),
-            pltpu.SemaphoreType.DMA((3,)),
+            pltpu.SemaphoreType.DMA((5,)),
         ],
         compiler_params=room(16),
         name="moment",
-    )(run_id, *(pltpu.with_memory_space_constraint(a, pltpu.HBM) for a in (xs, xt, proj_weight)))
+    )(run_id, *far_away)
     pieces = [pieces[0]] + [swap(pieces[k], k * near, runs) for k in range(1, far)]
-    unit, inv, counts, grad, part = pl.pallas_call(
+    even_count, odd_count, grad, part = pl.pallas_call(
         functools.partial(own_kernel, runs, reach),
         out_shape=(
-            jax.ShapeDtypeStruct((points, width), f32),
-            jax.ShapeDtypeStruct((points, lane), f32),
-            jax.ShapeDtypeStruct((points, 2 * reach * points), bf16),
+            jax.ShapeDtypeStruct((points, reach * points), bf16),
+            jax.ShapeDtypeStruct((points, reach * points), bf16),
             jax.ShapeDtypeStruct((points, width), f32),
             jax.ShapeDtypeStruct((width, width), f32),
         ),
-        in_specs=[smem] * 3 + [vmem] * 5,
-        out_specs=(vmem,) * 5,
+        in_specs=[smem] * 3 + [vmem] * 6,
+        out_specs=(vmem,) * 4,
         compiler_params=room(16 + 4 * reach),
         name="own",
     )(
-        run_id, match_blocks[0], match_count, xs, xt, proj_weight,
-        pair_src[0], pair_tgt[0],
-    )
+        run_id, match_blocks[0], match_count, xt, unit, tgt_unit, tgt_inv, sources, targets
+    )
+    grad, part = pl.pallas_call(
+        functools.partial(even_kernel, reach, block),
+        out_shape=(
+            jax.ShapeDtypeStruct((points, width), f32),
+            jax.ShapeDtypeStruct((width, width), f32),
+        ),
+        in_specs=[vmem] * (5 + reach),
+        out_specs=(vmem, vmem),
+        compiler_params=room(16 + 4 * reach),
+        name="even",
+    )(proj_weight, unit, even_count, grad, part, *even)
     keep, send = pl.pallas_call(
-        functools.partial(halo_kernel, reach, block, groups),
+        functools.partial(odd_kernel, reach, block, groups),
         out_shape=(
             jax.ShapeDtypeStruct((chunk, width), f32),
             jax.ShapeDtypeStruct((groups - 1, chunk, width), bf16),
         ),
-        in_specs=[smem] + [vmem] * (7 + 2 * reach),
+        in_specs=[smem] + [vmem] * (7 + reach),
         out_specs=(vmem, vmem),
         scratch_shapes=[pltpu.VMEM((width, width), f32)],
-        compiler_params=room(16 + 8 * reach),
-        name="halo",
-    )(grp_id, xs, proj_weight, unit, inv, counts, grad, part, *nbrs)
+        compiler_params=room(16 + 4 * reach),
+        name="odd",
+    )(grp_id, xs, proj_weight, unit, inv, odd_count, grad, part, *odd)
 
     got = [
         lax.ppermute(send[k - 1], "grp", [(i, (i + k) % groups) for i in range(groups)])

time: 61.6 us -> 59.1 us (0.959)
  local copies, waits for them, and re-layouts: 3.66 us -> 0.67 us
  waiting for transfers between devices: 24.9 us -> 23 us
  starting transfers between devices: 22.9 us -> 24.3 us
  Pallas kernels: 9.17 us -> 10.2 us
    ppermute x2, waiting for transfers between devices: 5.46 us -> 1.72 us  [the longest x1 1.72 us: body(): even = [lax.ppermute(xt, 'blk', partners(k, 0, runs)) for k in hops]]
    unnamed x18 -> x10, local copies, waits for them, and re-layouts: 3.66 us -> 0.67 us
    ppermute x12, waiting for transfers between devices: 19.1 us -> 20.9 us  [swap(): return lax.ppermute(array, 'blk', [(i, i ^ bits) for i in range(runs)])]
    pallas_call x1 -> x2, Pallas kernels: 2.04 us -> 3.16 us  [the longest x1 1.75 us: body(): pl.pallas_call(functools.partial(odd_kernel, reach, block, groups), out_s...]
    ppermute x12, starting transfers between devices: 15.7 us -> 16.6 us  [swap(): return lax.ppermute(array, 'blk', [(i, i ^ bits) for i in range(runs)])]
  transfers between devices with their start and end apart: 16 -> 16, of which waited for: 13 -> 12; matrix products, arithmetic and copies ran while one was open for 0% -> 0% of each run, Pallas kernels for 10% -> 12%
where the time goes in v4:
time: 59.1 us; the launch traced here: 58.9 us
  starting transfers between devices  24.3 us (41%)
  waiting for transfers between devices  23 us (39%)
  Pallas kernels  10.2 us (17%)
  between operations  0.75 us (1%)
  local copies, waits for them, and re-layouts  0.67 us (1%)
    ppermute x12, waiting for transfers between devices, swap(): return lax.ppermute(array, 'blk', [(i, i ^ bits) for i in range(runs)])  20.9 us
    ppermute x12, starting transfers between devices, swap(): return lax.ppermute(array, 'blk', [(i, i ^ bits) for i in range(runs)])  16.6 us
    ppermute x1, starting transfers between devices, body(): odd = [lax.ppermute(xt, 'blk', partners(k, 1, runs)) for k in hops]  4.53 us
    ppermute x1, starting transfers between devices, body(): even = [lax.ppermute(xt, 'blk', partners(k, 0, runs)) for k in hops]  3.03 us
    pallas_call x1, Pallas kernels, body(): pl.pallas_call(functools.partial(moment_kernel, far, near, scale), out_sh...  2.45 us
    pallas_call x1, Pallas kernels, body(): pl.pallas_call(functools.partial(own_kernel, runs, reach), out_shape=(jax...  2.09 us
    pallas_call x1, Pallas kernels, body(): pl.pallas_call(functools.partial(odd_kernel, reach, block, groups), out_s...  1.75 us
    ppermute x1, waiting for transfers between devices, body(): even = [lax.ppermute(xt, 'blk', partners(k, 0, runs)) for k in hops]  1.72 us
  transfers between devices with their start and end apart: 16, of which 12 were waited for; matrix products, arithmetic and copies ran while one was open for 0% of the time, Pallas kernels for 12%

profile of v4, /device:TPU:0, one launch (start us, length us, event | category | flops | bytes accessed | tf_op | source)
XLA Modules:
  0.0 58.9 jit_solution(17633052233345383139)
XLA Ops:
  0.6 3.0 %collective-permute-start = (bf16[256,512]{1,0:T(8,128)(2,1)}, bf16[256,512]{1,0:T(8,128)(2,1)S(1)}, u32[]{:S(2)}, u32[]{:S(2)}) collective-permute-start(bf16[256,512]{1,0:T(8,128)(2,1)} %bitcast.11), channel_id=1, source_target_pairs={{0,1},{2,3},{4,5},{6,7},{8,9},{10,11},{12,13},{14,15},{1,0},{3,2},... | collective-permute-start | bytes 786440 | tf_op jit(solution)/shard_map/ppermute | solution.py:320
  3.7 4.5 %collective-permute-start.1 = (bf16[256,512]{1,0:T(8,128)(2,1)}, bf16[256,512]{1,0:T(8,128)(2,1)S(1)}, u32[]{:S(2)}, u32[]{:S(2)}) collective-permute-start(bf16[256,512]{1,0:T(8,128)(2,1)} %bitcast.12), channel_id=1, source_target_pairs={{1,2},{3,4},{5,6},{7,8},{9,10},{11,12},{13,14},{15,0},{2,1},{4,3},... | collective-permute-start | bytes 786440 | tf_op jit(solution)/shard_map/ppermute | solution.py:319
  8.2 0.0 copy-start.2
  8.2 2.5 %moment.1 = (bf16[320,128]{1,0:T(8,128)(2,1)S(1)}, bf16[320,128]{1,0:T(8,128)(2,1)S(1)}, bf16[320,128]{1,0:T(8,128)(2,1)S(1)}, bf16[320,128]{1,0:T(8,128)(2,1)S(...) custom-call(s32[1]{0:T(128)} %bitcast.run_ref, ...), custom_call_target="tpu_custom_call" | custom-call | tf_op jit(solution)/shard_map/moment/pallas_call | solution.py:340
  10.7 0.0 copy-start.3
  10.7 0.0 copy-start.4
  10.7 0.0 copy-done.2
  10.7 0.6 %copy-done.3 = s32[1,2,4]{2,1,0:T(2,128)S(1)} copy-done((s32[1,2,4]{2,1,0:T(2,128)S(1)}, s32[1,2,4]{2,1,0:T(2,128)}, u32[]{:S(2)}) %copy-start.3) | copy-done | bytes 56
  11.3 0.0 copy-done.4
  11.3 0.0 copy-start
  11.3 2.1 %own.1 = (bf16[256,256]{1,0:T(8,128)(2,1)S(1)}, bf16[256,256]{1,0:T(8,128)(2,1)S(1)}, f32[256,512]{1,0:T(8,128)S(1)}, f32[512,512]{1,0:T(8,128)S(1)}) custom-call(s32[1]{0:T(128)} %bitcast.run_ref, s32[2,4]{1,0:T(2,128)S(1)} %bitcast.15, s32[1,2]{1,0:T(1,128)S(1)} %copy-done.4, bf16[256,512]{1,0:T(8,128)(2,1)S(1)} %bitcast.14, ...), custom_call_target="tpu_custom_call" | custom-call | tf_op jit(solution)/shard_map/own/pallas_call | solution.py:359
  13.4 1.7 %collective-permute-done.refs_0_ = bf16[256,512]{1,0:T(8,128)(2,1)S(1)} collective-permute-done((bf16[256,512]{1,0:T(8,128)(2,1)}, bf16[256,512]{1,0:T(8,128)(2,1)S(1)}, u32[]{:S(2)}, u32[]{:S(2)}) %collective-permute-start) | collective-permute-done | bytes 262176 | tf_op jit(solution)/shard_map/ppermute | solution.py:320
  15.2 0.0 copy-done
  15.2 1.4 %even.1 = (f32[256,512]{1,0:T(8,128)S(1)}, f32[512,512]{1,0:T(8,128)S(1)}) custom-call(bf16[512,512]{1,0:T(8,128)(2,1)S(1)} %copy-done, f32[256,512]{1,0:T(8,128)S(1)} %get-tuple-element.24.src_unit_ref.unit_ref, bf16[256,256]{1,0:T(8,128)(2,1)S(1)} %get-tuple-element.31.count_ref, f32[256,512]{1,0:T(8,128)S(1)} %get-tuple-element.32.grad_ref, ...), custom_call_target="tpu_custom_call" | custom-call | tf_op jit(solution)/shard_map/even/pallas_call | solution.py:374
  16.6 0.0 collective-permute-done.1.refs_0_
  16.6 0.0 copy-done.1
  16.6 1.8 %odd.1 = (f32[256,512]{1,0:T(8,128)S(1)}, bf16[1,256,512]{2,1,0:T(8,128)(2,1)S(1)}) custom-call(s32[1]{0:T(128)} %bitcast.1.grp_ref, bf16[256,512]{1,0:T(8,128)(2,1)S(1)} %bitcast.10, bf16[512,512]{1,0:T(8,128)(2,1)S(1)} %copy-done, f32[256,512]{1,0:T(8,128)S(1)} %get-tuple-element.24.src_unit_ref.unit_ref, f32[256,128]{1,0:T(8,128)S(1)} %get-tuple-element.25.inv_ref, ...), custom_call_target="tpu_custom_call" | custom-call | tf_op jit(solution)/shard_map/odd/pallas_call | solution.py:385
  18.4 0.1 collective-permute-start.2
  18.4 1.6 %collective-permute-start.3 = (bf16[320,128]{1,0:T(8,128)(2,1)S(1)}, bf16[320,128]{1,0:T(8,128)(2,1)S(1)}, u32[]{:S(2)}, u32[]{:S(2)}) collective-permute-start(bf16[320,128]{1,0:T(8,128)(2,1)S(1)} %get-tuple-element.39), channel_id=1, source_target_pairs={{0,4},{1,5},{2,6},{3,7},{4,0},{5,1},{6,2},{7,3},{8,12},{9,13},{10,... | collective-permute-start | bytes 245768 | tf_op jit(solution)/shard_map/ppermute | solution.py:290
  20.1 2.6 %collective-permute-start.4 = (bf16[320,128]{1,0:T(8,128)(2,1)S(1)}, bf16[320,128]{1,0:T(8,128)(2,1)S(1)}, u32[]{:S(2)}, u32[]{:S(2)}) collective-permute-start(bf16[320,128]{1,0:T(8,128)(2,1)S(1)} %get-tuple-element.40), channel_id=1, source_target_pairs={{0,8},{1,9},{2,10},{3,11},{4,12},{5,13},{6,14},{7,15},{8,0},{9,1},... | collective-permute-start | bytes 245768 | tf_op jit(solution)/shard_map/ppermute | solution.py:290
  22.7 0.2 collective-permute-start.5
  22.9 0.4 collective-permute-done.3.refs_3_
  23.3 6.3 %collective-permute-done.4.refs_4_ = bf16[320,128]{1,0:T(8,128)(2,1)S(1)} collective-permute-done((bf16[320,128]{1,0:T(8,128)(2,1)S(1)}, bf16[320,128]{1,0:T(8,128)(2,1)S(1)}, u32[]{:S(2)}, u32[]{:S(2)}) %collective-permute-start.4) | collective-permute-done | bytes 81952 | tf_op jit(solution)/shard_map/ppermute | solution.py:290
  29.6 0.0 collective-permute-done.5.refs_5_
  29.6 0.0 collective-permute-done.2.refs_1_
  29.6 0.1 shard_map.86
  29.7 2.4 %collective-permute-start.6 = (bf16[336,128]{1,0:T(8,128)(2,1)S(1)}, bf16[336,128]{1,0:T(8,128)(2,1)S(1)}, u32[]{:S(2)}, u32[]{:S(2)}) collective-permute-start(bf16[336,128]{1,0:T(8,128)(2,1)S(1)} %get-tuple-element.43), channel_id=1, source_target_pairs={{0,1},{1,0},{2,3},{3,2},{4,5},{5,4},{6,7},{7,6},{8,9},{9,8},{10,11... | collective-permute-start | bytes 258056 | tf_op jit(solution)/shard_map/ppermute | solution.py:290
  32.2 0.1 collective-permute-start.7
  32.3 1.4 %collective-permute-start.8 = (bf16[336,128]{1,0:T(8,128)(2,1)S(1)}, bf16[336,128]{1,0:T(8,128)(2,1)S(1)}, u32[]{:S(2)}, u32[]{:S(2)}) collective-permute-start(bf16[336,128]{1,0:T(8,128)(2,1)S(1)} %get-tuple-element.45), channel_id=1, source_target_pairs={{0,3},{1,2},{2,1},{3,0},{4,7},{5,6},{6,5},{7,4},{8,11},{9,10},{10,... | collective-permute-start | bytes 258056 | tf_op jit(solution)/shard_map/ppermute | solution.py:290
  33.7 1.6 %collective-permute-done.6.refs_1_ = bf16[336,128]{1,0:T(8,128)(2,1)S(1)} collective-permute-done((bf16[336,128]{1,0:T(8,128)(2,1)S(1)}, bf16[336,128]{1,0:T(8,128)(2,1)S(1)}, u32[]{:S(2)}, u32[]{:S(2)}) %collective-permute-start.6) | collective-permute-done | bytes 86048 | tf_op jit(solution)/shard_map/ppermute | solution.py:290
  35.3 1.3 %collective-permute-done.7.refs_2_ = bf16[336,128]{1,0:T(8,128)(2,1)S(1)} collective-permute-done((bf16[336,128]{1,0:T(8,128)(2,1)S(1)}, bf16[336,128]{1,0:T(8,128)(2,1)S(1)}, u32[]{:S(2)}, u32[]{:S(2)}) %collective-permute-start.7) | collective-permute-done | bytes 86048 | tf_op jit(solution)/shard_map/ppermute | solution.py:290
  36.7 1.0 %collective-permute-done.8.refs_3_ = bf16[336,128]{1,0:T(8,128)(2,1)S(1)} collective-permute-done((bf16[336,128]{1,0:T(8,128)(2,1)S(1)}, bf16[336,128]{1,0:T(8,128)(2,1)S(1)}, u32[]{:S(2)}, u32[]{:S(2)}) %collective-permute-start.8) | collective-permute-done | bytes 86048 | tf_op jit(solution)/shard_map/ppermute | solution.py:290
  37.7 2.2 %collective-permute-start.9 = (bf16[336,128]{1,0:T(8,128)(2,1)S(1)}, bf16[336,128]{1,0:T(8,128)(2,1)S(1)}, u32[]{:S(2)}, u32[]{:S(2)}) collective-permute-start(bf16[336,128]{1,0:T(8,128)(2,1)S(1)} %shard_map.87.refs_0_), channel_id=1, source_target_pairs={{0,4},{1,5},{2,6},{3,7},{4,0},{5,1},{6,2},{7,3},{8,12},{9,13},{10,... | collective-permute-start | bytes 258056 | tf_op jit(solution)/shard_map/ppermute | solution.py:290
  39.9 1.2 %collective-permute-start.10 = (bf16[336,128]{1,0:T(8,128)(2,1)S(1)}, bf16[336,128]{1,0:T(8,128)(2,1)S(1)}, u32[]{:S(2)}, u32[]{:S(2)}) collective-permute-start(bf16[336,128]{1,0:T(8,128)(2,1)S(1)} %shard_map.87.refs_0_), channel_id=1, source_target_pairs={{0,8},{1,9},{2,10},{3,11},{4,12},{5,13},{6,14},{7,15},{8,0},{9,1},... | collective-permute-start | bytes 258056 | tf_op jit(solution)/shard_map/ppermute | solution.py:290
  41.1 1.3 %collective-permute-start.11 = (bf16[336,128]{1,0:T(8,128)(2,1)S(1)}, bf16[336,128]{1,0:T(8,128)(2,1)S(1)}, u32[]{:S(2)}, u32[]{:S(2)}) collective-permute-start(bf16[336,128]{1,0:T(8,128)(2,1)S(1)} %shard_map.87.refs_0_), channel_id=1, source_target_pairs={{0,12},{1,13},{2,14},{3,15},{4,8},{5,9},{6,10},{7,11},{8,4},{9,5},... | collective-permute-start | bytes 258056 | tf_op jit(solution)/shard_map/ppermute | solution.py:290
  42.4 0.4 collective-permute-done.9.refs_1_
  42.8 5.2 %collective-permute-done.10.refs_2_ = bf16[336,128]{1,0:T(8,128)(2,1)S(1)} collective-permute-done((bf16[336,128]{1,0:T(8,128)(2,1)S(1)}, bf16[336,128]{1,0:T(8,128)(2,1)S(1)}, u32[]{:S(2)}, u32[]{:S(2)}) %collective-permute-start.10) | collective-permute-done | bytes 86048 | tf_op jit(solution)/shard_map/ppermute | solution.py:290
  48.0 0.0 collective-permute-done.11.refs_3_
  48.1 1.4 %collective-permute-start.12 = (bf16[576,128]{1,0:T(8,128)(2,1)S(1)}, bf16[576,128]{1,0:T(8,128)(2,1)S(1)}, u32[]{:S(2)}, u32[]{:S(2)}) collective-permute-start(bf16[576,128]{1,0:T(8,128)(2,1)S(1)} %shard_map.88.refs_0_), channel_id=1, source_target_pairs={{0,1},{1,0},{2,3},{3,2},{4,5},{5,4},{6,7},{7,6},{8,9},{9,8},{10,11... | collective-permute-start | bytes 442376 | tf_op jit(solution)/shard_map/ppermute | solution.py:290
  49.5 0.6 %collective-permute-start.13 = (bf16[576,128]{1,0:T(8,128)(2,1)S(1)}, bf16[576,128]{1,0:T(8,128)(2,1)S(1)}, u32[]{:S(2)}, u32[]{:S(2)}) collective-permute-start(bf16[576,128]{1,0:T(8,128)(2,1)S(1)} %shard_map.88.refs_0_), channel_id=1, source_target_pairs={{0,2},{1,3},{2,0},{3,1},{4,6},{5,7},{6,4},{7,5},{8,10},{9,11},{10,... | collective-permute-start | bytes 442376 | tf_op jit(solution)/shard_map/ppermute | solution.py:290
  50.1 1.5 %collective-permute-start.14 = (bf16[576,128]{1,0:T(8,128)(2,1)S(1)}, bf16[576,128]{1,0:T(8,128)(2,1)S(1)}, u32[]{:S(2)}, u32[]{:S(2)}) collective-permute-start(bf16[576,128]{1,0:T(8,128)(2,1)S(1)} %shard_map.88.refs_0_), channel_id=1, source_target_pairs={{0,3},{1,2},{2,1},{3,0},{4,7},{5,6},{6,5},{7,4},{8,11},{9,10},{10,... | collective-permute-start | bytes 442376 | tf_op jit(solution)/shard_map/ppermute | solution.py:290
  51.6 1.7 %collective-permute-done.12.refs_1_ = bf16[576,128]{1,0:T(8,128)(2,1)S(1)} collective-permute-done((bf16[576,128]{1,0:T(8,128)(2,1)S(1)}, bf16[576,128]{1,0:T(8,128)(2,1)S(1)}, u32[]{:S(2)}, u32[]{:S(2)}) %collective-permute-start.12) | collective-permute-done | bytes 147488 | tf_op jit(solution)/shard_map/ppermute | solution.py:290
  53.3 1.4 %collective-permute-done.13.refs_2_ = bf16[576,128]{1,0:T(8,128)(2,1)S(1)} collective-permute-done((bf16[576,128]{1,0:T(8,128)(2,1)S(1)}, bf16[576,128]{1,0:T(8,128)(2,1)S(1)}, u32[]{:S(2)}, u32[]{:S(2)}) %collective-permute-start.13) | collective-permute-done | bytes 147488 | tf_op jit(solution)/shard_map/ppermute | solution.py:290
  54.7 1.6 %collective-permute-done.14.refs_3_ = bf16[576,128]{1,0:T(8,128)(2,1)S(1)} collective-permute-done((bf16[576,128]{1,0:T(8,128)(2,1)S(1)}, bf16[576,128]{1,0:T(8,128)(2,1)S(1)}, u32[]{:S(2)}, u32[]{:S(2)}) %collective-permute-start.14) | collective-permute-done | bytes 147488 | tf_op jit(solution)/shard_map/ppermute | solution.py:290
  56.3 0.1 collective-permute-start.15
  56.3 1.2 %shard_map.91 = f32[512,512]{1,0:T(8,128)} custom-call(s32[1]{0:T(128)} %bitcast.run_ref, bf16[576,128]{1,0:T(8,128)(2,1)S(1)} %shard_map.88.refs_0_, bf16[576,128]{1,0:T(8,128)(2,1)S(1)} %collective-permute-done.12.refs_1_, bf16[576,128]{1,0:T(8,128)(2,1)S(1)} %collective-permute-done.13.refs_2_, bf16[576,128]{1,0:T(8,128)(2,1)S(1)} %collective-permute-done.14.refs_3_), custom_call_target="tpu_custom_call" | custom-call | tf_op jit(solution)/shard_map/pallas_call | solution.py:427
  57.5 0.4 collective-permute-done.15.refs_1_
  57.9 1.0 %shard_map.90 = f32[512,512]{1,0:T(8,128)} custom-call(s32[1]{0:T(128)} %bitcast.run_ref, s32[1]{0:T(128)} %bitcast.1.grp_ref, bf16[1024,128]{1,0:T(8,128)(2,1)S(1)} %shard_map.89.refs_0_, bf16[1024,128]{1,0:T(8,128)(2,1)S(1)} %collective-permute-done.15.refs_1_), custom_call_target="tpu_custom_call" | custom-call | tf_op jit(solution)/shard_map/pallas_call | solution.py:433
  (4 shorter events, 0.1 us)
Async XLA Ops:
  0.6 14.5 %collective-permute-start = (bf16[256,512]{1,0:T(8,128)(2,1)}, bf16[256,512]{1,0:T(8,128)(2,1)S(1)}, u32[]{:S(2)}, u32[]{:S(2)}) collective-permute-start(bf16[256,512]{1,0:T(8,128)(2,1)} %bitcast.11), channel_id=1, source_target_pairs={{0,1},{2,3},{4,5},{6,7},{8,9},{10,11},{12,13},{14,15},{1,0},{3,2},... | collective-permute-start | bytes 786440 | tf_op jit(solution)/shard_map/ppermute | solution.py:320
  3.7 12.9 %collective-permute-start.1 = (bf16[256,512]{1,0:T(8,128)(2,1)}, bf16[256,512]{1,0:T(8,128)(2,1)S(1)}, u32[]{:S(2)}, u32[]{:S(2)}) collective-permute-start(bf16[256,512]{1,0:T(8,128)(2,1)} %bitcast.12), channel_id=1, source_target_pairs={{1,2},{3,4},{5,6},{7,8},{9,10},{11,12},{13,14},{15,0},{2,1},{4,3},... | collective-permute-start | bytes 786440 | tf_op jit(solution)/shard_map/ppermute | solution.py:319
  8.2 2.5 %copy-start.2 = (bf16[1,256,512]{2,1,0:T(8,128)(2,1)S(1)}, bf16[1,256,512]{2,1,0:T(8,128)(2,1)}, u32[]{:S(2)}) copy-start(bf16[1,256,512]{2,1,0:T(8,128)(2,1)} %param.8) | copy-start | bytes 786436
  10.7 0.7 %copy-start.3 = (s32[1,2,4]{2,1,0:T(2,128)S(1)}, s32[1,2,4]{2,1,0:T(2,128)}, u32[]{:S(2)}) copy-start(s32[1,2,4]{2,1,0:T(2,128)} %param.10) | copy-start | bytes 100
  10.7 0.7 %copy-start.4 = (s32[1,2]{1,0:T(1,128)S(1)}, s32[1,2]{1,0:T(1,128)}, u32[]{:S(2)}) copy-start(s32[1,2]{1,0:T(1,128)} %live_ref.1) | copy-start | bytes 28
  11.3 3.8 %copy-start = (bf16[512,512]{1,0:T(8,128)(2,1)S(1)}, bf16[512,512]{1,0:T(8,128)(2,1)}, u32[]{:S(2)}) copy-start(bf16[512,512]{1,0:T(8,128)(2,1)} %w_ref.3) | copy-start | bytes 1572868
  15.2 1.4 %copy-start.1 = (bf16[1,256,512]{2,1,0:T(8,128)(2,1)S(1)}, bf16[1,256,512]{2,1,0:T(8,128)(2,1)}, u32[]{:S(2)}) copy-start(bf16[1,256,512]{2,1,0:T(8,128)(2,1)} %param.7) | copy-start | bytes 786436
  18.4 11.2 %collective-permute-start.2 = (bf16[256,512]{1,0:T(8,128)(2,1)S(1)}, bf16[256,512]{1,0:T(8,128)(2,1)S(1)}, u32[]{:S(2)}, u32[]{:S(2)}) collective-permute-start(bf16[256,512]{1,0:T(8,128)(2,1)S(1)} %bitcast.16), channel_id=1, source_target_pairs={{0,16},{16,0},{1,17},{17,1},{2,18},{18,2},{3,19},{19,3},{4,20},{20... | collective-permute-start | bytes 786440 | tf_op jit(solution)/shard_map/ppermute | solution.py:399
  18.4 4.8 %collective-permute-start.3 = (bf16[320,128]{1,0:T(8,128)(2,1)S(1)}, bf16[320,128]{1,0:T(8,128)(2,1)S(1)}, u32[]{:S(2)}, u32[]{:S(2)}) collective-permute-start(bf16[320,128]{1,0:T(8,128)(2,1)S(1)} %get-tuple-element.39), channel_id=1, source_target_pairs={{0,4},{1,5},{2,6},{3,7},{4,0},{5,1},{6,2},{7,3},{8,12},{9,13},{10,... | collective-permute-start | bytes 245768 | tf_op jit(solution)/shard_map/ppermute | solution.py:290
  20.1 9.5 %collective-permute-start.4 = (bf16[320,128]{1,0:T(8,128)(2,1)S(1)}, bf16[320,128]{1,0:T(8,128)(2,1)S(1)}, u32[]{:S(2)}, u32[]{:S(2)}) collective-permute-start(bf16[320,128]{1,0:T(8,128)(2,1)S(1)} %get-tuple-element.40), channel_id=1, source_target_pairs={{0,8},{1,9},{2,10},{3,11},{4,12},{5,13},{6,14},{7,15},{8,0},{9,1},... | collective-permute-start | bytes 245768 | tf_op jit(solution)/shard_map/ppermute | solution.py:290
  22.7 6.9 %collective-permute-start.5 = (bf16[320,128]{1,0:T(8,128)(2,1)S(1)}, bf16[320,128]{1,0:T(8,128)(2,1)S(1)}, u32[]{:S(2)}, u32[]{:S(2)}) collective-permute-start(bf16[320,128]{1,0:T(8,128)(2,1)S(1)} %get-tuple-element.41), channel_id=1, source_target_pairs={{0,12},{1,13},{2,14},{3,15},{4,8},{5,9},{6,10},{7,11},{8,4},{9,5},... | collective-permute-start | bytes 245768 | tf_op jit(solution)/shard_map/ppermute | solution.py:290
  29.7 5.6 %collective-permute-start.6 = (bf16[336,128]{1,0:T(8,128)(2,1)S(1)}, bf16[336,128]{1,0:T(8,128)(2,1)S(1)}, u32[]{:S(2)}, u32[]{:S(2)}) collective-permute-start(bf16[336,128]{1,0:T(8,128)(2,1)S(1)} %get-tuple-element.43), channel_id=1, source_target_pairs={{0,1},{1,0},{2,3},{3,2},{4,5},{5,4},{6,7},{7,6},{8,9},{9,8},{10,11... | collective-permute-start | bytes 258056 | tf_op jit(solution)/shard_map/ppermute | solution.py:290
  32.2 4.5 %collective-permute-start.7 = (bf16[336,128]{1,0:T(8,128)(2,1)S(1)}, bf16[336,128]{1,0:T(8,128)(2,1)S(1)}, u32[]{:S(2)}, u32[]{:S(2)}) collective-permute-start(bf16[336,128]{1,0:T(8,128)(2,1)S(1)} %get-tuple-element.44), channel_id=1, source_target_pairs={{0,2},{1,3},{2,0},{3,1},{4,6},{5,7},{6,4},{7,5},{8,10},{9,11},{10,... | collective-permute-start | bytes 258056 | tf_op jit(solution)/shard_map/ppermute | solution.py:290
  32.3 5.4 %collective-permute-start.8 = (bf16[336,128]{1,0:T(8,128)(2,1)S(1)}, bf16[336,128]{1,0:T(8,128)(2,1)S(1)}, u32[]{:S(2)}, u32[]{:S(2)}) collective-permute-start(bf16[336,128]{1,0:T(8,128)(2,1)S(1)} %get-tuple-element.45), channel_id=1, source_target_pairs={{0,3},{1,2},{2,1},{3,0},{4,7},{5,6},{6,5},{7,4},{8,11},{9,10},{10,... | collective-permute-start | bytes 258056 | tf_op jit(solution)/shard_map/ppermute | solution.py:290
  37.7 5.1 %collective-permute-start.9 = (bf16[336,128]{1,0:T(8,128)(2,1)S(1)}, bf16[336,128]{1,0:T(8,128)(2,1)S(1)}, u32[]{:S(2)}, u32[]{:S(2)}) collective-permute-start(bf16[336,128]{1,0:T(8,128)(2,1)S(1)} %shard_map.87.refs_0_), channel_id=1, source_target_pairs={{0,4},{1,5},{2,6},{3,7},{4,0},{5,1},{6,2},{7,3},{8,12},{9,13},{10,... | collective-permute-start | bytes 258056 | tf_op jit(solution)/shard_map/ppermute | solution.py:290
  39.9 8.1 %collective-permute-start.10 = (bf16[336,128]{1,0:T(8,128)(2,1)S(1)}, bf16[336,128]{1,0:T(8,128)(2,1)S(1)}, u32[]{:S(2)}, u32[]{:S(2)}) collective-permute-start(bf16[336,128]{1,0:T(8,128)(2,1)S(1)} %shard_map.87.refs_0_), channel_id=1, source_target_pairs={{0,8},{1,9},{2,10},{3,11},{4,12},{5,13},{6,14},{7,15},{8,0},{9,1},... | collective-permute-start | bytes 258056 | tf_op jit(solution)/shard_map/ppermute | solution.py:290
  41.1 6.9 %collective-permute-start.11 = (bf16[336,128]{1,0:T(8,128)(2,1)S(1)}, bf16[336,128]{1,0:T(8,128)(2,1)S(1)}, u32[]{:S(2)}, u32[]{:S(2)}) collective-permute-start(bf16[336,128]{1,0:T(8,128)(2,1)S(1)} %shard_map.87.refs_0_), channel_id=1, source_target_pairs={{0,12},{1,13},{2,14},{3,15},{4,8},{5,9},{6,10},{7,11},{8,4},{9,5},... | collective-permute-start | bytes 258056 | tf_op jit(solution)/shard_map/ppermute | solution.py:290
  48.1 5.2 %collective-permute-start.12 = (bf16[576,128]{1,0:T(8,128)(2,1)S(1)}, bf16[576,128]{1,0:T(8,128)(2,1)S(1)}, u32[]{:S(2)}, u32[]{:S(2)}) collective-permute-start(bf16[576,128]{1,0:T(8,128)(2,1)S(1)} %shard_map.88.refs_0_), channel_id=1, source_target_pairs={{0,1},{1,0},{2,3},{3,2},{4,5},{5,4},{6,7},{7,6},{8,9},{9,8},{10,11... | collective-permute-start | bytes 442376 | tf_op jit(solution)/shard_map/ppermute | solution.py:290
  49.5 5.2 %collective-permute-start.13 = (bf16[576,128]{1,0:T(8,128)(2,1)S(1)}, bf16[576,128]{1,0:T(8,128)(2,1)S(1)}, u32[]{:S(2)}, u32[]{:S(2)}) collective-permute-start(bf16[576,128]{1,0:T(8,128)(2,1)S(1)} %shard_map.88.refs_0_), channel_id=1, source_target_pairs={{0,2},{1,3},{2,0},{3,1},{4,6},{5,7},{6,4},{7,5},{8,10},{9,11},{10,... | collective-permute-start | bytes 442376 | tf_op jit(solution)/shard_map/ppermute | solution.py:290
  50.1 6.1 %collective-permute-start.14 = (bf16[576,128]{1,0:T(8,128)(2,1)S(1)}, bf16[576,128]{1,0:T(8,128)(2,1)S(1)}, u32[]{:S(2)}, u32[]{:S(2)}) collective-permute-start(bf16[576,128]{1,0:T(8,128)(2,1)S(1)} %shard_map.88.refs_0_), channel_id=1, source_target_pairs={{0,3},{1,2},{2,1},{3,0},{4,7},{5,6},{6,5},{7,4},{8,11},{9,10},{10,... | collective-permute-start | bytes 442376 | tf_op jit(solution)/shard_map/ppermute | solution.py:290
  56.3 1.6 %collective-permute-start.15 = (bf16[1024,128]{1,0:T(8,128)(2,1)S(1)}, bf16[1024,128]{1,0:T(8,128)(2,1)S(1)}, u32[]{:S(2)}, u32[]{:S(2)}) collective-permute-start(bf16[1024,128]{1,0:T(8,128)(2,1)S(1)} %shard_map.89.refs_0_), channel_id=1, source_target_pairs={{0,16},{16,0},{1,17},{17,1},{2,18},{18,2},{3,19},{19,3},{4,20},{20... | collective-permute-start | bytes 786440 | tf_op jit(solution)/shard_map/ppermute | solution.py:424

commit v5 on v4

--- a/solution.py
+++ b/solution.py
@@ -55,6 +55,11 @@
         total = jnp.sum(part, axis=1, keepdims=True)
         parts.append((part * (pairs / total) - count).astype(bf16))
     return jnp.concatenate(parts, axis=1)
+
+
+def split(runs):
+    near = 1 << (runs.bit_length() // 2)
+    return near, runs // near
 
 
 def turn(k):
@@ -150,7 +155,7 @@
 def own_kernel(
     runs, reach,
     run_ref, list_ref, live_ref, xt_ref, src_unit_ref, tgt_unit_ref, tgt_inv_ref, src_ref, tgt_ref,
-    even_ref, odd_ref, grad_ref, part_ref,
+    count_ref, grad_ref, part_ref,
 ):
     zs = src_unit_ref[...].astype(bf16)
     own = xt_ref.shape[0]
@@ -158,9 +163,7 @@
     counts = pair_counts(
         list_ref, live_ref, src_ref, tgt_ref, block, run_ref[0], runs, reach
     )
-    far = own * (1 + reach)
-    even_ref[...] = counts[:, own:far].astype(bf16)
-    odd_ref[...] = counts[:, far:].astype(bf16)
+    count_ref[...] = counts[:, own:].astype(bf16)
     grad_ref[...], part_ref[...] = score(
         xt_ref[...], tgt_unit_ref[...], tgt_inv_ref[:, :1], zs, counts[:, :own], block
     )
@@ -173,21 +176,12 @@
     return dot_nn(weights, zt), dot_tn(rows, back_norm(unit, inv_norm, grad_zt))
 
 
-def even_kernel(reach, block, w_ref, unit_ref, count_ref, grad_ref, part_ref, *refs):
-    out_grad_ref, out_part_ref = refs[reach:]
-    rows = jnp.concatenate([ref[...] for ref in refs[:reach]], axis=0)
-    zs = unit_ref[...].astype(bf16)
-    grad, part = score(rows, *project(rows, w_ref[...]), zs, count_ref[...], block)
-    out_grad_ref[...] = grad_ref[...] + grad
-    out_part_ref[...] = part_ref[...] + part
-
-
-def odd_kernel(
-    reach, block, groups,
+def halo_kernel(
+    nbrs, block, groups,
     grp_ref, xs_ref, w_ref, unit_ref, inv_ref, count_ref, grad_ref, part_ref, *refs,
 ):
-    keep_ref, send_ref, total_ref = refs[reach:]
-    rows = jnp.concatenate([ref[...] for ref in refs[:reach]], axis=0)
+    keep_ref, send_ref, total_ref = refs[nbrs:]
+    rows = jnp.concatenate([ref[...] for ref in refs[:nbrs]], axis=0)
     unit = unit_ref[...]
     zs = unit.astype(bf16)
     grad, part = score(rows, *project(rows, w_ref[...]), zs, count_ref[...], block)
@@ -320,8 +314,7 @@
     even = [lax.ppermute(xt, "blk", partners(k, 0, runs)) for k in hops]
 
     tiles = width // lane
-    near = 1 << (runs.bit_length() // 2)
-    far = runs // near
+    near, far = split(runs)
     piece_rows = -(-tiles * (tiles + 1) // 2 * lane // (16 * runs)) * 16
     column_rows = near * piece_rows
     chunk = width // groups
@@ -356,44 +349,32 @@
         name="moment",
     )(run_id, *far_away)
     pieces = [pieces[0]] + [swap(pieces[k], k * near, runs) for k in range(1, far)]
-    even_count, odd_count, grad, part = pl.pallas_call(
+    counts, grad, part = pl.pallas_call(
         functools.partial(own_kernel, runs, reach),
         out_shape=(
-            jax.ShapeDtypeStruct((points, reach * points), bf16),
-            jax.ShapeDtypeStruct((points, reach * points), bf16),
+            jax.ShapeDtypeStruct((points, 2 * reach * points), bf16),
             jax.ShapeDtypeStruct((points, width), f32),
             jax.ShapeDtypeStruct((width, width), f32),
         ),
         in_specs=[smem] * 3 + [vmem] * 6,
-        out_specs=(vmem,) * 4,
+        out_specs=(vmem,) * 3,
         compiler_params=room(16 + 4 * reach),
         name="own",
     )(
         run_id, match_blocks[0], match_count, xt, unit, tgt_unit, tgt_inv, sources, targets
     )
-    grad, part = pl.pallas_call(
-        functools.partial(even_kernel, reach, block),
-        out_shape=(
-            jax.ShapeDtypeStruct((points, width), f32),
-            jax.ShapeDtypeStruct((width, width), f32),
-        ),
-        in_specs=[vmem] * (5 + reach),
-        out_specs=(vmem, vmem),
-        compiler_params=room(16 + 4 * reach),
-        name="even",
-    )(proj_weight, unit, even_count, grad, part, *even)
     keep, send = pl.pallas_call(
-        functools.partial(odd_kernel, reach, block, groups),
+        functools.partial(halo_kernel, 2 * reach, block, groups),
         out_shape=(
             jax.ShapeDtypeStruct((chunk, width), f32),
             jax.ShapeDtypeStruct((groups - 1, chunk, width), bf16),
         ),
-        in_specs=[smem] + [vmem] * (7 + reach),
+        in_specs=[smem] + [vmem] * (7 + 2 * reach),
         out_specs=(vmem, vmem),
         scratch_shapes=[pltpu.VMEM((width, width), f32)],
         compiler_params=room(16 + 4 * reach),
-        name="odd",
-    )(grp_id, xs, proj_weight, unit, inv, odd_count, grad, part, *odd)
+        name="halo",
+    )(grp_id, xs, proj_weight, unit, inv, counts, grad, part, *even, *odd)
 
     got = [
         lax.ppermute(send[k - 1], "grp", [(i, (i + k) % groups) for i in range(groups)])

time: 59.1 us -> 58.1 us (0.983)
  waiting for transfers between devices: 23 us -> 24.2 us
  starting transfers between devices: 24.3 us -> 23.2 us
  Pallas kernels: 10.2 us -> 9.13 us
    ppermute x1, starting transfers between devices: 3.03 us -> 0.01 us  [body(): even = [lax.ppermute(xt, 'blk', partners(k, 0, runs)) for k in hops]]
    ppermute x1, starting transfers between devices: 4.53 us -> 7.02 us  [body(): odd = [lax.ppermute(xt, 'blk', partners(k, 1, runs)) for k in hops]]
    ppermute x1, waiting for transfers between devices: 0.01 us -> 1.36 us  [body(): odd = [lax.ppermute(xt, 'blk', partners(k, 1, runs)) for k in hops]]
    ppermute x12, waiting for transfers between devices: 20.9 us -> 19.8 us  [swap(): return lax.ppermute(array, 'blk', [(i, i ^ bits) for i in range(runs)])]
    pallas_call x2 -> x1, Pallas kernels: 3.16 us -> 2.13 us  [body(): pl.pallas_call(functools.partial(halo_kernel, 2 * reach, block, groups),...]
    ppermute x1, waiting for transfers between devices: 1.72 us -> 2.74 us  [body(): even = [lax.ppermute(xt, 'blk', partners(k, 0, runs)) for k in hops]]
    ppermute x12, starting transfers between devices: 16.6 us -> 16 us  [swap(): return lax.ppermute(array, 'blk', [(i, i ^ bits) for i in range(runs)])]
  transfers between devices with their start and end apart: 16 -> 16, of which waited for: 12 -> 13; matrix products, arithmetic and copies ran while one was open for 0% -> 0% of each run, Pallas kernels for 12% -> 10%
where the time goes in v5:
time: 58.1 us; the launch traced here: 57.9 us
  waiting for transfers between devices  24.2 us (42%)
  starting transfers between devices  23.2 us (40%)
  Pallas kernels  9.13 us (16%)
  between operations  0.72 us (1%)
  local copies, waits for them, and re-layouts  0.67 us (1%)
    ppermute x12, waiting for transfers between devices, swap(): return lax.ppermute(array, 'blk', [(i, i ^ bits) for i in range(runs)])  19.8 us
    ppermute x12, starting transfers between devices, swap(): return lax.ppermute(array, 'blk', [(i, i ^ bits) for i in range(runs)])  16 us
    ppermute x1, starting transfers between devices, body(): odd = [lax.ppermute(xt, 'blk', partners(k, 1, runs)) for k in hops]  7.02 us
    ppermute x1, waiting for transfers between devices, body(): even = [lax.ppermute(xt, 'blk', partners(k, 0, runs)) for k in hops]  2.74 us
    pallas_call x1, Pallas kernels, body(): pl.pallas_call(functools.partial(moment_kernel, far, near, scale), out_sh...  2.45 us
    pallas_call x1, Pallas kernels, body(): pl.pallas_call(functools.partial(halo_kernel, 2 * reach, block, groups),...  2.13 us
    pallas_call x1, Pallas kernels, body(): pl.pallas_call(functools.partial(own_kernel, runs, reach), out_shape=(jax...  2.1 us
    ppermute x1, waiting for transfers between devices, body(): odd = [lax.ppermute(xt, 'blk', partners(k, 1, runs)) for k in hops]  1.36 us
  transfers between devices with their start and end apart: 16, of which 13 were waited for; matrix products, arithmetic and copies ran while one was open for 0% of the time, Pallas kernels for 10%

profile of v5, /device:TPU:0, one launch (start us, length us, event | category | flops | bytes accessed | tf_op | source)
XLA Modules:
  0.0 57.9 jit_solution(17526786356907677743)
XLA Ops:
  0.6 7.0 %collective-permute-start.1 = (bf16[256,512]{1,0:T(8,128)(2,1)}, bf16[256,512]{1,0:T(8,128)(2,1)S(1)}, u32[]{:S(2)}, u32[]{:S(2)}) collective-permute-start(bf16[256,512]{1,0:T(8,128)(2,1)} %bitcast.11), channel_id=1, source_target_pairs={{1,2},{3,4},{5,6},{7,8},{9,10},{11,12},{13,14},{15,0},{2,1},{4,3},... | collective-permute-start | bytes 786440 | tf_op jit(solution)/shard_map/ppermute | solution.py:313
  7.7 0.0 collective-permute-start
  7.7 0.0 copy-start.2
  7.7 2.5 %moment.1 = (bf16[320,128]{1,0:T(8,128)(2,1)S(1)}, bf16[320,128]{1,0:T(8,128)(2,1)S(1)}, bf16[320,128]{1,0:T(8,128)(2,1)S(1)}, bf16[320,128]{1,0:T(8,128)(2,1)S(...) custom-call(s32[1]{0:T(128)} %bitcast.run_ref, ...), custom_call_target="tpu_custom_call" | custom-call | tf_op jit(solution)/shard_map/moment/pallas_call | solution.py:333
  10.1 0.0 copy-start.3
  10.1 0.0 copy-start.4
  10.1 0.0 copy-done.2
  10.2 0.6 %copy-done.3 = s32[1,2,4]{2,1,0:T(2,128)S(1)} copy-done((s32[1,2,4]{2,1,0:T(2,128)S(1)}, s32[1,2,4]{2,1,0:T(2,128)}, u32[]{:S(2)}) %copy-start.3) | copy-done | bytes 56
  10.8 0.0 copy-done.4
  10.8 0.0 copy-start
  10.8 0.0 copy-start.1
  10.8 2.1 %own.1 = (bf16[256,512]{1,0:T(8,128)(2,1)S(1)}, f32[256,512]{1,0:T(8,128)S(1)}, f32[512,512]{1,0:T(8,128)S(1)}) custom-call(s32[1]{0:T(128)} %bitcast.run_ref, s32[2,4]{1,0:T(2,128)S(1)} %bitcast.15, s32[1,2]{1,0:T(1,128)S(1)} %copy-done.4, bf16[256,512]{1,0:T(8,128)(2,1)S(1)} %bitcast.14, f32[256,512]{1,0:T(8,128)S(1)} %get-tuple-element.21.src_unit_ref.unit_ref, ...), custom_call_target="tpu_custom_call" | custom-call | tf_op jit(solution)/shard_map/own/pallas_call | solution.py:352
  12.9 1.4 %collective-permute-done.1.refs_1_ = bf16[256,512]{1,0:T(8,128)(2,1)S(1)} collective-permute-done((bf16[256,512]{1,0:T(8,128)(2,1)}, bf16[256,512]{1,0:T(8,128)(2,1)S(1)}, u32[]{:S(2)}, u32[]{:S(2)}) %collective-permute-start.1) | collective-permute-done | bytes 262176 | tf_op jit(solution)/shard_map/ppermute | solution.py:313
  14.3 2.7 %collective-permute-done.refs_0_ = bf16[256,512]{1,0:T(8,128)(2,1)S(1)} collective-permute-done((bf16[256,512]{1,0:T(8,128)(2,1)}, bf16[256,512]{1,0:T(8,128)(2,1)S(1)}, u32[]{:S(2)}, u32[]{:S(2)}) %collective-permute-start) | collective-permute-done | bytes 262176 | tf_op jit(solution)/shard_map/ppermute | solution.py:314
  17.0 0.0 copy-done
  17.0 0.0 copy-done.1
  17.0 2.1 %halo.1 = (f32[256,512]{1,0:T(8,128)S(1)}, bf16[1,256,512]{2,1,0:T(8,128)(2,1)S(1)}) custom-call(s32[1]{0:T(128)} %bitcast.1.grp_ref, bf16[256,512]{1,0:T(8,128)(2,1)S(1)} %bitcast.10, bf16[512,512]{1,0:T(8,128)(2,1)S(1)} %copy-done, f32[256,512]{1,0:T(8,128)S(1)} %get-tuple-element.21.src_unit_ref.unit_ref, f32[256,128]{1,0:T(8,128)S(1)} %get-tuple-element.22.inv_ref, ...), custom_call_target="tpu_custom_call" | custom-call | tf_op jit(solution)/shard_map/halo/pallas_call | solution.py:366
  19.2 0.1 collective-permute-start.2
  19.2 1.6 %collective-permute-start.3 = (bf16[320,128]{1,0:T(8,128)(2,1)S(1)}, bf16[320,128]{1,0:T(8,128)(2,1)S(1)}, u32[]{:S(2)}, u32[]{:S(2)}) collective-permute-start(bf16[320,128]{1,0:T(8,128)(2,1)S(1)} %get-tuple-element.33), channel_id=1, source_target_pairs={{0,4},{1,5},{2,6},{3,7},{4,0},{5,1},{6,2},{7,3},{8,12},{9,13},{10,... | collective-permute-start | bytes 245768 | tf_op jit(solution)/shard_map/ppermute | solution.py:284
  20.9 2.6 %collective-permute-start.4 = (bf16[320,128]{1,0:T(8,128)(2,1)S(1)}, bf16[320,128]{1,0:T(8,128)(2,1)S(1)}, u32[]{:S(2)}, u32[]{:S(2)}) collective-permute-start(bf16[320,128]{1,0:T(8,128)(2,1)S(1)} %get-tuple-element.34), channel_id=1, source_target_pairs={{0,8},{1,9},{2,10},{3,11},{4,12},{5,13},{6,14},{7,15},{8,0},{9,1},... | collective-permute-start | bytes 245768 | tf_op jit(solution)/shard_map/ppermute | solution.py:284
  23.5 0.2 collective-permute-start.5
  23.7 0.4 collective-permute-done.3.refs_3_
  24.1 6.3 %collective-permute-done.4.refs_4_ = bf16[320,128]{1,0:T(8,128)(2,1)S(1)} collective-permute-done((bf16[320,128]{1,0:T(8,128)(2,1)S(1)}, bf16[320,128]{1,0:T(8,128)(2,1)S(1)}, u32[]{:S(2)}, u32[]{:S(2)}) %collective-permute-start.4) | collective-permute-done | bytes 81952 | tf_op jit(solution)/shard_map/ppermute | solution.py:284
  30.4 0.0 collective-permute-done.5.refs_5_
  30.4 0.0 collective-permute-done.2.refs_1_
  30.4 0.1 shard_map.86
  30.5 1.9 %collective-permute-start.6 = (bf16[336,128]{1,0:T(8,128)(2,1)S(1)}, bf16[336,128]{1,0:T(8,128)(2,1)S(1)}, u32[]{:S(2)}, u32[]{:S(2)}) collective-permute-start(bf16[336,128]{1,0:T(8,128)(2,1)S(1)} %get-tuple-element.37), channel_id=1, source_target_pairs={{0,1},{1,0},{2,3},{3,2},{4,5},{5,4},{6,7},{7,6},{8,9},{9,8},{10,11... | collective-permute-start | bytes 258056 | tf_op jit(solution)/shard_map/ppermute | solution.py:284
  32.4 0.2 collective-permute-start.7
  32.6 1.5 %collective-permute-start.8 = (bf16[336,128]{1,0:T(8,128)(2,1)S(1)}, bf16[336,128]{1,0:T(8,128)(2,1)S(1)}, u32[]{:S(2)}, u32[]{:S(2)}) collective-permute-start(bf16[336,128]{1,0:T(8,128)(2,1)S(1)} %get-tuple-element.39), channel_id=1, source_target_pairs={{0,3},{1,2},{2,1},{3,0},{4,7},{5,6},{6,5},{7,4},{8,11},{9,10},{10,... | collective-permute-start | bytes 258056 | tf_op jit(solution)/shard_map/ppermute | solution.py:284
  34.1 1.9 %collective-permute-done.6.refs_1_ = bf16[336,128]{1,0:T(8,128)(2,1)S(1)} collective-permute-done((bf16[336,128]{1,0:T(8,128)(2,1)S(1)}, bf16[336,128]{1,0:T(8,128)(2,1)S(1)}, u32[]{:S(2)}, u32[]{:S(2)}) %collective-permute-start.6) | collective-permute-done | bytes 86048 | tf_op jit(solution)/shard_map/ppermute | solution.py:284
  36.0 1.0 %collective-permute-done.7.refs_2_ = bf16[336,128]{1,0:T(8,128)(2,1)S(1)} collective-permute-done((bf16[336,128]{1,0:T(8,128)(2,1)S(1)}, bf16[336,128]{1,0:T(8,128)(2,1)S(1)}, u32[]{:S(2)}, u32[]{:S(2)}) %collective-permute-start.7) | collective-permute-done | bytes 86048 | tf_op jit(solution)/shard_map/ppermute | solution.py:284
  36.9 1.1 %collective-permute-done.8.refs_3_ = bf16[336,128]{1,0:T(8,128)(2,1)S(1)} collective-permute-done((bf16[336,128]{1,0:T(8,128)(2,1)S(1)}, bf16[336,128]{1,0:T(8,128)(2,1)S(1)}, u32[]{:S(2)}, u32[]{:S(2)}) %collective-permute-start.8) | collective-permute-done | bytes 86048 | tf_op jit(solution)/shard_map/ppermute | solution.py:284
  38.0 2.8 %collective-permute-start.11 = (bf16[336,128]{1,0:T(8,128)(2,1)S(1)}, bf16[336,128]{1,0:T(8,128)(2,1)S(1)}, u32[]{:S(2)}, u32[]{:S(2)}) collective-permute-start(bf16[336,128]{1,0:T(8,128)(2,1)S(1)} %shard_map.87.refs_0_), channel_id=1, source_target_pairs={{0,12},{1,13},{2,14},{3,15},{4,8},{5,9},{6,10},{7,11},{8,4},{9,5},... | collective-permute-start | bytes 258056 | tf_op jit(solution)/shard_map/ppermute | solution.py:284
  40.8 0.8 %collective-permute-start.10 = (bf16[336,128]{1,0:T(8,128)(2,1)S(1)}, bf16[336,128]{1,0:T(8,128)(2,1)S(1)}, u32[]{:S(2)}, u32[]{:S(2)}) collective-permute-start(bf16[336,128]{1,0:T(8,128)(2,1)S(1)} %shard_map.87.refs_0_), channel_id=1, source_target_pairs={{0,8},{1,9},{2,10},{3,11},{4,12},{5,13},{6,14},{7,15},{8,0},{9,1},... | collective-permute-start | bytes 258056 | tf_op jit(solution)/shard_map/ppermute | solution.py:284
  41.6 0.9 %collective-permute-start.9 = (bf16[336,128]{1,0:T(8,128)(2,1)S(1)}, bf16[336,128]{1,0:T(8,128)(2,1)S(1)}, u32[]{:S(2)}, u32[]{:S(2)}) collective-permute-start(bf16[336,128]{1,0:T(8,128)(2,1)S(1)} %shard_map.87.refs_0_), channel_id=1, source_target_pairs={{0,4},{1,5},{2,6},{3,7},{4,0},{5,1},{6,2},{7,3},{8,12},{9,13},{10,... | collective-permute-start | bytes 258056 | tf_op jit(solution)/shard_map/ppermute | solution.py:284
  42.5 2.7 %collective-permute-done.11.refs_3_ = bf16[336,128]{1,0:T(8,128)(2,1)S(1)} collective-permute-done((bf16[336,128]{1,0:T(8,128)(2,1)S(1)}, bf16[336,128]{1,0:T(8,128)(2,1)S(1)}, u32[]{:S(2)}, u32[]{:S(2)}) %collective-permute-start.11) | collective-permute-done | bytes 86048 | tf_op jit(solution)/shard_map/ppermute | solution.py:284
  45.2 1.9 %collective-permute-done.10.refs_2_ = bf16[336,128]{1,0:T(8,128)(2,1)S(1)} collective-permute-done((bf16[336,128]{1,0:T(8,128)(2,1)S(1)}, bf16[336,128]{1,0:T(8,128)(2,1)S(1)}, u32[]{:S(2)}, u32[]{:S(2)}) %collective-permute-start.10) | collective-permute-done | bytes 86048 | tf_op jit(solution)/shard_map/ppermute | solution.py:284
  47.1 0.0 collective-permute-done.9.refs_1_
  47.2 1.6 %collective-permute-start.14 = (bf16[576,128]{1,0:T(8,128)(2,1)S(1)}, bf16[576,128]{1,0:T(8,128)(2,1)S(1)}, u32[]{:S(2)}, u32[]{:S(2)}) collective-permute-start(bf16[576,128]{1,0:T(8,128)(2,1)S(1)} %shard_map.88.refs_0_), channel_id=1, source_target_pairs={{0,3},{1,2},{2,1},{3,0},{4,7},{5,6},{6,5},{7,4},{8,11},{9,10},{10,... | collective-permute-start | bytes 442376 | tf_op jit(solution)/shard_map/ppermute | solution.py:284
  48.7 1.4 %collective-permute-start.13 = (bf16[576,128]{1,0:T(8,128)(2,1)S(1)}, bf16[576,128]{1,0:T(8,128)(2,1)S(1)}, u32[]{:S(2)}, u32[]{:S(2)}) collective-permute-start(bf16[576,128]{1,0:T(8,128)(2,1)S(1)} %shard_map.88.refs_0_), channel_id=1, source_target_pairs={{0,2},{1,3},{2,0},{3,1},{4,6},{5,7},{6,4},{7,5},{8,10},{9,11},{10,... | collective-permute-start | bytes 442376 | tf_op jit(solution)/shard_map/ppermute | solution.py:284
  50.1 0.6 %collective-permute-start.12 = (bf16[576,128]{1,0:T(8,128)(2,1)S(1)}, bf16[576,128]{1,0:T(8,128)(2,1)S(1)}, u32[]{:S(2)}, u32[]{:S(2)}) collective-permute-start(bf16[576,128]{1,0:T(8,128)(2,1)S(1)} %shard_map.88.refs_0_), channel_id=1, source_target_pairs={{0,1},{1,0},{2,3},{3,2},{4,5},{5,4},{6,7},{7,6},{8,9},{9,8},{10,11... | collective-permute-start | bytes 442376 | tf_op jit(solution)/shard_map/ppermute | solution.py:284
  50.7 2.7 %collective-permute-done.14.refs_3_ = bf16[576,128]{1,0:T(8,128)(2,1)S(1)} collective-permute-done((bf16[576,128]{1,0:T(8,128)(2,1)S(1)}, bf16[576,128]{1,0:T(8,128)(2,1)S(1)}, u32[]{:S(2)}, u32[]{:S(2)}) %collective-permute-start.14) | collective-permute-done | bytes 147488 | tf_op jit(solution)/shard_map/ppermute | solution.py:284
  53.4 1.5 %collective-permute-done.13.refs_2_ = bf16[576,128]{1,0:T(8,128)(2,1)S(1)} collective-permute-done((bf16[576,128]{1,0:T(8,128)(2,1)S(1)}, bf16[576,128]{1,0:T(8,128)(2,1)S(1)}, u32[]{:S(2)}, u32[]{:S(2)}) %collective-permute-start.13) | collective-permute-done | bytes 147488 | tf_op jit(solution)/shard_map/ppermute | solution.py:284
  54.8 0.4 collective-permute-done.12.refs_1_
  55.3 0.1 collective-permute-start.15
  55.4 1.2 %shard_map.91 = f32[512,512]{1,0:T(8,128)} custom-call(s32[1]{0:T(128)} %bitcast.run_ref, bf16[576,128]{1,0:T(8,128)(2,1)S(1)} %shard_map.88.refs_0_, bf16[576,128]{1,0:T(8,128)(2,1)S(1)} %collective-permute-done.12.refs_1_, bf16[576,128]{1,0:T(8,128)(2,1)S(1)} %collective-permute-done.13.refs_2_, bf16[576,128]{1,0:T(8,128)(2,1)S(1)} %collective-permute-done.14.refs_3_), custom_call_target="tpu_custom_call" | custom-call | tf_op jit(solution)/shard_map/pallas_call | solution.py:408
  56.5 0.4 collective-permute-done.15.refs_1_
  56.9 1.0 %shard_map.90 = f32[512,512]{1,0:T(8,128)} custom-call(s32[1]{0:T(128)} %bitcast.run_ref, s32[1]{0:T(128)} %bitcast.1.grp_ref, bf16[1024,128]{1,0:T(8,128)(2,1)S(1)} %shard_map.89.refs_0_, bf16[1024,128]{1,0:T(8,128)(2,1)S(1)} %collective-permute-done.15.refs_1_), custom_call_target="tpu_custom_call" | custom-call | tf_op jit(solution)/shard_map/pallas_call | solution.py:414
  (3 shorter events, 0.1 us)
Async XLA Ops:
  0.6 13.6 %collective-permute-start.1 = (bf16[256,512]{1,0:T(8,128)(2,1)}, bf16[256,512]{1,0:T(8,128)(2,1)S(1)}, u32[]{:S(2)}, u32[]{:S(2)}) collective-permute-start(bf16[256,512]{1,0:T(8,128)(2,1)} %bitcast.11), channel_id=1, source_target_pairs={{1,2},{3,4},{5,6},{7,8},{9,10},{11,12},{13,14},{15,0},{2,1},{4,3},... | collective-permute-start | bytes 786440 | tf_op jit(solution)/shard_map/ppermute | solution.py:313
  7.7 9.4 %collective-permute-start = (bf16[256,512]{1,0:T(8,128)(2,1)}, bf16[256,512]{1,0:T(8,128)(2,1)S(1)}, u32[]{:S(2)}, u32[]{:S(2)}) collective-permute-start(bf16[256,512]{1,0:T(8,128)(2,1)} %bitcast.12), channel_id=1, source_target_pairs={{0,1},{2,3},{4,5},{6,7},{8,9},{10,11},{12,13},{14,15},{1,0},{3,2},... | collective-permute-start | bytes 786440 | tf_op jit(solution)/shard_map/ppermute | solution.py:314
  7.7 2.5 %copy-start.2 = (bf16[1,256,512]{2,1,0:T(8,128)(2,1)S(1)}, bf16[1,256,512]{2,1,0:T(8,128)(2,1)}, u32[]{:S(2)}) copy-start(bf16[1,256,512]{2,1,0:T(8,128)(2,1)} %param.8) | copy-start | bytes 786436
  10.1 0.7 %copy-start.3 = (s32[1,2,4]{2,1,0:T(2,128)S(1)}, s32[1,2,4]{2,1,0:T(2,128)}, u32[]{:S(2)}) copy-start(s32[1,2,4]{2,1,0:T(2,128)} %param.10) | copy-start | bytes 100
  10.1 0.7 %copy-start.4 = (s32[1,2]{1,0:T(1,128)S(1)}, s32[1,2]{1,0:T(1,128)}, u32[]{:S(2)}) copy-start(s32[1,2]{1,0:T(1,128)} %live_ref.1) | copy-start | bytes 28
  10.8 6.2 %copy-start = (bf16[512,512]{1,0:T(8,128)(2,1)S(1)}, bf16[512,512]{1,0:T(8,128)(2,1)}, u32[]{:S(2)}) copy-start(bf16[512,512]{1,0:T(8,128)(2,1)} %w_ref.1) | copy-start | bytes 1572868
  10.8 6.2 %copy-start.1 = (bf16[1,256,512]{2,1,0:T(8,128)(2,1)S(1)}, bf16[1,256,512]{2,1,0:T(8,128)(2,1)}, u32[]{:S(2)}) copy-start(bf16[1,256,512]{2,1,0:T(8,128)(2,1)} %param.7) | copy-start | bytes 786436
  19.2 11.2 %collective-permute-start.2 = (bf16[256,512]{1,0:T(8,128)(2,1)S(1)}, bf16[256,512]{1,0:T(8,128)(2,1)S(1)}, u32[]{:S(2)}, u32[]{:S(2)}) collective-permute-start(bf16[256,512]{1,0:T(8,128)(2,1)S(1)} %bitcast.16), channel_id=1, source_target_pairs={{0,16},{16,0},{1,17},{17,1},{2,18},{18,2},{3,19},{19,3},{4,20},{20... | collective-permute-start | bytes 786440 | tf_op jit(solution)/shard_map/ppermute | solution.py:380
  19.2 4.8 %collective-permute-start.3 = (bf16[320,128]{1,0:T(8,128)(2,1)S(1)}, bf16[320,128]{1,0:T(8,128)(2,1)S(1)}, u32[]{:S(2)}, u32[]{:S(2)}) collective-permute-start(bf16[320,128]{1,0:T(8,128)(2,1)S(1)} %get-tuple-element.33), channel_id=1, source_target_pairs={{0,4},{1,5},{2,6},{3,7},{4,0},{5,1},{6,2},{7,3},{8,12},{9,13},{10,... | collective-permute-start | bytes 245768 | tf_op jit(solution)/shard_map/ppermute | solution.py:284
  20.9 9.5 %collective-permute-start.4 = (bf16[320,128]{1,0:T(8,128)(2,1)S(1)}, bf16[320,128]{1,0:T(8,128)(2,1)S(1)}, u32[]{:S(2)}, u32[]{:S(2)}) collective-permute-start(bf16[320,128]{1,0:T(8,128)(2,1)S(1)} %get-tuple-element.34), channel_id=1, source_target_pairs={{0,8},{1,9},{2,10},{3,11},{4,12},{5,13},{6,14},{7,15},{8,0},{9,1},... | collective-permute-start | bytes 245768 | tf_op jit(solution)/shard_map/ppermute | solution.py:284
  23.5 6.9 %collective-permute-start.5 = (bf16[320,128]{1,0:T(8,128)(2,1)S(1)}, bf16[320,128]{1,0:T(8,128)(2,1)S(1)}, u32[]{:S(2)}, u32[]{:S(2)}) collective-permute-start(bf16[320,128]{1,0:T(8,128)(2,1)S(1)} %get-tuple-element.35), channel_id=1, source_target_pairs={{0,12},{1,13},{2,14},{3,15},{4,8},{5,9},{6,10},{7,11},{8,4},{9,5},... | collective-permute-start | bytes 245768 | tf_op jit(solution)/shard_map/ppermute | solution.py:284
  30.5 5.4 %collective-permute-start.6 = (bf16[336,128]{1,0:T(8,128)(2,1)S(1)}, bf16[336,128]{1,0:T(8,128)(2,1)S(1)}, u32[]{:S(2)}, u32[]{:S(2)}) collective-permute-start(bf16[336,128]{1,0:T(8,128)(2,1)S(1)} %get-tuple-element.37), channel_id=1, source_target_pairs={{0,1},{1,0},{2,3},{3,2},{4,5},{5,4},{6,7},{7,6},{8,9},{9,8},{10,11... | collective-permute-start | bytes 258056 | tf_op jit(solution)/shard_map/ppermute | solution.py:284
  32.4 4.5 %collective-permute-start.7 = (bf16[336,128]{1,0:T(8,128)(2,1)S(1)}, bf16[336,128]{1,0:T(8,128)(2,1)S(1)}, u32[]{:S(2)}, u32[]{:S(2)}) collective-permute-start(bf16[336,128]{1,0:T(8,128)(2,1)S(1)} %get-tuple-element.38), channel_id=1, source_target_pairs={{0,2},{1,3},{2,0},{3,1},{4,6},{5,7},{6,4},{7,5},{8,10},{9,11},{10,... | collective-permute-start | bytes 258056 | tf_op jit(solution)/shard_map/ppermute | solution.py:284
  32.6 5.4 %collective-permute-start.8 = (bf16[336,128]{1,0:T(8,128)(2,1)S(1)}, bf16[336,128]{1,0:T(8,128)(2,1)S(1)}, u32[]{:S(2)}, u32[]{:S(2)}) collective-permute-start(bf16[336,128]{1,0:T(8,128)(2,1)S(1)} %get-tuple-element.39), channel_id=1, source_target_pairs={{0,3},{1,2},{2,1},{3,0},{4,7},{5,6},{6,5},{7,4},{8,11},{9,10},{10,... | collective-permute-start | bytes 258056 | tf_op jit(solution)/shard_map/ppermute | solution.py:284
  38.0 7.2 %collective-permute-start.11 = (bf16[336,128]{1,0:T(8,128)(2,1)S(1)}, bf16[336,128]{1,0:T(8,128)(2,1)S(1)}, u32[]{:S(2)}, u32[]{:S(2)}) collective-permute-start(bf16[336,128]{1,0:T(8,128)(2,1)S(1)} %shard_map.87.refs_0_), channel_id=1, source_target_pairs={{0,12},{1,13},{2,14},{3,15},{4,8},{5,9},{6,10},{7,11},{8,4},{9,5},... | collective-permute-start | bytes 258056 | tf_op jit(solution)/shard_map/ppermute | solution.py:284
  40.8 6.3 %collective-permute-start.10 = (bf16[336,128]{1,0:T(8,128)(2,1)S(1)}, bf16[336,128]{1,0:T(8,128)(2,1)S(1)}, u32[]{:S(2)}, u32[]{:S(2)}) collective-permute-start(bf16[336,128]{1,0:T(8,128)(2,1)S(1)} %shard_map.87.refs_0_), channel_id=1, source_target_pairs={{0,8},{1,9},{2,10},{3,11},{4,12},{5,13},{6,14},{7,15},{8,0},{9,1},... | collective-permute-start | bytes 258056 | tf_op jit(solution)/shard_map/ppermute | solution.py:284
  41.6 5.5 %collective-permute-start.9 = (bf16[336,128]{1,0:T(8,128)(2,1)S(1)}, bf16[336,128]{1,0:T(8,128)(2,1)S(1)}, u32[]{:S(2)}, u32[]{:S(2)}) collective-permute-start(bf16[336,128]{1,0:T(8,128)(2,1)S(1)} %shard_map.87.refs_0_), channel_id=1, source_target_pairs={{0,4},{1,5},{2,6},{3,7},{4,0},{5,1},{6,2},{7,3},{8,12},{9,13},{10,... | collective-permute-start | bytes 258056 | tf_op jit(solution)/shard_map/ppermute | solution.py:284
  47.2 6.2 %collective-permute-start.14 = (bf16[576,128]{1,0:T(8,128)(2,1)S(1)}, bf16[576,128]{1,0:T(8,128)(2,1)S(1)}, u32[]{:S(2)}, u32[]{:S(2)}) collective-permute-start(bf16[576,128]{1,0:T(8,128)(2,1)S(1)} %shard_map.88.refs_0_), channel_id=1, source_target_pairs={{0,3},{1,2},{2,1},{3,0},{4,7},{5,6},{6,5},{7,4},{8,11},{9,10},{10,... | collective-permute-start | bytes 442376 | tf_op jit(solution)/shard_map/ppermute | solution.py:284
  48.7 6.1 %collective-permute-start.13 = (bf16[576,128]{1,0:T(8,128)(2,1)S(1)}, bf16[576,128]{1,0:T(8,128)(2,1)S(1)}, u32[]{:S(2)}, u32[]{:S(2)}) collective-permute-start(bf16[576,128]{1,0:T(8,128)(2,1)S(1)} %shard_map.88.refs_0_), channel_id=1, source_target_pairs={{0,2},{1,3},{2,0},{3,1},{4,6},{5,7},{6,4},{7,5},{8,10},{9,11},{10,... | collective-permute-start | bytes 442376 | tf_op jit(solution)/shard_map/ppermute | solution.py:284
  50.1 5.1 %collective-permute-start.12 = (bf16[576,128]{1,0:T(8,128)(2,1)S(1)}, bf16[576,128]{1,0:T(8,128)(2,1)S(1)}, u32[]{:S(2)}, u32[]{:S(2)}) collective-permute-start(bf16[576,128]{1,0:T(8,128)(2,1)S(1)} %shard_map.88.refs_0_), channel_id=1, source_target_pairs={{0,1},{1,0},{2,3},{3,2},{4,5},{5,4},{6,7},{7,6},{8,9},{9,8},{10,11... | collective-permute-start | bytes 442376 | tf_op jit(solution)/shard_map/ppermute | solution.py:284
  55.3 1.6 %collective-permute-start.15 = (bf16[1024,128]{1,0:T(8,128)(2,1)S(1)}, bf16[1024,128]{1,0:T(8,128)(2,1)S(1)}, u32[]{:S(2)}, u32[]{:S(2)}) collective-permute-start(bf16[1024,128]{1,0:T(8,128)(2,1)S(1)} %shard_map.89.refs_0_), channel_id=1, source_target_pairs={{0,16},{16,0},{1,17},{17,1},{2,18},{18,2},{3,19},{19,3},{4,20},{20... | collective-permute-start | bytes 786440 | tf_op jit(solution)/shard_map/ppermute | solution.py:405

commit v6 on v5

--- a/solution.py
+++ b/solution.py
@@ -164,36 +164,60 @@
         list_ref, live_ref, src_ref, tgt_ref, block, run_ref[0], runs, reach
     )
     count_ref[...] = counts[:, own:].astype(bf16)
-    grad_ref[...], part_ref[...] = score(
-        xt_ref[...], tgt_unit_ref[...], tgt_inv_ref[:, :1], zs, counts[:, :own], block
-    )
-
-
-def score(rows, unit, inv_norm, zs, counts, block):
+    rows = xt_ref[...]
+    grad_ref[...], tgt_grad = score(
+        tgt_unit_ref[...], tgt_inv_ref[:, :1], zs, counts[:, :own], block
+    )
+    part_ref[...] = dot_tn(rows, tgt_grad)
+
+
+def score(unit, inv_norm, zs, counts, block):
     zt = unit.astype(bf16)
     weights = pair_weights(zs, zt, counts, block)
     grad_zt = dot_tn(weights, zs) * inverse_sharpness
-    return dot_nn(weights, zt), dot_tn(rows, back_norm(unit, inv_norm, grad_zt))
+    return dot_nn(weights, zt), back_norm(unit, inv_norm, grad_zt)
+
+
+def chunk_grad(first, chunk, row_refs, grads, part_ref, total_ref):
+    if chunk % lane == 0:
+        columns = pl.ds(pl.multiple_of(first, chunk), chunk)
+        rows = jnp.concatenate([ref[:, columns] for ref in row_refs], axis=0)
+        return part_ref[columns, :] + dot_tn(rows, grads)
+    rows = jnp.concatenate([ref[...] for ref in row_refs], axis=0)
+    total_ref[...] = part_ref[...] + dot_tn(rows, grads)
+    return total_ref[pl.ds(pl.multiple_of(first, chunk), chunk), :]
 
 
 def halo_kernel(
-    nbrs, block, groups,
-    grp_ref, xs_ref, w_ref, unit_ref, inv_ref, count_ref, grad_ref, part_ref, *refs,
+    block, groups,
+    grp_ref, w_ref, unit_ref, inv_ref, count_ref, grad_ref, part_ref, xs_ref, *refs,
 ):
-    keep_ref, send_ref, total_ref = refs[nbrs:]
-    rows = jnp.concatenate([ref[...] for ref in refs[:nbrs]], axis=0)
+    send_ref, src_grad_ref, tgt_grad_ref, total_ref = refs[-4:]
+    row_refs = refs[:-4]
+    rows = jnp.concatenate([ref[...] for ref in row_refs], axis=0)
     unit = unit_ref[...]
     zs = unit.astype(bf16)
-    grad, part = score(rows, *project(rows, w_ref[...]), zs, count_ref[...], block)
+    grad, tgt_grad = score(*project(rows, w_ref[...]), zs, count_ref[...], block)
     grad_zs = (grad_ref[...] + grad) * inverse_sharpness
     src_grad = back_norm(unit, inv_ref[:, :1], grad_zs)
-    total_ref[...] = part_ref[...] + part + dot_tn(xs_ref[...], src_grad)
-    chunk = total_ref.shape[0] // groups
-    me = grp_ref[0]
-    keep_ref[...] = total_ref[pl.ds(pl.multiple_of(me * chunk, chunk), chunk), :]
+    src_grad_ref[...] = src_grad
+    tgt_grad_ref[...] = tgt_grad
+    grads = jnp.concatenate([src_grad, tgt_grad], axis=0)
+    chunk = part_ref.shape[0] // groups
     for k in range(1, groups):
-        first = lax.rem(me + k, groups) * chunk
-        send_ref[k - 1] = total_ref[pl.ds(pl.multiple_of(first, chunk), chunk), :].astype(bf16)
+        first = lax.rem(grp_ref[0] + k, groups) * chunk
+        send_ref[k - 1] = chunk_grad(
+            first, chunk, (xs_ref,) + row_refs, grads, part_ref, total_ref
+        ).astype(bf16)
+
+
+def keep_kernel(grp_ref, part_ref, src_grad_ref, tgt_grad_ref, *refs):
+    keep_ref, total_ref = refs[-2:]
+    grads = jnp.concatenate([src_grad_ref[...], tgt_grad_ref[...]], axis=0)
+    chunk = keep_ref.shape[0]
+    keep_ref[...] = chunk_grad(
+        grp_ref[0] * chunk, chunk, refs[:-2], grads, part_ref, total_ref
+    )
 
 
 def tree(parts):
@@ -226,15 +250,17 @@
         out_refs[k][at : at + below, :] = sum_ref[pl.ds(first, below), :]
 
 
-def near_kernel(*refs):
-    refs[-1][...] = tree([ref[...].astype(f32) for ref in refs[:-1]]).astype(bf16)
+def near_kernel(rows, *refs):
+    part = tree([ref[...].astype(f32) for ref in refs[:-2]]).astype(bf16)
+    refs[-2][...] = part
+    refs[-1][...] = part[rows:, :]
 
 
 def far_kernel(rows, *refs):
     out_ref = refs[-1]
     out_ref[:rows, :] = tree([ref[:rows, :].astype(f32) for ref in refs[:-1]]).astype(bf16)
     below = refs[0].shape[0] - rows
-    for i, ref in enumerate(refs[:-1]):
+    for i, ref in enumerate(refs[1:-1]):
         at = rows + i * below
         out_ref[at : at + below, :] = ref[rows:, :]
 
@@ -245,39 +271,68 @@
         out_ref[i * rows : (i + 1) * rows, :] = ref[:rows, :]
 
 
-def unpack_kernel(near, far, skip, run_ref, *refs):
+def spread_rows(chunk_ref, half_ref, near, place):
+    rows = half_ref.shape[0] // near
+    at = 0
+    for m in range(near):
+        first = pl.multiple_of(lax.bitwise_xor(place, m) * rows, rows)
+        for c in range(0, half_ref.shape[1], lane):
+            half_ref[pl.ds(first, rows), c : c + lane] = chunk_ref[at : at + rows, :].astype(f32)
+            at += rows
+
+
+def unpack_kernel(near, far, run_ref, grp_ref, half_in_ref, *refs):
     column_refs = refs[:near]
-    out_ref, packed_ref = refs[near:]
-    rows = (column_refs[0].shape[0] - skip) // far
+    side_refs = refs[near : 2 * near]
+    cov_hbm, grad_hbm, packed_ref, cov_ref, half_ref, sem = refs[2 * near :]
+    chunk = half_ref.shape[0]
+    spread_rows(half_in_ref, half_ref, near, lax.rem(run_ref[0], near))
+    first = pl.multiple_of(grp_ref[0] * chunk, chunk)
+    copies = [
+        pltpu.make_async_copy(half_ref, grad_hbm.at[pl.ds(first, chunk), :], sem.at[0])
+    ]
+    copies[0].start()
+    rows = packed_ref.shape[0] // (near * far)
+    skip = column_refs[0].shape[0] - (far - 1) * rows
     for m, ref in enumerate(column_refs):
         for k in range(far):
             owner = lax.bitwise_xor(run_ref[0], k * near + m)
-            at = skip + k * rows
-            packed_ref[pl.ds(pl.multiple_of(owner * rows, 16), rows), :] = ref[at : at + rows, :]
+            at = skip + (k - 1) * rows
+            piece = ref[at : at + rows, :] if k else side_refs[m][...]
+            packed_ref[pl.ds(pl.multiple_of(owner * rows, 16), rows), :] = piece
     at = 0
-    for r in range(0, out_ref.shape[0], lane):
-        for c in range(r, out_ref.shape[1], lane):
+    for i, r in enumerate(range(0, cov_ref.shape[0], lane)):
+        for c in range(r, cov_ref.shape[1], lane):
             tile = packed_ref[at : at + lane, :].astype(f32)
-            out_ref[r : r + lane, c : c + lane] = tile
+            cov_ref[r : r + lane, c : c + lane] = tile
             if c > r:
-                out_ref[c : c + lane, r : r + lane] = tile.T
+                cov_ref[c : c + lane, r : r + lane] = tile.T
             at += lane
+        copy = pltpu.make_async_copy(
+            cov_ref.at[r : r + lane, :], cov_hbm.at[r : r + lane, :], sem.at[i + 1]
+        )
+        copy.start()
+        copies.append(copy)
+    for copy in copies:
+        copy.wait()
 
 
 def place_kernel(near, run_ref, grp_ref, *refs):
-    out_ref = refs[-1]
-    groups = len(refs) - 1
-    chunk = out_ref.shape[0] // groups
-    rows = chunk // near
-    place = lax.rem(run_ref[0], near)
-    for j, ref in enumerate(refs[:-1]):
-        base = lax.rem(grp_ref[0] + j, groups) * chunk
-        at = 0
-        for m in range(near):
-            first = pl.multiple_of(base + lax.bitwise_xor(place, m) * rows, rows)
-            for c in range(0, out_ref.shape[1], lane):
-                out_ref[pl.ds(first, rows), c : c + lane] = ref[at : at + rows, :].astype(f32)
-                at += rows
+    grad_hbm, chunk_ref, sem = refs[-3:]
+    half_refs = refs[:-4]
+    groups = len(half_refs) + 1
+    chunk = chunk_ref.shape[1]
+    copies = []
+    for j, ref in enumerate(half_refs):
+        spread_rows(ref, chunk_ref.at[j], near, lax.rem(run_ref[0], near))
+        first = pl.multiple_of(lax.rem(grp_ref[0] + j + 1, groups) * chunk, chunk)
+        copy = pltpu.make_async_copy(
+            chunk_ref.at[j], grad_hbm.at[pl.ds(first, chunk), :], sem.at[j]
+        )
+        copy.start()
+        copies.append(copy)
+    for copy in copies:
+        copy.wait()
 
 
 def swap(array, bits, runs):
@@ -293,7 +348,7 @@
         in_specs=specs,
         out_specs=(vmem,) * len(shapes) if many else vmem,
         scratch_shapes=scratch,
-        compiler_params=room(12),
+        compiler_params=room(16),
     )
 
 
@@ -363,23 +418,30 @@
     )(
         run_id, match_blocks[0], match_count, xt, unit, tgt_unit, tgt_inv, sources, targets
     )
-    keep, send = pl.pallas_call(
-        functools.partial(halo_kernel, 2 * reach, block, groups),
+    total = [pltpu.VMEM((width, width), f32)]
+    send, src_grad, tgt_grad = pl.pallas_call(
+        functools.partial(halo_kernel, block, groups),
         out_shape=(
-            jax.ShapeDtypeStruct((chunk, width), f32),
             jax.ShapeDtypeStruct((groups - 1, chunk, width), bf16),
+            jax.ShapeDtypeStruct((points, width), bf16),
+            jax.ShapeDtypeStruct((2 * reach * points, width), bf16),
         ),
         in_specs=[smem] + [vmem] * (7 + 2 * reach),
-        out_specs=(vmem, vmem),
-        scratch_shapes=[pltpu.VMEM((width, width), f32)],
+        out_specs=(vmem,) * 3,
+        scratch_shapes=total,
         compiler_params=room(16 + 4 * reach),
         name="halo",
-    )(grp_id, xs, proj_weight, unit, inv, counts, grad, part, *even, *odd)
-
+    )(grp_id, proj_weight, unit, inv, counts, grad, part, xs, *even, *odd)
     got = [
         lax.ppermute(send[k - 1], "grp", [(i, (i + k) % groups) for i in range(groups)])
         for k in range(1, groups)
     ]
+    keep = small_call(
+        keep_kernel,
+        jax.ShapeDtypeStruct((chunk, width), f32),
+        [smem] + [vmem] * (4 + 2 * reach),
+        total,
+    )(grp_id, part, src_grad, tgt_grad, xs, *even, *odd)
     part_shape = jax.ShapeDtypeStruct((grad_rows + piece_rows, lane), bf16)
     parts = small_call(
         functools.partial(deal_kernel, near, groups),
@@ -388,11 +450,16 @@
         [pltpu.VMEM((chunk, width), f32), pltpu.VMEM((column_rows, lane), bf16)],
     )(run_id, keep, *got, *pieces)
     parts = [parts[0]] + [swap(parts[k], k, runs) for k in range(1, near)]
-    part = small_call(near_kernel, part_shape, [vmem] * near)(*parts)
+    part, piece = small_call(
+        functools.partial(near_kernel, grad_rows),
+        (part_shape, jax.ShapeDtypeStruct((piece_rows, lane), bf16)),
+        [vmem] * near,
+    )(*parts)
     parts = [part] + [swap(part, k * near, runs) for k in range(1, far)]
+    sides = [piece] + [swap(piece, k, runs) for k in range(1, near)]
     part = small_call(
         functools.partial(far_kernel, grad_rows),
-        jax.ShapeDtypeStruct((grad_rows + far * piece_rows, lane), bf16),
+        jax.ShapeDtypeStruct((grad_rows + (far - 1) * piece_rows, lane), bf16),
         [vmem] * far,
     )(*parts)
     columns = [part] + [swap(part, k, runs) for k in range(1, near)]
@@ -405,17 +472,34 @@
         lax.ppermute(half, "grp", [(i, (i - k) % groups) for i in range(groups)])
         for k in range(1, groups)
     ]
-    covariance = small_call(
-        functools.partial(unpack_kernel, near, far, grad_rows),
-        jax.ShapeDtypeStruct((width, width), f32),
-        [smem] + [vmem] * near,
-        [pltpu.VMEM((far * column_rows, lane), bf16)],
-    )(run_id, *columns)
-    weight_grad = small_call(
+    square = jax.ShapeDtypeStruct((width, width), f32)
+    covariance, own_rows = pl.pallas_call(
+        functools.partial(unpack_kernel, near, far),
+        out_shape=(square, square),
+        in_specs=[smem] * 2 + [vmem] * (1 + 2 * near),
+        out_specs=(hbm, hbm),
+        scratch_shapes=[
+            pltpu.VMEM((far * column_rows, lane), bf16),
+            pltpu.VMEM((width, width), f32),
+            pltpu.VMEM((chunk, width), f32),
+            pltpu.SemaphoreType.DMA((1 + tiles,)),
+        ],
+        compiler_params=room(16),
+        name="unpack",
+    )(run_id, grp_id, half, *columns, *sides)
+    weight_grad = pl.pallas_call(
         functools.partial(place_kernel, near),
-        jax.ShapeDtypeStruct((width, width), f32),
-        [smem] * 2 + [vmem] * groups,
-    )(run_id, grp_id, *halves)
+        out_shape=square,
+        in_specs=[smem] * 2 + [vmem] * (groups - 1) + [hbm],
+        out_specs=hbm,
+        scratch_shapes=[
+            pltpu.VMEM((groups - 1, chunk, width), f32),
+            pltpu.SemaphoreType.DMA((groups - 1,)),
+        ],
+        input_output_aliases={1 + groups: 0},
+        compiler_params=room(16),
+        name="place",
+    )(run_id, grp_id, *halves[1:], own_rows)
     return (weight_grad, covariance[None])
 
 

time: 58.1 us -> 63.4 us (1.091)
  starting transfers between devices: 23.2 us -> 26.7 us
  waiting for transfers between devices: 24.2 us -> 25.8 us
    ppermute x12 -> x15, starting transfers between devices: 16 us -> 19.6 us  [swap(): return lax.ppermute(array, 'blk', [(i, i ^ bits) for i in range(runs)])]
    ppermute x12 -> x15, waiting for transfers between devices: 19.8 us -> 21.7 us  [swap(): return lax.ppermute(array, 'blk', [(i, i ^ bits) for i in range(runs)])]
    pallas_call x4 -> x5, Pallas kernels: 4.38 us -> 4.55 us  [the longest x1 1.99 us: body(): pl.pallas_call(functools.partial(halo_kernel, block, groups), out_shape=(...]
  transfers between devices with their start and end apart: 16 -> 19, of which waited for: 13 -> 14; matrix products, arithmetic and copies ran while one was open for 0% -> 0% of each run, Pallas kernels for 10% -> 10%
where the time goes in v6:
time: 63.4 us; the launch traced here: 63.3 us
  starting transfers between devices  26.7 us (42%)
  waiting for transfers between devices  25.8 us (41%)
  Pallas kernels  9.3 us (15%)
  between operations  0.75 us (1%)
  local copies, waits for them, and re-layouts  0.67 us (1%)
    ppermute x15, waiting for transfers between devices, swap(): return lax.ppermute(array, 'blk', [(i, i ^ bits) for i in range(runs)])  21.7 us
    ppermute x15, starting transfers between devices, swap(): return lax.ppermute(array, 'blk', [(i, i ^ bits) for i in range(runs)])  19.6 us
    ppermute x1, starting transfers between devices, body(): odd = [lax.ppermute(xt, 'blk', partners(k, 1, runs)) for k in hops]  7.02 us
    ppermute x1, waiting for transfers between devices, body(): even = [lax.ppermute(xt, 'blk', partners(k, 0, runs)) for k in hops]  2.74 us
    pallas_call x1, Pallas kernels, body(): pl.pallas_call(functools.partial(moment_kernel, far, near, scale), out_sh...  2.45 us
    pallas_call x1, Pallas kernels, body(): pl.pallas_call(functools.partial(own_kernel, runs, reach), out_shape=(jax...  2.1 us
    pallas_call x1, Pallas kernels, body(): pl.pallas_call(functools.partial(halo_kernel, block, groups), out_shape=(...  1.99 us
    ppermute x1, waiting for transfers between devices, body(): odd = [lax.ppermute(xt, 'blk', partners(k, 1, runs)) for k in hops]  1.36 us
  transfers between devices with their start and end apart: 19, of which 14 were waited for; matrix products, arithmetic and copies ran while one was open for 0% of the time, Pallas kernels for 10%

profile of v6, /device:TPU:0, one launch (start us, length us, event | category | flops | bytes accessed | tf_op | source)
XLA Modules:
  0.0 63.3 jit_solution(15236637643008521436)
XLA Ops:
  0.6 7.0 %collective-permute-start.1 = (bf16[256,512]{1,0:T(8,128)(2,1)}, bf16[256,512]{1,0:T(8,128)(2,1)S(1)}, u32[]{:S(2)}, u32[]{:S(2)}) collective-permute-start(bf16[256,512]{1,0:T(8,128)(2,1)} %bitcast.12), channel_id=1, source_target_pairs={{1,2},{3,4},{5,6},{7,8},{9,10},{11,12},{13,14},{15,0},{2,1},{4,3},... | collective-permute-start | bytes 786440 | tf_op jit(solution)/shard_map/ppermute | solution.py:368
  7.7 0.0 collective-permute-start
  7.7 2.5 %moment.1 = (bf16[320,128]{1,0:T(8,128)(2,1)S(1)}, bf16[320,128]{1,0:T(8,128)(2,1)S(1)}, bf16[320,128]{1,0:T(8,128)(2,1)S(1)}, bf16[320,128]{1,0:T(8,128)(2,1)S(...) custom-call(s32[1]{0:T(128)} %bitcast.run_ref, ...), custom_call_target="tpu_custom_call" | custom-call | tf_op jit(solution)/shard_map/moment/pallas_call | solution.py:388
  10.1 0.0 copy-start.3
  10.1 0.0 copy-start.4
  10.2 0.6 %copy-done.3 = s32[1,2,4]{2,1,0:T(2,128)S(1)} copy-done((s32[1,2,4]{2,1,0:T(2,128)S(1)}, s32[1,2,4]{2,1,0:T(2,128)}, u32[]{:S(2)}) %copy-start.3) | copy-done | bytes 56
  10.8 2.1 %own.1 = (bf16[256,512]{1,0:T(8,128)(2,1)S(1)}, f32[256,512]{1,0:T(8,128)S(1)}, f32[512,512]{1,0:T(8,128)S(1)}) custom-call(s32[1]{0:T(128)} %bitcast.run_ref, s32[2,4]{1,0:T(2,128)S(1)} %bitcast.16, s32[1,2]{1,0:T(1,128)S(1)} %copy-done.4, bf16[256,512]{1,0:T(8,128)(2,1)S(1)} %bitcast.15, f32[256,512]{1,0:T(8,128)S(1)} %get-tuple-element.26.src_unit_ref.unit_ref, ...), custom_call_target="tpu_custom_call" | custom-call | tf_op jit(solution)/shard_map/own/pallas_call | solution.py:407
  12.9 1.4 %collective-permute-done.1.refs_1_.refs_2_ = bf16[256,512]{1,0:T(8,128)(2,1)S(1)} collective-permute-done((bf16[256,512]{1,0:T(8,128)(2,1)}, bf16[256,512]{1,0:T(8,128)(2,1)S(1)}, u32[]{:S(2)}, u32[]{:S(2)}) %collective-permute-start.1) | collective-permute-done | bytes 262176 | tf_op jit(solution)/shard_map/ppermute | solution.py:368
  14.3 2.7 %collective-permute-done.refs_0_.refs_1_ = bf16[256,512]{1,0:T(8,128)(2,1)S(1)} collective-permute-done((bf16[256,512]{1,0:T(8,128)(2,1)}, bf16[256,512]{1,0:T(8,128)(2,1)S(1)}, u32[]{:S(2)}, u32[]{:S(2)}) %collective-permute-start) | collective-permute-done | bytes 262176 | tf_op jit(solution)/shard_map/ppermute | solution.py:369
  17.0 2.0 %halo.1 = (bf16[1,256,512]{2,1,0:T(8,128)(2,1)S(1)}, bf16[256,512]{1,0:T(8,128)(2,1)S(1)}, bf16[512,512]{1,0:T(8,128)(2,1)S(1)}) custom-call(s32[1]{0:T(128)} %bitcast.1.grp_ref, bf16[512,512]{1,0:T(8,128)(2,1)S(1)} %copy-done.1, f32[256,512]{1,0:T(8,128)S(1)} %get-tuple-element.26.src_unit_ref.unit_ref, f32[256,128]{1,0:T(8,128)S(1)} %get-tuple-element.32.inv_ref, ...), custom_call_target="tpu_custom_call" | custom-call | tf_op jit(solution)/shard_map/halo/pallas_call | solution.py:422
  19.0 0.1 collective-permute-start.2
  19.1 1.6 %collective-permute-start.3 = (bf16[320,128]{1,0:T(8,128)(2,1)S(1)}, bf16[320,128]{1,0:T(8,128)(2,1)S(1)}, u32[]{:S(2)}, u32[]{:S(2)}) collective-permute-start(bf16[320,128]{1,0:T(8,128)(2,1)S(1)} %get-tuple-element.39), channel_id=1, source_target_pairs={{0,4},{1,5},{2,6},{3,7},{4,0},{5,1},{6,2},{7,3},{8,12},{9,13},{10,... | collective-permute-start | bytes 245768 | tf_op jit(solution)/shard_map/ppermute | solution.py:339
  20.7 2.6 %collective-permute-start.4 = (bf16[320,128]{1,0:T(8,128)(2,1)S(1)}, bf16[320,128]{1,0:T(8,128)(2,1)S(1)}, u32[]{:S(2)}, u32[]{:S(2)}) collective-permute-start(bf16[320,128]{1,0:T(8,128)(2,1)S(1)} %get-tuple-element.40), channel_id=1, source_target_pairs={{0,8},{1,9},{2,10},{3,11},{4,12},{5,13},{6,14},{7,15},{8,0},{9,1},... | collective-permute-start | bytes 245768 | tf_op jit(solution)/shard_map/ppermute | solution.py:339
  23.3 0.2 collective-permute-start.5
  23.6 0.4 shard_map.86.refs_0_
  24.0 0.0 collective-permute-done.3.refs_3_
  24.0 6.2 %collective-permute-done.4.refs_4_ = bf16[320,128]{1,0:T(8,128)(2,1)S(1)} collective-permute-done((bf16[320,128]{1,0:T(8,128)(2,1)S(1)}, bf16[320,128]{1,0:T(8,128)(2,1)S(1)}, u32[]{:S(2)}, u32[]{:S(2)}) %collective-permute-start.4) | collective-permute-done | bytes 81952 | tf_op jit(solution)/shard_map/ppermute | solution.py:339
  30.2 0.0 collective-permute-done.5.refs_5_
  30.2 0.0 collective-permute-done.2.refs_1_
  30.2 0.1 shard_map.87
  30.4 1.9 %collective-permute-start.6 = (bf16[336,128]{1,0:T(8,128)(2,1)S(1)}, bf16[336,128]{1,0:T(8,128)(2,1)S(1)}, u32[]{:S(2)}, u32[]{:S(2)}) collective-permute-start(bf16[336,128]{1,0:T(8,128)(2,1)S(1)} %get-tuple-element.43), channel_id=1, source_target_pairs={{0,1},{1,0},{2,3},{3,2},{4,5},{5,4},{6,7},{7,6},{8,9},{9,8},{10,11... | collective-permute-start | bytes 258056 | tf_op jit(solution)/shard_map/ppermute | solution.py:339
  32.3 0.2 collective-permute-start.7
  32.4 1.5 %collective-permute-start.8 = (bf16[336,128]{1,0:T(8,128)(2,1)S(1)}, bf16[336,128]{1,0:T(8,128)(2,1)S(1)}, u32[]{:S(2)}, u32[]{:S(2)}) collective-permute-start(bf16[336,128]{1,0:T(8,128)(2,1)S(1)} %get-tuple-element.45), channel_id=1, source_target_pairs={{0,3},{1,2},{2,1},{3,0},{4,7},{5,6},{6,5},{7,4},{8,11},{9,10},{10,... | collective-permute-start | bytes 258056 | tf_op jit(solution)/shard_map/ppermute | solution.py:339
  33.9 1.9 %collective-permute-done.6.refs_1_ = bf16[336,128]{1,0:T(8,128)(2,1)S(1)} collective-permute-done((bf16[336,128]{1,0:T(8,128)(2,1)S(1)}, bf16[336,128]{1,0:T(8,128)(2,1)S(1)}, u32[]{:S(2)}, u32[]{:S(2)}) %collective-permute-start.6) | collective-permute-done | bytes 86048 | tf_op jit(solution)/shard_map/ppermute | solution.py:339
  35.8 0.9 %collective-permute-done.7.refs_2_ = bf16[336,128]{1,0:T(8,128)(2,1)S(1)} collective-permute-done((bf16[336,128]{1,0:T(8,128)(2,1)S(1)}, bf16[336,128]{1,0:T(8,128)(2,1)S(1)}, u32[]{:S(2)}, u32[]{:S(2)}) %collective-permute-start.7) | collective-permute-done | bytes 86048 | tf_op jit(solution)/shard_map/ppermute | solution.py:339
  36.8 1.1 %collective-permute-done.8.refs_3_ = bf16[336,128]{1,0:T(8,128)(2,1)S(1)} collective-permute-done((bf16[336,128]{1,0:T(8,128)(2,1)S(1)}, bf16[336,128]{1,0:T(8,128)(2,1)S(1)}, u32[]{:S(2)}, u32[]{:S(2)}) %collective-permute-start.8) | collective-permute-done | bytes 86048 | tf_op jit(solution)/shard_map/ppermute | solution.py:339
  37.9 2.8 %collective-permute-start.11 = (bf16[336,128]{1,0:T(8,128)(2,1)S(1)}, bf16[336,128]{1,0:T(8,128)(2,1)S(1)}, u32[]{:S(2)}, u32[]{:S(2)}) collective-permute-start(bf16[336,128]{1,0:T(8,128)(2,1)S(1)} %get-tuple-element.46.refs_0_), channel_id=1, source_target_pairs={{0,12},{1,13},{2,14},{3,15},{4,8},{5,9},{6,10},{7,11},{8,4},{9,5},... | collective-permute-start | bytes 258056 | tf_op jit(solution)/shard_map/ppermute | solution.py:339
  40.7 0.8 %collective-permute-start.10 = (bf16[336,128]{1,0:T(8,128)(2,1)S(1)}, bf16[336,128]{1,0:T(8,128)(2,1)S(1)}, u32[]{:S(2)}, u32[]{:S(2)}) collective-permute-start(bf16[336,128]{1,0:T(8,128)(2,1)S(1)} %get-tuple-element.46.refs_0_), channel_id=1, source_target_pairs={{0,8},{1,9},{2,10},{3,11},{4,12},{5,13},{6,14},{7,15},{8,0},{9,1},... | collective-permute-start | bytes 258056 | tf_op jit(solution)/shard_map/ppermute | solution.py:339
  41.5 0.9 %collective-permute-start.9 = (bf16[336,128]{1,0:T(8,128)(2,1)S(1)}, bf16[336,128]{1,0:T(8,128)(2,1)S(1)}, u32[]{:S(2)}, u32[]{:S(2)}) collective-permute-start(bf16[336,128]{1,0:T(8,128)(2,1)S(1)} %get-tuple-element.46.refs_0_), channel_id=1, source_target_pairs={{0,4},{1,5},{2,6},{3,7},{4,0},{5,1},{6,2},{7,3},{8,12},{9,13},{10,... | collective-permute-start | bytes 258056 | tf_op jit(solution)/shard_map/ppermute | solution.py:339
  42.3 2.7 %collective-permute-done.11.refs_3_ = bf16[336,128]{1,0:T(8,128)(2,1)S(1)} collective-permute-done((bf16[336,128]{1,0:T(8,128)(2,1)S(1)}, bf16[336,128]{1,0:T(8,128)(2,1)S(1)}, u32[]{:S(2)}, u32[]{:S(2)}) %collective-permute-start.11) | collective-permute-done | bytes 86048 | tf_op jit(solution)/shard_map/ppermute | solution.py:339
  45.0 1.9 %collective-permute-done.10.refs_2_ = bf16[336,128]{1,0:T(8,128)(2,1)S(1)} collective-permute-done((bf16[336,128]{1,0:T(8,128)(2,1)S(1)}, bf16[336,128]{1,0:T(8,128)(2,1)S(1)}, u32[]{:S(2)}, u32[]{:S(2)}) %collective-permute-start.10) | collective-permute-done | bytes 86048 | tf_op jit(solution)/shard_map/ppermute | solution.py:339
  47.0 0.0 collective-permute-done.9.refs_1_
  47.0 1.6 %collective-permute-start.14 = (bf16[496,128]{1,0:T(8,128)(2,1)S(1)}, bf16[496,128]{1,0:T(8,128)(2,1)S(1)}, u32[]{:S(2)}, u32[]{:S(2)}) collective-permute-start(bf16[496,128]{1,0:T(8,128)(2,1)S(1)} %shard_map.89.refs_0_), channel_id=1, source_target_pairs={{0,3},{1,2},{2,1},{3,0},{4,7},{5,6},{6,5},{7,4},{8,11},{9,10},{10,... | collective-permute-start | bytes 380936 | tf_op jit(solution)/shard_map/ppermute | solution.py:339
  48.6 1.4 %collective-permute-start.13 = (bf16[496,128]{1,0:T(8,128)(2,1)S(1)}, bf16[496,128]{1,0:T(8,128)(2,1)S(1)}, u32[]{:S(2)}, u32[]{:S(2)}) collective-permute-start(bf16[496,128]{1,0:T(8,128)(2,1)S(1)} %shard_map.89.refs_0_), channel_id=1, source_target_pairs={{0,2},{1,3},{2,0},{3,1},{4,6},{5,7},{6,4},{7,5},{8,10},{9,11},{10,... | collective-permute-start | bytes 380936 | tf_op jit(solution)/shard_map/ppermute | solution.py:339
  50.0 0.6 collective-permute-start.12
  50.6 2.4 %collective-permute-done.14.refs_3_ = bf16[496,128]{1,0:T(8,128)(2,1)S(1)} collective-permute-done((bf16[496,128]{1,0:T(8,128)(2,1)S(1)}, bf16[496,128]{1,0:T(8,128)(2,1)S(1)}, u32[]{:S(2)}, u32[]{:S(2)}) %collective-permute-start.14) | collective-permute-done | bytes 127008 | tf_op jit(solution)/shard_map/ppermute | solution.py:339
  53.0 1.3 %collective-permute-done.13.refs_2_ = bf16[496,128]{1,0:T(8,128)(2,1)S(1)} collective-permute-done((bf16[496,128]{1,0:T(8,128)(2,1)S(1)}, bf16[496,128]{1,0:T(8,128)(2,1)S(1)}, u32[]{:S(2)}, u32[]{:S(2)}) %collective-permute-start.13) | collective-permute-done | bytes 127008 | tf_op jit(solution)/shard_map/ppermute | solution.py:339
  54.3 0.6 %collective-permute-done.12.refs_1_ = bf16[496,128]{1,0:T(8,128)(2,1)S(1)} collective-permute-done((bf16[496,128]{1,0:T(8,128)(2,1)S(1)}, bf16[496,128]{1,0:T(8,128)(2,1)S(1)}, u32[]{:S(2)}, u32[]{:S(2)}) %collective-permute-start.12) | collective-permute-done | bytes 127008 | tf_op jit(solution)/shard_map/ppermute | solution.py:339
  54.9 0.1 collective-permute-start.15
  55.0 1.9 %collective-permute-start.18 = (bf16[80,128]{1,0:T(8,128)(2,1)S(1)}, bf16[80,128]{1,0:T(8,128)(2,1)S(1)}, u32[]{:S(2)}, u32[]{:S(2)}) collective-permute-start(bf16[80,128]{1,0:T(8,128)(2,1)S(1)} %get-tuple-element.47.refs_4_), channel_id=1, source_target_pairs={{0,3},{1,2},{2,1},{3,0},{4,7},{5,6},{6,5},{7,4},{8,11},{9,10},{10,... | collective-permute-start | bytes 61448 | tf_op jit(solution)/shard_map/ppermute | solution.py:339
  56.9 0.4 collective-permute-start.17
  57.3 1.2 %collective-permute-start.16 = (bf16[80,128]{1,0:T(8,128)(2,1)S(1)}, bf16[80,128]{1,0:T(8,128)(2,1)S(1)}, u32[]{:S(2)}, u32[]{:S(2)}) collective-permute-start(bf16[80,128]{1,0:T(8,128)(2,1)S(1)} %get-tuple-element.47.refs_4_), channel_id=1, source_target_pairs={{0,1},{1,0},{2,3},{3,2},{4,5},{5,4},{6,7},{7,6},{8,9},{9,8},{10,11... | collective-permute-start | bytes 61448 | tf_op jit(solution)/shard_map/ppermute | solution.py:339
  58.6 1.2 %collective-permute-done.18.refs_7_ = bf16[80,128]{1,0:T(8,128)(2,1)S(1)} collective-permute-done((bf16[80,128]{1,0:T(8,128)(2,1)S(1)}, bf16[80,128]{1,0:T(8,128)(2,1)S(1)}, u32[]{:S(2)}, u32[]{:S(2)}) %collective-permute-start.18) | collective-permute-done | bytes 20512 | tf_op jit(solution)/shard_map/ppermute | solution.py:339
  59.8 0.9 %collective-permute-done.17.refs_6_ = bf16[80,128]{1,0:T(8,128)(2,1)S(1)} collective-permute-done((bf16[80,128]{1,0:T(8,128)(2,1)S(1)}, bf16[80,128]{1,0:T(8,128)(2,1)S(1)}, u32[]{:S(2)}, u32[]{:S(2)}) %collective-permute-start.17) | collective-permute-done | bytes 20512 | tf_op jit(solution)/shard_map/ppermute | solution.py:339
  60.7 0.4 collective-permute-done.16.refs_5_
  61.1 1.3 %unpack.1 = (f32[512,512]{1,0:T(8,128)}, f32[512,512]{1,0:T(8,128)}) custom-call(s32[1]{0:T(128)} %bitcast.run_ref, s32[1]{0:T(128)} %bitcast.1.grp_ref, bf16[1024,128]{1,0:T(8,128)(2,1)S(1)} %shard_map.90.half_in_ref, bf16[496,128]{1,0:T(8,128)(2,1)S(1)} %shard_map.89.refs_0_, bf16[496,128]{1,0:T(8,128)(2,1)S(1)} %collective-permute-done.12.refs_1_, ...), custom_call_target="tpu_custom_call" | custom-call | tf_op jit(solution)/shard_map/unpack/pallas_call | solution.py:476
  62.4 0.0 collective-permute-done.15.refs_0_
  62.4 0.8 %place.1 = f32[512,512]{1,0:T(8,128)} custom-call(s32[1]{0:T(128)} %bitcast.run_ref, s32[1]{0:T(128)} %bitcast.1.grp_ref, bf16[1024,128]{1,0:T(8,128)(2,1)S(1)} %collective-permute-done.15.refs_0_, f32[512,512]{1,0:T(8,128)} %get-tuple-element.48.refs_1_), custom_call_target="tpu_custom_call", output_to_operand_aliasing={{}: (3, {})} | custom-call | tf_op jit(solution)/shard_map/place/pallas_call | solution.py:490
  (10 shorter events, 0.1 us)
Async XLA Ops:
  0.6 13.6 %collective-permute-start.1 = (bf16[256,512]{1,0:T(8,128)(2,1)}, bf16[256,512]{1,0:T(8,128)(2,1)S(1)}, u32[]{:S(2)}, u32[]{:S(2)}) collective-permute-start(bf16[256,512]{1,0:T(8,128)(2,1)} %bitcast.12), channel_id=1, source_target_pairs={{1,2},{3,4},{5,6},{7,8},{9,10},{11,12},{13,14},{15,0},{2,1},{4,3},... | collective-permute-start | bytes 786440 | tf_op jit(solution)/shard_map/ppermute | solution.py:368
  7.7 9.4 %collective-permute-start = (bf16[256,512]{1,0:T(8,128)(2,1)}, bf16[256,512]{1,0:T(8,128)(2,1)S(1)}, u32[]{:S(2)}, u32[]{:S(2)}) collective-permute-start(bf16[256,512]{1,0:T(8,128)(2,1)} %bitcast.13), channel_id=1, source_target_pairs={{0,1},{2,3},{4,5},{6,7},{8,9},{10,11},{12,13},{14,15},{1,0},{3,2},... | collective-permute-start | bytes 786440 | tf_op jit(solution)/shard_map/ppermute | solution.py:369
  7.7 2.5 %copy-start.2 = (bf16[1,256,512]{2,1,0:T(8,128)(2,1)S(1)}, bf16[1,256,512]{2,1,0:T(8,128)(2,1)}, u32[]{:S(2)}) copy-start(bf16[1,256,512]{2,1,0:T(8,128)(2,1)} %param.8) | copy-start | bytes 786436
  10.1 0.7 %copy-start.3 = (s32[1,2,4]{2,1,0:T(2,128)S(1)}, s32[1,2,4]{2,1,0:T(2,128)}, u32[]{:S(2)}) copy-start(s32[1,2,4]{2,1,0:T(2,128)} %param.10) | copy-start | bytes 100
  10.1 0.7 %copy-start.4 = (s32[1,2]{1,0:T(1,128)S(1)}, s32[1,2]{1,0:T(1,128)}, u32[]{:S(2)}) copy-start(s32[1,2]{1,0:T(1,128)} %live_ref.1) | copy-start | bytes 28
  10.8 6.2 %copy-start = (bf16[1,256,512]{2,1,0:T(8,128)(2,1)S(1)}, bf16[1,256,512]{2,1,0:T(8,128)(2,1)}, u32[]{:S(2)}) copy-start(bf16[1,256,512]{2,1,0:T(8,128)(2,1)} %param.7) | copy-start | bytes 786436
  10.8 6.2 %copy-start.1 = (bf16[512,512]{1,0:T(8,128)(2,1)S(1)}, bf16[512,512]{1,0:T(8,128)(2,1)}, u32[]{:S(2)}) copy-start(bf16[512,512]{1,0:T(8,128)(2,1)} %w_ref.1) | copy-start | bytes 1572868
  19.0 11.2 %collective-permute-start.2 = (bf16[256,512]{1,0:T(8,128)(2,1)S(1)}, bf16[256,512]{1,0:T(8,128)(2,1)S(1)}, u32[]{:S(2)}, u32[]{:S(2)}) collective-permute-start(bf16[256,512]{1,0:T(8,128)(2,1)S(1)} %bitcast.17), channel_id=1, source_target_pairs={{0,16},{16,0},{1,17},{17,1},{2,18},{18,2},{3,19},{19,3},{4,20},{20... | collective-permute-start | bytes 786440 | tf_op jit(solution)/shard_map/ppermute | solution.py:436
  19.1 4.9 %collective-permute-start.3 = (bf16[320,128]{1,0:T(8,128)(2,1)S(1)}, bf16[320,128]{1,0:T(8,128)(2,1)S(1)}, u32[]{:S(2)}, u32[]{:S(2)}) collective-permute-start(bf16[320,128]{1,0:T(8,128)(2,1)S(1)} %get-tuple-element.39), channel_id=1, source_target_pairs={{0,4},{1,5},{2,6},{3,7},{4,0},{5,1},{6,2},{7,3},{8,12},{9,13},{10,... | collective-permute-start | bytes 245768 | tf_op jit(solution)/shard_map/ppermute | solution.py:339
  20.7 9.5 %collective-permute-start.4 = (bf16[320,128]{1,0:T(8,128)(2,1)S(1)}, bf16[320,128]{1,0:T(8,128)(2,1)S(1)}, u32[]{:S(2)}, u32[]{:S(2)}) collective-permute-start(bf16[320,128]{1,0:T(8,128)(2,1)S(1)} %get-tuple-element.40), channel_id=1, source_target_pairs={{0,8},{1,9},{2,10},{3,11},{4,12},{5,13},{6,14},{7,15},{8,0},{9,1},... | collective-permute-start | bytes 245768 | tf_op jit(solution)/shard_map/ppermute | solution.py:339
  23.3 6.9 %collective-permute-start.5 = (bf16[320,128]{1,0:T(8,128)(2,1)S(1)}, bf16[320,128]{1,0:T(8,128)(2,1)S(1)}, u32[]{:S(2)}, u32[]{:S(2)}) collective-permute-start(bf16[320,128]{1,0:T(8,128)(2,1)S(1)} %get-tuple-element.41), channel_id=1, source_target_pairs={{0,12},{1,13},{2,14},{3,15},{4,8},{5,9},{6,10},{7,11},{8,4},{9,5},... | collective-permute-start | bytes 245768 | tf_op jit(solution)/shard_map/ppermute | solution.py:339
  30.4 5.4 %collective-permute-start.6 = (bf16[336,128]{1,0:T(8,128)(2,1)S(1)}, bf16[336,128]{1,0:T(8,128)(2,1)S(1)}, u32[]{:S(2)}, u32[]{:S(2)}) collective-permute-start(bf16[336,128]{1,0:T(8,128)(2,1)S(1)} %get-tuple-element.43), channel_id=1, source_target_pairs={{0,1},{1,0},{2,3},{3,2},{4,5},{5,4},{6,7},{7,6},{8,9},{9,8},{10,11... | collective-permute-start | bytes 258056 | tf_op jit(solution)/shard_map/ppermute | solution.py:339
  32.3 4.5 %collective-permute-start.7 = (bf16[336,128]{1,0:T(8,128)(2,1)S(1)}, bf16[336,128]{1,0:T(8,128)(2,1)S(1)}, u32[]{:S(2)}, u32[]{:S(2)}) collective-permute-start(bf16[336,128]{1,0:T(8,128)(2,1)S(1)} %get-tuple-element.44), channel_id=1, source_target_pairs={{0,2},{1,3},{2,0},{3,1},{4,6},{5,7},{6,4},{7,5},{8,10},{9,11},{10,... | collective-permute-start | bytes 258056 | tf_op jit(solution)/shard_map/ppermute | solution.py:339
  32.4 5.4 %collective-permute-start.8 = (bf16[336,128]{1,0:T(8,128)(2,1)S(1)}, bf16[336,128]{1,0:T(8,128)(2,1)S(1)}, u32[]{:S(2)}, u32[]{:S(2)}) collective-permute-start(bf16[336,128]{1,0:T(8,128)(2,1)S(1)} %get-tuple-element.45), channel_id=1, source_target_pairs={{0,3},{1,2},{2,1},{3,0},{4,7},{5,6},{6,5},{7,4},{8,11},{9,10},{10,... | collective-permute-start | bytes 258056 | tf_op jit(solution)/shard_map/ppermute | solution.py:339
  37.9 7.2 %collective-permute-start.11 = (bf16[336,128]{1,0:T(8,128)(2,1)S(1)}, bf16[336,128]{1,0:T(8,128)(2,1)S(1)}, u32[]{:S(2)}, u32[]{:S(2)}) collective-permute-start(bf16[336,128]{1,0:T(8,128)(2,1)S(1)} %get-tuple-element.46.refs_0_), channel_id=1, source_target_pairs={{0,12},{1,13},{2,14},{3,15},{4,8},{5,9},{6,10},{7,11},{8,4},{9,5},... | collective-permute-start | bytes 258056 | tf_op jit(solution)/shard_map/ppermute | solution.py:339
  40.7 6.3 %collective-permute-start.10 = (bf16[336,128]{1,0:T(8,128)(2,1)S(1)}, bf16[336,128]{1,0:T(8,128)(2,1)S(1)}, u32[]{:S(2)}, u32[]{:S(2)}) collective-permute-start(bf16[336,128]{1,0:T(8,128)(2,1)S(1)} %get-tuple-element.46.refs_0_), channel_id=1, source_target_pairs={{0,8},{1,9},{2,10},{3,11},{4,12},{5,13},{6,14},{7,15},{8,0},{9,1},... | collective-permute-start | bytes 258056 | tf_op jit(solution)/shard_map/ppermute | solution.py:339
  41.5 5.5 %collective-permute-start.9 = (bf16[336,128]{1,0:T(8,128)(2,1)S(1)}, bf16[336,128]{1,0:T(8,128)(2,1)S(1)}, u32[]{:S(2)}, u32[]{:S(2)}) collective-permute-start(bf16[336,128]{1,0:T(8,128)(2,1)S(1)} %get-tuple-element.46.refs_0_), channel_id=1, source_target_pairs={{0,4},{1,5},{2,6},{3,7},{4,0},{5,1},{6,2},{7,3},{8,12},{9,13},{10,... | collective-permute-start | bytes 258056 | tf_op jit(solution)/shard_map/ppermute | solution.py:339
  47.0 6.0 %collective-permute-start.14 = (bf16[496,128]{1,0:T(8,128)(2,1)S(1)}, bf16[496,128]{1,0:T(8,128)(2,1)S(1)}, u32[]{:S(2)}, u32[]{:S(2)}) collective-permute-start(bf16[496,128]{1,0:T(8,128)(2,1)S(1)} %shard_map.89.refs_0_), channel_id=1, source_target_pairs={{0,3},{1,2},{2,1},{3,0},{4,7},{5,6},{6,5},{7,4},{8,11},{9,10},{10,... | collective-permute-start | bytes 380936 | tf_op jit(solution)/shard_map/ppermute | solution.py:339
  48.6 5.7 %collective-permute-start.13 = (bf16[496,128]{1,0:T(8,128)(2,1)S(1)}, bf16[496,128]{1,0:T(8,128)(2,1)S(1)}, u32[]{:S(2)}, u32[]{:S(2)}) collective-permute-start(bf16[496,128]{1,0:T(8,128)(2,1)S(1)} %shard_map.89.refs_0_), channel_id=1, source_target_pairs={{0,2},{1,3},{2,0},{3,1},{4,6},{5,7},{6,4},{7,5},{8,10},{9,11},{10,... | collective-permute-start | bytes 380936 | tf_op jit(solution)/shard_map/ppermute | solution.py:339
  50.0 4.9 %collective-permute-start.12 = (bf16[496,128]{1,0:T(8,128)(2,1)S(1)}, bf16[496,128]{1,0:T(8,128)(2,1)S(1)}, u32[]{:S(2)}, u32[]{:S(2)}) collective-permute-start(bf16[496,128]{1,0:T(8,128)(2,1)S(1)} %shard_map.89.refs_0_), channel_id=1, source_target_pairs={{0,1},{1,0},{2,3},{3,2},{4,5},{5,4},{6,7},{7,6},{8,9},{9,8},{10,11... | collective-permute-start | bytes 380936 | tf_op jit(solution)/shard_map/ppermute | solution.py:339
  54.9 7.5 %collective-permute-start.15 = (bf16[1024,128]{1,0:T(8,128)(2,1)S(1)}, bf16[1024,128]{1,0:T(8,128)(2,1)S(1)}, u32[]{:S(2)}, u32[]{:S(2)}) collective-permute-start(bf16[1024,128]{1,0:T(8,128)(2,1)S(1)} %shard_map.90.half_in_ref), channel_id=1, source_target_pairs={{0,16},{16,0},{1,17},{17,1},{2,18},{18,2},{3,19},{19,3},{4,20},{20... | collective-permute-start | bytes 786440 | tf_op jit(solution)/shard_map/ppermute | solution.py:472
  55.0 4.8 %collective-permute-start.18 = (bf16[80,128]{1,0:T(8,128)(2,1)S(1)}, bf16[80,128]{1,0:T(8,128)(2,1)S(1)}, u32[]{:S(2)}, u32[]{:S(2)}) collective-permute-start(bf16[80,128]{1,0:T(8,128)(2,1)S(1)} %get-tuple-element.47.refs_4_), channel_id=1, source_target_pairs={{0,3},{1,2},{2,1},{3,0},{4,7},{5,6},{6,5},{7,4},{8,11},{9,10},{10,... | collective-permute-start | bytes 61448 | tf_op jit(solution)/shard_map/ppermute | solution.py:339
  56.9 3.8 %collective-permute-start.17 = (bf16[80,128]{1,0:T(8,128)(2,1)S(1)}, bf16[80,128]{1,0:T(8,128)(2,1)S(1)}, u32[]{:S(2)}, u32[]{:S(2)}) collective-permute-start(bf16[80,128]{1,0:T(8,128)(2,1)S(1)} %get-tuple-element.47.refs_4_), channel_id=1, source_target_pairs={{0,2},{1,3},{2,0},{3,1},{4,6},{5,7},{6,4},{7,5},{8,10},{9,11},{10,... | collective-permute-start | bytes 61448 | tf_op jit(solution)/shard_map/ppermute | solution.py:339
  57.3 3.8 %collective-permute-start.16 = (bf16[80,128]{1,0:T(8,128)(2,1)S(1)}, bf16[80,128]{1,0:T(8,128)(2,1)S(1)}, u32[]{:S(2)}, u32[]{:S(2)}) collective-permute-start(bf16[80,128]{1,0:T(8,128)(2,1)S(1)} %get-tuple-element.47.refs_4_), channel_id=1, source_target_pairs={{0,1},{1,0},{2,3},{3,2},{4,5},{5,4},{6,7},{7,6},{8,9},{9,8},{10,11... | collective-permute-start | bytes 61448 | tf_op jit(solution)/shard_map/ppermute | solution.py:339

commit v7 on v6

--- a/solution.py
+++ b/solution.py
@@ -81,23 +81,19 @@
     return (order * blocks + lax.rem(listed, blocks)) * block
 
 
-def pair_counts(list_ref, live_ref, src_ref, tgt_ref, block, run, runs, reach):
+def pair_counts(list_ref, live_ref, src_ref, tgt_ref, count_ref, block, run, runs, reach):
     blocks, slots, pairs = src_ref.shape
-    candidates = (2 * reach + 1) * blocks
+    spare = (2 * reach + 1) * blocks * block
     point = lax.broadcasted_iota(jnp.int32, (block, pairs), 0)
-    place = lax.broadcasted_iota(jnp.int32, (candidates * block, pairs), 0)
-    rows = []
+    count_ref[...] = jnp.zeros_like(count_ref)
     for b in range(blocks):
-        left = []
-        right = []
         for s in range(slots):
             first = slot_start(list_ref[b, s], blocks, block, run, runs, reach)
-            first = jnp.where(s < live_ref[0, b], first, -block)
-            key = tgt_ref[b, s : s + 1, :] + first
-            left.append(jnp.where(src_ref[b, s : s + 1, :] == point, 1.0, 0.0).astype(bf16))
-            right.append(jnp.where(key == place, 1.0, 0.0).astype(bf16))
-        rows.append(dot_nt(jnp.concatenate(left, axis=1), jnp.concatenate(right, axis=1)))
-    return jnp.concatenate(rows, axis=0)
+            first = jnp.where(s < live_ref[0, b], first, spare)
+            left = jnp.where(src_ref[b, s : s + 1, :] == point, 1.0, 0.0).astype(bf16)
+            right = jnp.where(tgt_ref[b, s : s + 1, :] == point, 1.0, 0.0).astype(bf16)
+            place = (slice(b * block, (b + 1) * block), pl.ds(pl.multiple_of(first, block), block))
+            count_ref[place] = count_ref[place] + dot_nt(left, right)
 
 
 def load(pairs, sem):
@@ -155,18 +151,18 @@
 def own_kernel(
     runs, reach,
     run_ref, list_ref, live_ref, xt_ref, src_unit_ref, tgt_unit_ref, tgt_inv_ref, src_ref, tgt_ref,
-    count_ref, grad_ref, part_ref,
+    count_ref, grad_ref, part_ref, all_ref,
 ):
     zs = src_unit_ref[...].astype(bf16)
     own = xt_ref.shape[0]
     block = own // src_ref.shape[0]
-    counts = pair_counts(
-        list_ref, live_ref, src_ref, tgt_ref, block, run_ref[0], runs, reach
-    )
-    count_ref[...] = counts[:, own:].astype(bf16)
+    pair_counts(
+        list_ref, live_ref, src_ref, tgt_ref, all_ref, block, run_ref[0], runs, reach
+    )
+    count_ref[...] = all_ref[:, own : own * (2 * reach + 1)].astype(bf16)
     rows = xt_ref[...]
     grad_ref[...], tgt_grad = score(
-        tgt_unit_ref[...], tgt_inv_ref[:, :1], zs, counts[:, :own], block
+        tgt_unit_ref[...], tgt_inv_ref[:, :1], zs, all_ref[:, :own], block
     )
     part_ref[...] = dot_tn(rows, tgt_grad)
 
@@ -413,6 +409,7 @@
         ),
         in_specs=[smem] * 3 + [vmem] * 6,
         out_specs=(vmem,) * 3,
+        scratch_shapes=[pltpu.VMEM((points, (2 * reach + 1) * points + block), f32)],
         compiler_params=room(16 + 4 * reach),
         name="own",
     )(

time: 63.4 us -> 63.4 us (level)
  transfers between devices with their start and end apart: 19 -> 19, of which waited for: 14 -> 14; matrix products, arithmetic and copies ran while one was open for 0% -> 0% of each run, Pallas kernels for 10% -> 9%
where the time goes in v7:
time: 63.4 us; the launch traced here: 63.3 us
  starting transfers between devices  26.7 us (42%)
  waiting for transfers between devices  26 us (41%)
  Pallas kernels  9.06 us (14%)
  between operations  0.75 us (1%)
  local copies, waits for them, and re-layouts  0.67 us (1%)
    ppermute x15, waiting for transfers between devices, swap(): return lax.ppermute(array, 'blk', [(i, i ^ bits) for i in range(runs)])  21.7 us
    ppermute x15, starting transfers between devices, swap(): return lax.ppermute(array, 'blk', [(i, i ^ bits) for i in range(runs)])  19.6 us
    ppermute x1, starting transfers between devices, body(): odd = [lax.ppermute(xt, 'blk', partners(k, 1, runs)) for k in hops]  7.02 us
    ppermute x1, waiting for transfers between devices, body(): even = [lax.ppermute(xt, 'blk', partners(k, 0, runs)) for k in hops]  2.74 us
    pallas_call x1, Pallas kernels, body(): pl.pallas_call(functools.partial(moment_kernel, far, near, scale), out_sh...  2.45 us
    pallas_call x1, Pallas kernels, body(): pl.pallas_call(functools.partial(halo_kernel, block, groups), out_shape=(...  1.99 us
    pallas_call x1, Pallas kernels, body(): pl.pallas_call(functools.partial(own_kernel, runs, reach), out_shape=(jax...  1.86 us
    ppermute x1, waiting for transfers between devices, body(): odd = [lax.ppermute(xt, 'blk', partners(k, 1, runs)) for k in hops]  1.6 us
  transfers between devices with their start and end apart: 19, of which 14 were waited for; matrix products, arithmetic and copies ran while one was open for 0% of the time, Pallas kernels for 9%

profile of v7, /device:TPU:0, one launch (start us, length us, event | category | flops | bytes accessed | tf_op | source)
XLA Modules:
  0.0 63.3 jit_solution(2171253212795900261)
XLA Ops:
  0.6 7.0 %collective-permute-start.1 = (bf16[256,512]{1,0:T(8,128)(2,1)}, bf16[256,512]{1,0:T(8,128)(2,1)S(1)}, u32[]{:S(2)}, u32[]{:S(2)}) collective-permute-start(bf16[256,512]{1,0:T(8,128)(2,1)} %bitcast.12), channel_id=1, source_target_pairs={{1,2},{3,4},{5,6},{7,8},{9,10},{11,12},{13,14},{15,0},{2,1},{4,3},... | collective-permute-start | bytes 786440 | tf_op jit(solution)/shard_map/ppermute | solution.py:364
  7.7 0.0 collective-permute-start
  7.7 2.5 %moment.1 = (bf16[320,128]{1,0:T(8,128)(2,1)S(1)}, bf16[320,128]{1,0:T(8,128)(2,1)S(1)}, bf16[320,128]{1,0:T(8,128)(2,1)S(1)}, bf16[320,128]{1,0:T(8,128)(2,1)S(...) custom-call(s32[1]{0:T(128)} %bitcast.run_ref, ...), custom_call_target="tpu_custom_call" | custom-call | tf_op jit(solution)/shard_map/moment/pallas_call | solution.py:384
  10.1 0.0 copy-start.3
  10.1 0.0 copy-start.4
  10.2 0.6 %copy-done.3 = s32[1,2,4]{2,1,0:T(2,128)S(1)} copy-done((s32[1,2,4]{2,1,0:T(2,128)S(1)}, s32[1,2,4]{2,1,0:T(2,128)}, u32[]{:S(2)}) %copy-start.3) | copy-done | bytes 56
  10.8 1.9 %own.1 = (bf16[256,512]{1,0:T(8,128)(2,1)S(1)}, f32[256,512]{1,0:T(8,128)S(1)}, f32[512,512]{1,0:T(8,128)S(1)}) custom-call(s32[1]{0:T(128)} %bitcast.run_ref, s32[2,4]{1,0:T(2,128)S(1)} %bitcast.16, s32[1,2]{1,0:T(1,128)S(1)} %copy-done.4, bf16[256,512]{1,0:T(8,128)(2,1)S(1)} %bitcast.15, f32[256,512]{1,0:T(8,128)S(1)} %get-tuple-element.26.src_unit_ref.unit_ref, ...), custom_call_target="tpu_custom_call" | custom-call | tf_op jit(solution)/shard_map/own/pallas_call | solution.py:403
  12.7 1.6 %collective-permute-done.1.refs_1_.refs_2_ = bf16[256,512]{1,0:T(8,128)(2,1)S(1)} collective-permute-done((bf16[256,512]{1,0:T(8,128)(2,1)}, bf16[256,512]{1,0:T(8,128)(2,1)S(1)}, u32[]{:S(2)}, u32[]{:S(2)}) %collective-permute-start.1) | collective-permute-done | bytes 262176 | tf_op jit(solution)/shard_map/ppermute | solution.py:364
  14.3 2.7 %collective-permute-done.refs_0_.refs_1_ = bf16[256,512]{1,0:T(8,128)(2,1)S(1)} collective-permute-done((bf16[256,512]{1,0:T(8,128)(2,1)}, bf16[256,512]{1,0:T(8,128)(2,1)S(1)}, u32[]{:S(2)}, u32[]{:S(2)}) %collective-permute-start) | collective-permute-done | bytes 262176 | tf_op jit(solution)/shard_map/ppermute | solution.py:365
  17.0 2.0 %halo.1 = (bf16[1,256,512]{2,1,0:T(8,128)(2,1)S(1)}, bf16[256,512]{1,0:T(8,128)(2,1)S(1)}, bf16[512,512]{1,0:T(8,128)(2,1)S(1)}) custom-call(s32[1]{0:T(128)} %bitcast.1.grp_ref, bf16[512,512]{1,0:T(8,128)(2,1)S(1)} %copy-done.1, f32[256,512]{1,0:T(8,128)S(1)} %get-tuple-element.26.src_unit_ref.unit_ref, f32[256,128]{1,0:T(8,128)S(1)} %get-tuple-element.32.inv_ref, ...), custom_call_target="tpu_custom_call" | custom-call | tf_op jit(solution)/shard_map/halo/pallas_call | solution.py:419
  19.0 0.1 collective-permute-start.2
  19.1 1.6 %collective-permute-start.3 = (bf16[320,128]{1,0:T(8,128)(2,1)S(1)}, bf16[320,128]{1,0:T(8,128)(2,1)S(1)}, u32[]{:S(2)}, u32[]{:S(2)}) collective-permute-start(bf16[320,128]{1,0:T(8,128)(2,1)S(1)} %get-tuple-element.39), channel_id=1, source_target_pairs={{0,4},{1,5},{2,6},{3,7},{4,0},{5,1},{6,2},{7,3},{8,12},{9,13},{10,... | collective-permute-start | bytes 245768 | tf_op jit(solution)/shard_map/ppermute | solution.py:335
  20.7 2.6 %collective-permute-start.4 = (bf16[320,128]{1,0:T(8,128)(2,1)S(1)}, bf16[320,128]{1,0:T(8,128)(2,1)S(1)}, u32[]{:S(2)}, u32[]{:S(2)}) collective-permute-start(bf16[320,128]{1,0:T(8,128)(2,1)S(1)} %get-tuple-element.40), channel_id=1, source_target_pairs={{0,8},{1,9},{2,10},{3,11},{4,12},{5,13},{6,14},{7,15},{8,0},{9,1},... | collective-permute-start | bytes 245768 | tf_op jit(solution)/shard_map/ppermute | solution.py:335
  23.3 0.2 collective-permute-start.5
  23.6 0.4 shard_map.86.refs_0_
  24.0 0.0 collective-permute-done.3.refs_3_
  24.0 6.2 %collective-permute-done.4.refs_4_ = bf16[320,128]{1,0:T(8,128)(2,1)S(1)} collective-permute-done((bf16[320,128]{1,0:T(8,128)(2,1)S(1)}, bf16[320,128]{1,0:T(8,128)(2,1)S(1)}, u32[]{:S(2)}, u32[]{:S(2)}) %collective-permute-start.4) | collective-permute-done | bytes 81952 | tf_op jit(solution)/shard_map/ppermute | solution.py:335
  30.2 0.0 collective-permute-done.5.refs_5_
  30.2 0.0 collective-permute-done.2.refs_1_
  30.2 0.1 shard_map.87
  30.4 1.9 %collective-permute-start.6 = (bf16[336,128]{1,0:T(8,128)(2,1)S(1)}, bf16[336,128]{1,0:T(8,128)(2,1)S(1)}, u32[]{:S(2)}, u32[]{:S(2)}) collective-permute-start(bf16[336,128]{1,0:T(8,128)(2,1)S(1)} %get-tuple-element.43), channel_id=1, source_target_pairs={{0,1},{1,0},{2,3},{3,2},{4,5},{5,4},{6,7},{7,6},{8,9},{9,8},{10,11... | collective-permute-start | bytes 258056 | tf_op jit(solution)/shard_map/ppermute | solution.py:335
  32.3 0.2 collective-permute-start.7
  32.4 1.5 %collective-permute-start.8 = (bf16[336,128]{1,0:T(8,128)(2,1)S(1)}, bf16[336,128]{1,0:T(8,128)(2,1)S(1)}, u32[]{:S(2)}, u32[]{:S(2)}) collective-permute-start(bf16[336,128]{1,0:T(8,128)(2,1)S(1)} %get-tuple-element.45), channel_id=1, source_target_pairs={{0,3},{1,2},{2,1},{3,0},{4,7},{5,6},{6,5},{7,4},{8,11},{9,10},{10,... | collective-permute-start | bytes 258056 | tf_op jit(solution)/shard_map/ppermute | solution.py:335
  33.9 1.9 %collective-permute-done.6.refs_1_ = bf16[336,128]{1,0:T(8,128)(2,1)S(1)} collective-permute-done((bf16[336,128]{1,0:T(8,128)(2,1)S(1)}, bf16[336,128]{1,0:T(8,128)(2,1)S(1)}, u32[]{:S(2)}, u32[]{:S(2)}) %collective-permute-start.6) | collective-permute-done | bytes 86048 | tf_op jit(solution)/shard_map/ppermute | solution.py:335
  35.8 0.9 %collective-permute-done.7.refs_2_ = bf16[336,128]{1,0:T(8,128)(2,1)S(1)} collective-permute-done((bf16[336,128]{1,0:T(8,128)(2,1)S(1)}, bf16[336,128]{1,0:T(8,128)(2,1)S(1)}, u32[]{:S(2)}, u32[]{:S(2)}) %collective-permute-start.7) | collective-permute-done | bytes 86048 | tf_op jit(solution)/shard_map/ppermute | solution.py:335
  36.8 1.1 %collective-permute-done.8.refs_3_ = bf16[336,128]{1,0:T(8,128)(2,1)S(1)} collective-permute-done((bf16[336,128]{1,0:T(8,128)(2,1)S(1)}, bf16[336,128]{1,0:T(8,128)(2,1)S(1)}, u32[]{:S(2)}, u32[]{:S(2)}) %collective-permute-start.8) | collective-permute-done | bytes 86048 | tf_op jit(solution)/shard_map/ppermute | solution.py:335
  37.9 2.8 %collective-permute-start.11 = (bf16[336,128]{1,0:T(8,128)(2,1)S(1)}, bf16[336,128]{1,0:T(8,128)(2,1)S(1)}, u32[]{:S(2)}, u32[]{:S(2)}) collective-permute-start(bf16[336,128]{1,0:T(8,128)(2,1)S(1)} %get-tuple-element.46.refs_0_), channel_id=1, source_target_pairs={{0,12},{1,13},{2,14},{3,15},{4,8},{5,9},{6,10},{7,11},{8,4},{9,5},... | collective-permute-start | bytes 258056 | tf_op jit(solution)/shard_map/ppermute | solution.py:335
  40.7 0.8 %collective-permute-start.10 = (bf16[336,128]{1,0:T(8,128)(2,1)S(1)}, bf16[336,128]{1,0:T(8,128)(2,1)S(1)}, u32[]{:S(2)}, u32[]{:S(2)}) collective-permute-start(bf16[336,128]{1,0:T(8,128)(2,1)S(1)} %get-tuple-element.46.refs_0_), channel_id=1, source_target_pairs={{0,8},{1,9},{2,10},{3,11},{4,12},{5,13},{6,14},{7,15},{8,0},{9,1},... | collective-permute-start | bytes 258056 | tf_op jit(solution)/shard_map/ppermute | solution.py:335
  41.5 0.9 %collective-permute-start.9 = (bf16[336,128]{1,0:T(8,128)(2,1)S(1)}, bf16[336,128]{1,0:T(8,128)(2,1)S(1)}, u32[]{:S(2)}, u32[]{:S(2)}) collective-permute-start(bf16[336,128]{1,0:T(8,128)(2,1)S(1)} %get-tuple-element.46.refs_0_), channel_id=1, source_target_pairs={{0,4},{1,5},{2,6},{3,7},{4,0},{5,1},{6,2},{7,3},{8,12},{9,13},{10,... | collective-permute-start | bytes 258056 | tf_op jit(solution)/shard_map/ppermute | solution.py:335
  42.3 2.7 %collective-permute-done.11.refs_3_ = bf16[336,128]{1,0:T(8,128)(2,1)S(1)} collective-permute-done((bf16[336,128]{1,0:T(8,128)(2,1)S(1)}, bf16[336,128]{1,0:T(8,128)(2,1)S(1)}, u32[]{:S(2)}, u32[]{:S(2)}) %collective-permute-start.11) | collective-permute-done | bytes 86048 | tf_op jit(solution)/shard_map/ppermute | solution.py:335
  45.0 1.9 %collective-permute-done.10.refs_2_ = bf16[336,128]{1,0:T(8,128)(2,1)S(1)} collective-permute-done((bf16[336,128]{1,0:T(8,128)(2,1)S(1)}, bf16[336,128]{1,0:T(8,128)(2,1)S(1)}, u32[]{:S(2)}, u32[]{:S(2)}) %collective-permute-start.10) | collective-permute-done | bytes 86048 | tf_op jit(solution)/shard_map/ppermute | solution.py:335
  47.0 0.0 collective-permute-done.9.refs_1_
  47.0 1.6 %collective-permute-start.14 = (bf16[496,128]{1,0:T(8,128)(2,1)S(1)}, bf16[496,128]{1,0:T(8,128)(2,1)S(1)}, u32[]{:S(2)}, u32[]{:S(2)}) collective-permute-start(bf16[496,128]{1,0:T(8,128)(2,1)S(1)} %shard_map.89.refs_0_), channel_id=1, source_target_pairs={{0,3},{1,2},{2,1},{3,0},{4,7},{5,6},{6,5},{7,4},{8,11},{9,10},{10,... | collective-permute-start | bytes 380936 | tf_op jit(solution)/shard_map/ppermute | solution.py:335
  48.6 1.4 %collective-permute-start.13 = (bf16[496,128]{1,0:T(8,128)(2,1)S(1)}, bf16[496,128]{1,0:T(8,128)(2,1)S(1)}, u32[]{:S(2)}, u32[]{:S(2)}) collective-permute-start(bf16[496,128]{1,0:T(8,128)(2,1)S(1)} %shard_map.89.refs_0_), channel_id=1, source_target_pairs={{0,2},{1,3},{2,0},{3,1},{4,6},{5,7},{6,4},{7,5},{8,10},{9,11},{10,... | collective-permute-start | bytes 380936 | tf_op jit(solution)/shard_map/ppermute | solution.py:335
  50.0 0.6 collective-permute-start.12
  50.6 2.4 %collective-permute-done.14.refs_3_ = bf16[496,128]{1,0:T(8,128)(2,1)S(1)} collective-permute-done((bf16[496,128]{1,0:T(8,128)(2,1)S(1)}, bf16[496,128]{1,0:T(8,128)(2,1)S(1)}, u32[]{:S(2)}, u32[]{:S(2)}) %collective-permute-start.14) | collective-permute-done | bytes 127008 | tf_op jit(solution)/shard_map/ppermute | solution.py:335
  53.0 1.3 %collective-permute-done.13.refs_2_ = bf16[496,128]{1,0:T(8,128)(2,1)S(1)} collective-permute-done((bf16[496,128]{1,0:T(8,128)(2,1)S(1)}, bf16[496,128]{1,0:T(8,128)(2,1)S(1)}, u32[]{:S(2)}, u32[]{:S(2)}) %collective-permute-start.13) | collective-permute-done | bytes 127008 | tf_op jit(solution)/shard_map/ppermute | solution.py:335
  54.3 0.6 %collective-permute-done.12.refs_1_ = bf16[496,128]{1,0:T(8,128)(2,1)S(1)} collective-permute-done((bf16[496,128]{1,0:T(8,128)(2,1)S(1)}, bf16[496,128]{1,0:T(8,128)(2,1)S(1)}, u32[]{:S(2)}, u32[]{:S(2)}) %collective-permute-start.12) | collective-permute-done | bytes 127008 | tf_op jit(solution)/shard_map/ppermute | solution.py:335
  54.9 0.1 collective-permute-start.15
  55.0 1.9 %collective-permute-start.18 = (bf16[80,128]{1,0:T(8,128)(2,1)S(1)}, bf16[80,128]{1,0:T(8,128)(2,1)S(1)}, u32[]{:S(2)}, u32[]{:S(2)}) collective-permute-start(bf16[80,128]{1,0:T(8,128)(2,1)S(1)} %get-tuple-element.47.refs_4_), channel_id=1, source_target_pairs={{0,3},{1,2},{2,1},{3,0},{4,7},{5,6},{6,5},{7,4},{8,11},{9,10},{10,... | collective-permute-start | bytes 61448 | tf_op jit(solution)/shard_map/ppermute | solution.py:335
  56.9 0.4 collective-permute-start.17
  57.3 1.2 %collective-permute-start.16 = (bf16[80,128]{1,0:T(8,128)(2,1)S(1)}, bf16[80,128]{1,0:T(8,128)(2,1)S(1)}, u32[]{:S(2)}, u32[]{:S(2)}) collective-permute-start(bf16[80,128]{1,0:T(8,128)(2,1)S(1)} %get-tuple-element.47.refs_4_), channel_id=1, source_target_pairs={{0,1},{1,0},{2,3},{3,2},{4,5},{5,4},{6,7},{7,6},{8,9},{9,8},{10,11... | collective-permute-start | bytes 61448 | tf_op jit(solution)/shard_map/ppermute | solution.py:335
  58.6 1.2 %collective-permute-done.18.refs_7_ = bf16[80,128]{1,0:T(8,128)(2,1)S(1)} collective-permute-done((bf16[80,128]{1,0:T(8,128)(2,1)S(1)}, bf16[80,128]{1,0:T(8,128)(2,1)S(1)}, u32[]{:S(2)}, u32[]{:S(2)}) %collective-permute-start.18) | collective-permute-done | bytes 20512 | tf_op jit(solution)/shard_map/ppermute | solution.py:335
  59.8 0.9 %collective-permute-done.17.refs_6_ = bf16[80,128]{1,0:T(8,128)(2,1)S(1)} collective-permute-done((bf16[80,128]{1,0:T(8,128)(2,1)S(1)}, bf16[80,128]{1,0:T(8,128)(2,1)S(1)}, u32[]{:S(2)}, u32[]{:S(2)}) %collective-permute-start.17) | collective-permute-done | bytes 20512 | tf_op jit(solution)/shard_map/ppermute | solution.py:335
  60.7 0.4 collective-permute-done.16.refs_5_
  61.1 1.3 %unpack.1 = (f32[512,512]{1,0:T(8,128)}, f32[512,512]{1,0:T(8,128)}) custom-call(s32[1]{0:T(128)} %bitcast.run_ref, s32[1]{0:T(128)} %bitcast.1.grp_ref, bf16[1024,128]{1,0:T(8,128)(2,1)S(1)} %shard_map.90.half_in_ref, bf16[496,128]{1,0:T(8,128)(2,1)S(1)} %shard_map.89.refs_0_, bf16[496,128]{1,0:T(8,128)(2,1)S(1)} %collective-permute-done.12.refs_1_, ...), custom_call_target="tpu_custom_call" | custom-call | tf_op jit(solution)/shard_map/unpack/pallas_call | solution.py:473
  62.4 0.0 collective-permute-done.15.refs_0_
  62.4 0.8 %place.1 = f32[512,512]{1,0:T(8,128)} custom-call(s32[1]{0:T(128)} %bitcast.run_ref, s32[1]{0:T(128)} %bitcast.1.grp_ref, bf16[1024,128]{1,0:T(8,128)(2,1)S(1)} %collective-permute-done.15.refs_0_, f32[512,512]{1,0:T(8,128)} %get-tuple-element.48.refs_1_), custom_call_target="tpu_custom_call", output_to_operand_aliasing={{}: (3, {})} | custom-call | tf_op jit(solution)/shard_map/place/pallas_call | solution.py:487
  (10 shorter events, 0.1 us)
Async XLA Ops:
  0.6 13.6 %collective-permute-start.1 = (bf16[256,512]{1,0:T(8,128)(2,1)}, bf16[256,512]{1,0:T(8,128)(2,1)S(1)}, u32[]{:S(2)}, u32[]{:S(2)}) collective-permute-start(bf16[256,512]{1,0:T(8,128)(2,1)} %bitcast.12), channel_id=1, source_target_pairs={{1,2},{3,4},{5,6},{7,8},{9,10},{11,12},{13,14},{15,0},{2,1},{4,3},... | collective-permute-start | bytes 786440 | tf_op jit(solution)/shard_map/ppermute | solution.py:364
  7.7 9.4 %collective-permute-start = (bf16[256,512]{1,0:T(8,128)(2,1)}, bf16[256,512]{1,0:T(8,128)(2,1)S(1)}, u32[]{:S(2)}, u32[]{:S(2)}) collective-permute-start(bf16[256,512]{1,0:T(8,128)(2,1)} %bitcast.13), channel_id=1, source_target_pairs={{0,1},{2,3},{4,5},{6,7},{8,9},{10,11},{12,13},{14,15},{1,0},{3,2},... | collective-permute-start | bytes 786440 | tf_op jit(solution)/shard_map/ppermute | solution.py:365
  7.7 2.5 %copy-start.2 = (bf16[1,256,512]{2,1,0:T(8,128)(2,1)S(1)}, bf16[1,256,512]{2,1,0:T(8,128)(2,1)}, u32[]{:S(2)}) copy-start(bf16[1,256,512]{2,1,0:T(8,128)(2,1)} %param.8) | copy-start | bytes 786436
  10.1 0.7 %copy-start.3 = (s32[1,2,4]{2,1,0:T(2,128)S(1)}, s32[1,2,4]{2,1,0:T(2,128)}, u32[]{:S(2)}) copy-start(s32[1,2,4]{2,1,0:T(2,128)} %param.10) | copy-start | bytes 100
  10.1 0.7 %copy-start.4 = (s32[1,2]{1,0:T(1,128)S(1)}, s32[1,2]{1,0:T(1,128)}, u32[]{:S(2)}) copy-start(s32[1,2]{1,0:T(1,128)} %live_ref.1) | copy-start | bytes 28
  10.8 6.2 %copy-start = (bf16[1,256,512]{2,1,0:T(8,128)(2,1)S(1)}, bf16[1,256,512]{2,1,0:T(8,128)(2,1)}, u32[]{:S(2)}) copy-start(bf16[1,256,512]{2,1,0:T(8,128)(2,1)} %param.7) | copy-start | bytes 786436
  10.8 6.2 %copy-start.1 = (bf16[512,512]{1,0:T(8,128)(2,1)S(1)}, bf16[512,512]{1,0:T(8,128)(2,1)}, u32[]{:S(2)}) copy-start(bf16[512,512]{1,0:T(8,128)(2,1)} %w_ref.1) | copy-start | bytes 1572868
  19.0 11.2 %collective-permute-start.2 = (bf16[256,512]{1,0:T(8,128)(2,1)S(1)}, bf16[256,512]{1,0:T(8,128)(2,1)S(1)}, u32[]{:S(2)}, u32[]{:S(2)}) collective-permute-start(bf16[256,512]{1,0:T(8,128)(2,1)S(1)} %bitcast.17), channel_id=1, source_target_pairs={{0,16},{16,0},{1,17},{17,1},{2,18},{18,2},{3,19},{19,3},{4,20},{20... | collective-permute-start | bytes 786440 | tf_op jit(solution)/shard_map/ppermute | solution.py:433
  19.1 4.9 %collective-permute-start.3 = (bf16[320,128]{1,0:T(8,128)(2,1)S(1)}, bf16[320,128]{1,0:T(8,128)(2,1)S(1)}, u32[]{:S(2)}, u32[]{:S(2)}) collective-permute-start(bf16[320,128]{1,0:T(8,128)(2,1)S(1)} %get-tuple-element.39), channel_id=1, source_target_pairs={{0,4},{1,5},{2,6},{3,7},{4,0},{5,1},{6,2},{7,3},{8,12},{9,13},{10,... | collective-permute-start | bytes 245768 | tf_op jit(solution)/shard_map/ppermute | solution.py:335
  20.7 9.5 %collective-permute-start.4 = (bf16[320,128]{1,0:T(8,128)(2,1)S(1)}, bf16[320,128]{1,0:T(8,128)(2,1)S(1)}, u32[]{:S(2)}, u32[]{:S(2)}) collective-permute-start(bf16[320,128]{1,0:T(8,128)(2,1)S(1)} %get-tuple-element.40), channel_id=1, source_target_pairs={{0,8},{1,9},{2,10},{3,11},{4,12},{5,13},{6,14},{7,15},{8,0},{9,1},... | collective-permute-start | bytes 245768 | tf_op jit(solution)/shard_map/ppermute | solution.py:335
  23.3 6.9 %collective-permute-start.5 = (bf16[320,128]{1,0:T(8,128)(2,1)S(1)}, bf16[320,128]{1,0:T(8,128)(2,1)S(1)}, u32[]{:S(2)}, u32[]{:S(2)}) collective-permute-start(bf16[320,128]{1,0:T(8,128)(2,1)S(1)} %get-tuple-element.41), channel_id=1, source_target_pairs={{0,12},{1,13},{2,14},{3,15},{4,8},{5,9},{6,10},{7,11},{8,4},{9,5},... | collective-permute-start | bytes 245768 | tf_op jit(solution)/shard_map/ppermute | solution.py:335
  30.4 5.4 %collective-permute-start.6 = (bf16[336,128]{1,0:T(8,128)(2,1)S(1)}, bf16[336,128]{1,0:T(8,128)(2,1)S(1)}, u32[]{:S(2)}, u32[]{:S(2)}) collective-permute-start(bf16[336,128]{1,0:T(8,128)(2,1)S(1)} %get-tuple-element.43), channel_id=1, source_target_pairs={{0,1},{1,0},{2,3},{3,2},{4,5},{5,4},{6,7},{7,6},{8,9},{9,8},{10,11... | collective-permute-start | bytes 258056 | tf_op jit(solution)/shard_map/ppermute | solution.py:335
  32.3 4.5 %collective-permute-start.7 = (bf16[336,128]{1,0:T(8,128)(2,1)S(1)}, bf16[336,128]{1,0:T(8,128)(2,1)S(1)}, u32[]{:S(2)}, u32[]{:S(2)}) collective-permute-start(bf16[336,128]{1,0:T(8,128)(2,1)S(1)} %get-tuple-element.44), channel_id=1, source_target_pairs={{0,2},{1,3},{2,0},{3,1},{4,6},{5,7},{6,4},{7,5},{8,10},{9,11},{10,... | collective-permute-start | bytes 258056 | tf_op jit(solution)/shard_map/ppermute | solution.py:335
  32.4 5.4 %collective-permute-start.8 = (bf16[336,128]{1,0:T(8,128)(2,1)S(1)}, bf16[336,128]{1,0:T(8,128)(2,1)S(1)}, u32[]{:S(2)}, u32[]{:S(2)}) collective-permute-start(bf16[336,128]{1,0:T(8,128)(2,1)S(1)} %get-tuple-element.45), channel_id=1, source_target_pairs={{0,3},{1,2},{2,1},{3,0},{4,7},{5,6},{6,5},{7,4},{8,11},{9,10},{10,... | collective-permute-start | bytes 258056 | tf_op jit(solution)/shard_map/ppermute | solution.py:335
  37.9 7.2 %collective-permute-start.11 = (bf16[336,128]{1,0:T(8,128)(2,1)S(1)}, bf16[336,128]{1,0:T(8,128)(2,1)S(1)}, u32[]{:S(2)}, u32[]{:S(2)}) collective-permute-start(bf16[336,128]{1,0:T(8,128)(2,1)S(1)} %get-tuple-element.46.refs_0_), channel_id=1, source_target_pairs={{0,12},{1,13},{2,14},{3,15},{4,8},{5,9},{6,10},{7,11},{8,4},{9,5},... | collective-permute-start | bytes 258056 | tf_op jit(solution)/shard_map/ppermute | solution.py:335
  40.7 6.3 %collective-permute-start.10 = (bf16[336,128]{1,0:T(8,128)(2,1)S(1)}, bf16[336,128]{1,0:T(8,128)(2,1)S(1)}, u32[]{:S(2)}, u32[]{:S(2)}) collective-permute-start(bf16[336,128]{1,0:T(8,128)(2,1)S(1)} %get-tuple-element.46.refs_0_), channel_id=1, source_target_pairs={{0,8},{1,9},{2,10},{3,11},{4,12},{5,13},{6,14},{7,15},{8,0},{9,1},... | collective-permute-start | bytes 258056 | tf_op jit(solution)/shard_map/ppermute | solution.py:335
  41.5 5.5 %collective-permute-start.9 = (bf16[336,128]{1,0:T(8,128)(2,1)S(1)}, bf16[336,128]{1,0:T(8,128)(2,1)S(1)}, u32[]{:S(2)}, u32[]{:S(2)}) collective-permute-start(bf16[336,128]{1,0:T(8,128)(2,1)S(1)} %get-tuple-element.46.refs_0_), channel_id=1, source_target_pairs={{0,4},{1,5},{2,6},{3,7},{4,0},{5,1},{6,2},{7,3},{8,12},{9,13},{10,... | collective-permute-start | bytes 258056 | tf_op jit(solution)/shard_map/ppermute | solution.py:335
  47.0 6.0 %collective-permute-start.14 = (bf16[496,128]{1,0:T(8,128)(2,1)S(1)}, bf16[496,128]{1,0:T(8,128)(2,1)S(1)}, u32[]{:S(2)}, u32[]{:S(2)}) collective-permute-start(bf16[496,128]{1,0:T(8,128)(2,1)S(1)} %shard_map.89.refs_0_), channel_id=1, source_target_pairs={{0,3},{1,2},{2,1},{3,0},{4,7},{5,6},{6,5},{7,4},{8,11},{9,10},{10,... | collective-permute-start | bytes 380936 | tf_op jit(solution)/shard_map/ppermute | solution.py:335
  48.6 5.7 %collective-permute-start.13 = (bf16[496,128]{1,0:T(8,128)(2,1)S(1)}, bf16[496,128]{1,0:T(8,128)(2,1)S(1)}, u32[]{:S(2)}, u32[]{:S(2)}) collective-permute-start(bf16[496,128]{1,0:T(8,128)(2,1)S(1)} %shard_map.89.refs_0_), channel_id=1, source_target_pairs={{0,2},{1,3},{2,0},{3,1},{4,6},{5,7},{6,4},{7,5},{8,10},{9,11},{10,... | collective-permute-start | bytes 380936 | tf_op jit(solution)/shard_map/ppermute | solution.py:335
  50.0 4.9 %collective-permute-start.12 = (bf16[496,128]{1,0:T(8,128)(2,1)S(1)}, bf16[496,128]{1,0:T(8,128)(2,1)S(1)}, u32[]{:S(2)}, u32[]{:S(2)}) collective-permute-start(bf16[496,128]{1,0:T(8,128)(2,1)S(1)} %shard_map.89.refs_0_), channel_id=1, source_target_pairs={{0,1},{1,0},{2,3},{3,2},{4,5},{5,4},{6,7},{7,6},{8,9},{9,8},{10,11... | collective-permute-start | bytes 380936 | tf_op jit(solution)/shard_map/ppermute | solution.py:335
  54.9 7.5 %collective-permute-start.15 = (bf16[1024,128]{1,0:T(8,128)(2,1)S(1)}, bf16[1024,128]{1,0:T(8,128)(2,1)S(1)}, u32[]{:S(2)}, u32[]{:S(2)}) collective-permute-start(bf16[1024,128]{1,0:T(8,128)(2,1)S(1)} %shard_map.90.half_in_ref), channel_id=1, source_target_pairs={{0,16},{16,0},{1,17},{17,1},{2,18},{18,2},{3,19},{19,3},{4,20},{20... | collective-permute-start | bytes 786440 | tf_op jit(solution)/shard_map/ppermute | solution.py:469
  55.0 4.8 %collective-permute-start.18 = (bf16[80,128]{1,0:T(8,128)(2,1)S(1)}, bf16[80,128]{1,0:T(8,128)(2,1)S(1)}, u32[]{:S(2)}, u32[]{:S(2)}) collective-permute-start(bf16[80,128]{1,0:T(8,128)(2,1)S(1)} %get-tuple-element.47.refs_4_), channel_id=1, source_target_pairs={{0,3},{1,2},{2,1},{3,0},{4,7},{5,6},{6,5},{7,4},{8,11},{9,10},{10,... | collective-permute-start | bytes 61448 | tf_op jit(solution)/shard_map/ppermute | solution.py:335
  56.9 3.8 %collective-permute-start.17 = (bf16[80,128]{1,0:T(8,128)(2,1)S(1)}, bf16[80,128]{1,0:T(8,128)(2,1)S(1)}, u32[]{:S(2)}, u32[]{:S(2)}) collective-permute-start(bf16[80,128]{1,0:T(8,128)(2,1)S(1)} %get-tuple-element.47.refs_4_), channel_id=1, source_target_pairs={{0,2},{1,3},{2,0},{3,1},{4,6},{5,7},{6,4},{7,5},{8,10},{9,11},{10,... | collective-permute-start | bytes 61448 | tf_op jit(solution)/shard_map/ppermute | solution.py:335
  57.3 3.8 %collective-permute-start.16 = (bf16[80,128]{1,0:T(8,128)(2,1)S(1)}, bf16[80,128]{1,0:T(8,128)(2,1)S(1)}, u32[]{:S(2)}, u32[]{:S(2)}) collective-permute-start(bf16[80,128]{1,0:T(8,128)(2,1)S(1)} %get-tuple-element.47.refs_4_), channel_id=1, source_target_pairs={{0,1},{1,0},{2,3},{3,2},{4,5},{5,4},{6,7},{7,6},{8,9},{9,8},{10,11... | collective-permute-start | bytes 61448 | tf_op jit(solution)/shard_map/ppermute | solution.py:335

commit v8 on v7

--- a/solution.py
+++ b/solution.py
@@ -344,7 +344,7 @@
         in_specs=specs,
         out_specs=(vmem,) * len(shapes) if many else vmem,
         scratch_shapes=scratch,
-        compiler_params=room(16),
+        compiler_params=room(8),
     )
 
 
@@ -396,7 +396,7 @@
             pltpu.VMEM((far * column_rows, lane), bf16),
             pltpu.SemaphoreType.DMA((5,)),
         ],
-        compiler_params=room(16),
+        compiler_params=room(8),
         name="moment",
     )(run_id, *far_away)
     pieces = [pieces[0]] + [swap(pieces[k], k * near, runs) for k in range(1, far)]
@@ -410,7 +410,7 @@
         in_specs=[smem] * 3 + [vmem] * 6,
         out_specs=(vmem,) * 3,
         scratch_shapes=[pltpu.VMEM((points, (2 * reach + 1) * points + block), f32)],
-        compiler_params=room(16 + 4 * reach),
+        compiler_params=room(8 + 4 * reach),
         name="own",
     )(
         run_id, match_blocks[0], match_count, xt, unit, tgt_unit, tgt_inv, sources, targets
@@ -426,7 +426,7 @@
         in_specs=[smem] + [vmem] * (7 + 2 * reach),
         out_specs=(vmem,) * 3,
         scratch_shapes=total,
-        compiler_params=room(16 + 4 * reach),
+        compiler_params=room(8 + 4 * reach),
         name="halo",
     )(grp_id, proj_weight, unit, inv, counts, grad, part, xs, *even, *odd)
     got = [
@@ -481,7 +481,7 @@
             pltpu.VMEM((chunk, width), f32),
             pltpu.SemaphoreType.DMA((1 + tiles,)),
         ],
-        compiler_params=room(16),
+        compiler_params=room(8),
         name="unpack",
     )(run_id, grp_id, half, *columns, *sides)
     weight_grad = pl.pallas_call(
@@ -494,7 +494,7 @@
             pltpu.SemaphoreType.DMA((groups - 1,)),
         ],
         input_output_aliases={1 + groups: 0},
-        compiler_params=room(16),
+        compiler_params=room(8),
         name="place",
     )(run_id, grp_id, *halves[1:], own_rows)
     return (weight_grad, covariance[None])

time: 63.4 us -> 63.4 us (level)
  no operation moved by 1% of the time
where the time goes in v8:
time: 63.4 us; the launch traced here: 63.3 us
  starting transfers between devices  26.7 us (42%)
  waiting for transfers between devices  26 us (41%)
  Pallas kernels  9.06 us (14%)
  between operations  0.75 us (1%)
  local copies, waits for them, and re-layouts  0.67 us (1%)
    ppermute x15, waiting for transfers between devices, swap(): return lax.ppermute(array, 'blk', [(i, i ^ bits) for i in range(runs)])  21.7 us
    ppermute x15, starting transfers between devices, swap(): return lax.ppermute(array, 'blk', [(i, i ^ bits) for i in range(runs)])  19.6 us
    ppermute x1, starting transfers between devices, body(): odd = [lax.ppermute(xt, 'blk', partners(k, 1, runs)) for k in hops]  7.02 us
    ppermute x1, waiting for transfers between devices, body(): even = [lax.ppermute(xt, 'blk', partners(k, 0, runs)) for k in hops]  2.74 us
    pallas_call x1, Pallas kernels, body(): pl.pallas_call(functools.partial(moment_kernel, far, near, scale), out_sh...  2.45 us
    pallas_call x1, Pallas kernels, body(): pl.pallas_call(functools.partial(halo_kernel, block, groups), out_shape=(...  1.99 us
    pallas_call x1, Pallas kernels, body(): pl.pallas_call(functools.partial(own_kernel, runs, reach), out_shape=(jax...  1.86 us
    ppermute x1, waiting for transfers between devices, body(): odd = [lax.ppermute(xt, 'blk', partners(k, 1, runs)) for k in hops]  1.6 us
  transfers between devices with their start and end apart: 19, of which 14 were waited for; matrix products, arithmetic and copies ran while one was open for 0% of the time, Pallas kernels for 9%

profile of v8, /device:TPU:0, one launch (start us, length us, event | category | flops | bytes accessed | tf_op | source)
XLA Modules:
  0.0 63.3 jit_solution(7434541067337547872)
XLA Ops:
  0.6 7.0 %collective-permute-start.1 = (bf16[256,512]{1,0:T(8,128)(2,1)}, bf16[256,512]{1,0:T(8,128)(2,1)S(1)}, u32[]{:S(2)}, u32[]{:S(2)}) collective-permute-start(bf16[256,512]{1,0:T(8,128)(2,1)} %bitcast.12), channel_id=1, source_target_pairs={{1,2},{3,4},{5,6},{7,8},{9,10},{11,12},{13,14},{15,0},{2,1},{4,3},... | collective-permute-start | bytes 786440 | tf_op jit(solution)/shard_map/ppermute | solution.py:364
  7.7 0.0 collective-permute-start
  7.7 2.5 %moment.1 = (bf16[320,128]{1,0:T(8,128)(2,1)S(1)}, bf16[320,128]{1,0:T(8,128)(2,1)S(1)}, bf16[320,128]{1,0:T(8,128)(2,1)S(1)}, bf16[320,128]{1,0:T(8,128)(2,1)S(...) custom-call(s32[1]{0:T(128)} %bitcast.run_ref, ...), custom_call_target="tpu_custom_call" | custom-call | tf_op jit(solution)/shard_map/moment/pallas_call | solution.py:384
  10.1 0.0 copy-start.3
  10.1 0.0 copy-start.4
  10.2 0.6 %copy-done.3 = s32[1,2,4]{2,1,0:T(2,128)S(1)} copy-done((s32[1,2,4]{2,1,0:T(2,128)S(1)}, s32[1,2,4]{2,1,0:T(2,128)}, u32[]{:S(2)}) %copy-start.3) | copy-done | bytes 56
  10.8 1.9 %own.1 = (bf16[256,512]{1,0:T(8,128)(2,1)S(1)}, f32[256,512]{1,0:T(8,128)S(1)}, f32[512,512]{1,0:T(8,128)S(1)}) custom-call(s32[1]{0:T(128)} %bitcast.run_ref, s32[2,4]{1,0:T(2,128)S(1)} %bitcast.16, s32[1,2]{1,0:T(1,128)S(1)} %copy-done.4, bf16[256,512]{1,0:T(8,128)(2,1)S(1)} %bitcast.15, f32[256,512]{1,0:T(8,128)S(1)} %get-tuple-element.26.src_unit_ref.unit_ref, ...), custom_call_target="tpu_custom_call" | custom-call | tf_op jit(solution)/shard_map/own/pallas_call | solution.py:403
  12.7 1.6 %collective-permute-done.1.refs_1_.refs_2_ = bf16[256,512]{1,0:T(8,128)(2,1)S(1)} collective-permute-done((bf16[256,512]{1,0:T(8,128)(2,1)}, bf16[256,512]{1,0:T(8,128)(2,1)S(1)}, u32[]{:S(2)}, u32[]{:S(2)}) %collective-permute-start.1) | collective-permute-done | bytes 262176 | tf_op jit(solution)/shard_map/ppermute | solution.py:364
  14.3 2.7 %collective-permute-done.refs_0_.refs_1_ = bf16[256,512]{1,0:T(8,128)(2,1)S(1)} collective-permute-done((bf16[256,512]{1,0:T(8,128)(2,1)}, bf16[256,512]{1,0:T(8,128)(2,1)S(1)}, u32[]{:S(2)}, u32[]{:S(2)}) %collective-permute-start) | collective-permute-done | bytes 262176 | tf_op jit(solution)/shard_map/ppermute | solution.py:365
  17.0 2.0 %halo.1 = (bf16[1,256,512]{2,1,0:T(8,128)(2,1)S(1)}, bf16[256,512]{1,0:T(8,128)(2,1)S(1)}, bf16[512,512]{1,0:T(8,128)(2,1)S(1)}) custom-call(s32[1]{0:T(128)} %bitcast.1.grp_ref, bf16[512,512]{1,0:T(8,128)(2,1)S(1)} %copy-done.1, f32[256,512]{1,0:T(8,128)S(1)} %get-tuple-element.26.src_unit_ref.unit_ref, f32[256,128]{1,0:T(8,128)S(1)} %get-tuple-element.32.inv_ref, ...), custom_call_target="tpu_custom_call" | custom-call | tf_op jit(solution)/shard_map/halo/pallas_call | solution.py:419
  19.0 0.1 collective-permute-start.2
  19.1 1.6 %collective-permute-start.3 = (bf16[320,128]{1,0:T(8,128)(2,1)S(1)}, bf16[320,128]{1,0:T(8,128)(2,1)S(1)}, u32[]{:S(2)}, u32[]{:S(2)}) collective-permute-start(bf16[320,128]{1,0:T(8,128)(2,1)S(1)} %get-tuple-element.39), channel_id=1, source_target_pairs={{0,4},{1,5},{2,6},{3,7},{4,0},{5,1},{6,2},{7,3},{8,12},{9,13},{10,... | collective-permute-start | bytes 245768 | tf_op jit(solution)/shard_map/ppermute | solution.py:335
  20.7 2.6 %collective-permute-start.4 = (bf16[320,128]{1,0:T(8,128)(2,1)S(1)}, bf16[320,128]{1,0:T(8,128)(2,1)S(1)}, u32[]{:S(2)}, u32[]{:S(2)}) collective-permute-start(bf16[320,128]{1,0:T(8,128)(2,1)S(1)} %get-tuple-element.40), channel_id=1, source_target_pairs={{0,8},{1,9},{2,10},{3,11},{4,12},{5,13},{6,14},{7,15},{8,0},{9,1},... | collective-permute-start | bytes 245768 | tf_op jit(solution)/shard_map/ppermute | solution.py:335
  23.3 0.2 collective-permute-start.5
  23.6 0.4 shard_map.86.refs_0_
  24.0 0.0 collective-permute-done.3.refs_3_
  24.0 6.2 %collective-permute-done.4.refs_4_ = bf16[320,128]{1,0:T(8,128)(2,1)S(1)} collective-permute-done((bf16[320,128]{1,0:T(8,128)(2,1)S(1)}, bf16[320,128]{1,0:T(8,128)(2,1)S(1)}, u32[]{:S(2)}, u32[]{:S(2)}) %collective-permute-start.4) | collective-permute-done | bytes 81952 | tf_op jit(solution)/shard_map/ppermute | solution.py:335
  30.2 0.0 collective-permute-done.5.refs_5_
  30.2 0.0 collective-permute-done.2.refs_1_
  30.2 0.1 shard_map.87
  30.4 1.9 %collective-permute-start.6 = (bf16[336,128]{1,0:T(8,128)(2,1)S(1)}, bf16[336,128]{1,0:T(8,128)(2,1)S(1)}, u32[]{:S(2)}, u32[]{:S(2)}) collective-permute-start(bf16[336,128]{1,0:T(8,128)(2,1)S(1)} %get-tuple-element.43), channel_id=1, source_target_pairs={{0,1},{1,0},{2,3},{3,2},{4,5},{5,4},{6,7},{7,6},{8,9},{9,8},{10,11... | collective-permute-start | bytes 258056 | tf_op jit(solution)/shard_map/ppermute | solution.py:335
  32.3 0.2 collective-permute-start.7
  32.4 1.5 %collective-permute-start.8 = (bf16[336,128]{1,0:T(8,128)(2,1)S(1)}, bf16[336,128]{1,0:T(8,128)(2,1)S(1)}, u32[]{:S(2)}, u32[]{:S(2)}) collective-permute-start(bf16[336,128]{1,0:T(8,128)(2,1)S(1)} %get-tuple-element.45), channel_id=1, source_target_pairs={{0,3},{1,2},{2,1},{3,0},{4,7},{5,6},{6,5},{7,4},{8,11},{9,10},{10,... | collective-permute-start | bytes 258056 | tf_op jit(solution)/shard_map/ppermute | solution.py:335
  33.9 1.9 %collective-permute-done.6.refs_1_ = bf16[336,128]{1,0:T(8,128)(2,1)S(1)} collective-permute-done((bf16[336,128]{1,0:T(8,128)(2,1)S(1)}, bf16[336,128]{1,0:T(8,128)(2,1)S(1)}, u32[]{:S(2)}, u32[]{:S(2)}) %collective-permute-start.6) | collective-permute-done | bytes 86048 | tf_op jit(solution)/shard_map/ppermute | solution.py:335
  35.8 0.9 %collective-permute-done.7.refs_2_ = bf16[336,128]{1,0:T(8,128)(2,1)S(1)} collective-permute-done((bf16[336,128]{1,0:T(8,128)(2,1)S(1)}, bf16[336,128]{1,0:T(8,128)(2,1)S(1)}, u32[]{:S(2)}, u32[]{:S(2)}) %collective-permute-start.7) | collective-permute-done | bytes 86048 | tf_op jit(solution)/shard_map/ppermute | solution.py:335
  36.8 1.1 %collective-permute-done.8.refs_3_ = bf16[336,128]{1,0:T(8,128)(2,1)S(1)} collective-permute-done((bf16[336,128]{1,0:T(8,128)(2,1)S(1)}, bf16[336,128]{1,0:T(8,128)(2,1)S(1)}, u32[]{:S(2)}, u32[]{:S(2)}) %collective-permute-start.8) | collective-permute-done | bytes 86048 | tf_op jit(solution)/shard_map/ppermute | solution.py:335
  37.9 2.8 %collective-permute-start.11 = (bf16[336,128]{1,0:T(8,128)(2,1)S(1)}, bf16[336,128]{1,0:T(8,128)(2,1)S(1)}, u32[]{:S(2)}, u32[]{:S(2)}) collective-permute-start(bf16[336,128]{1,0:T(8,128)(2,1)S(1)} %get-tuple-element.46.refs_0_), channel_id=1, source_target_pairs={{0,12},{1,13},{2,14},{3,15},{4,8},{5,9},{6,10},{7,11},{8,4},{9,5},... | collective-permute-start | bytes 258056 | tf_op jit(solution)/shard_map/ppermute | solution.py:335
  40.7 0.8 %collective-permute-start.10 = (bf16[336,128]{1,0:T(8,128)(2,1)S(1)}, bf16[336,128]{1,0:T(8,128)(2,1)S(1)}, u32[]{:S(2)}, u32[]{:S(2)}) collective-permute-start(bf16[336,128]{1,0:T(8,128)(2,1)S(1)} %get-tuple-element.46.refs_0_), channel_id=1, source_target_pairs={{0,8},{1,9},{2,10},{3,11},{4,12},{5,13},{6,14},{7,15},{8,0},{9,1},... | collective-permute-start | bytes 258056 | tf_op jit(solution)/shard_map/ppermute | solution.py:335
  41.5 0.9 %collective-permute-start.9 = (bf16[336,128]{1,0:T(8,128)(2,1)S(1)}, bf16[336,128]{1,0:T(8,128)(2,1)S(1)}, u32[]{:S(2)}, u32[]{:S(2)}) collective-permute-start(bf16[336,128]{1,0:T(8,128)(2,1)S(1)} %get-tuple-element.46.refs_0_), channel_id=1, source_target_pairs={{0,4},{1,5},{2,6},{3,7},{4,0},{5,1},{6,2},{7,3},{8,12},{9,13},{10,... | collective-permute-start | bytes 258056 | tf_op jit(solution)/shard_map/ppermute | solution.py:335
  42.3 2.7 %collective-permute-done.11.refs_3_ = bf16[336,128]{1,0:T(8,128)(2,1)S(1)} collective-permute-done((bf16[336,128]{1,0:T(8,128)(2,1)S(1)}, bf16[336,128]{1,0:T(8,128)(2,1)S(1)}, u32[]{:S(2)}, u32[]{:S(2)}) %collective-permute-start.11) | collective-permute-done | bytes 86048 | tf_op jit(solution)/shard_map/ppermute | solution.py:335
  45.0 1.9 %collective-permute-done.10.refs_2_ = bf16[336,128]{1,0:T(8,128)(2,1)S(1)} collective-permute-done((bf16[336,128]{1,0:T(8,128)(2,1)S(1)}, bf16[336,128]{1,0:T(8,128)(2,1)S(1)}, u32[]{:S(2)}, u32[]{:S(2)}) %collective-permute-start.10) | collective-permute-done | bytes 86048 | tf_op jit(solution)/shard_map/ppermute | solution.py:335
  47.0 0.0 collective-permute-done.9.refs_1_
  47.0 1.6 %collective-permute-start.14 = (bf16[496,128]{1,0:T(8,128)(2,1)S(1)}, bf16[496,128]{1,0:T(8,128)(2,1)S(1)}, u32[]{:S(2)}, u32[]{:S(2)}) collective-permute-start(bf16[496,128]{1,0:T(8,128)(2,1)S(1)} %shard_map.89.refs_0_), channel_id=1, source_target_pairs={{0,3},{1,2},{2,1},{3,0},{4,7},{5,6},{6,5},{7,4},{8,11},{9,10},{10,... | collective-permute-start | bytes 380936 | tf_op jit(solution)/shard_map/ppermute | solution.py:335
  48.6 1.4 %collective-permute-start.13 = (bf16[496,128]{1,0:T(8,128)(2,1)S(1)}, bf16[496,128]{1,0:T(8,128)(2,1)S(1)}, u32[]{:S(2)}, u32[]{:S(2)}) collective-permute-start(bf16[496,128]{1,0:T(8,128)(2,1)S(1)} %shard_map.89.refs_0_), channel_id=1, source_target_pairs={{0,2},{1,3},{2,0},{3,1},{4,6},{5,7},{6,4},{7,5},{8,10},{9,11},{10,... | collective-permute-start | bytes 380936 | tf_op jit(solution)/shard_map/ppermute | solution.py:335
  50.0 0.6 collective-permute-start.12
  50.6 2.4 %collective-permute-done.14.refs_3_ = bf16[496,128]{1,0:T(8,128)(2,1)S(1)} collective-permute-done((bf16[496,128]{1,0:T(8,128)(2,1)S(1)}, bf16[496,128]{1,0:T(8,128)(2,1)S(1)}, u32[]{:S(2)}, u32[]{:S(2)}) %collective-permute-start.14) | collective-permute-done | bytes 127008 | tf_op jit(solution)/shard_map/ppermute | solution.py:335
  53.0 1.3 %collective-permute-done.13.refs_2_ = bf16[496,128]{1,0:T(8,128)(2,1)S(1)} collective-permute-done((bf16[496,128]{1,0:T(8,128)(2,1)S(1)}, bf16[496,128]{1,0:T(8,128)(2,1)S(1)}, u32[]{:S(2)}, u32[]{:S(2)}) %collective-permute-start.13) | collective-permute-done | bytes 127008 | tf_op jit(solution)/shard_map/ppermute | solution.py:335
  54.3 0.6 %collective-permute-done.12.refs_1_ = bf16[496,128]{1,0:T(8,128)(2,1)S(1)} collective-permute-done((bf16[496,128]{1,0:T(8,128)(2,1)S(1)}, bf16[496,128]{1,0:T(8,128)(2,1)S(1)}, u32[]{:S(2)}, u32[]{:S(2)}) %collective-permute-start.12) | collective-permute-done | bytes 127008 | tf_op jit(solution)/shard_map/ppermute | solution.py:335
  54.9 0.1 collective-permute-start.15
  55.0 1.9 %collective-permute-start.18 = (bf16[80,128]{1,0:T(8,128)(2,1)S(1)}, bf16[80,128]{1,0:T(8,128)(2,1)S(1)}, u32[]{:S(2)}, u32[]{:S(2)}) collective-permute-start(bf16[80,128]{1,0:T(8,128)(2,1)S(1)} %get-tuple-element.47.refs_4_), channel_id=1, source_target_pairs={{0,3},{1,2},{2,1},{3,0},{4,7},{5,6},{6,5},{7,4},{8,11},{9,10},{10,... | collective-permute-start | bytes 61448 | tf_op jit(solution)/shard_map/ppermute | solution.py:335
  56.9 0.4 collective-permute-start.17
  57.3 1.2 %collective-permute-start.16 = (bf16[80,128]{1,0:T(8,128)(2,1)S(1)}, bf16[80,128]{1,0:T(8,128)(2,1)S(1)}, u32[]{:S(2)}, u32[]{:S(2)}) collective-permute-start(bf16[80,128]{1,0:T(8,128)(2,1)S(1)} %get-tuple-element.47.refs_4_), channel_id=1, source_target_pairs={{0,1},{1,0},{2,3},{3,2},{4,5},{5,4},{6,7},{7,6},{8,9},{9,8},{10,11... | collective-permute-start | bytes 61448 | tf_op jit(solution)/shard_map/ppermute | solution.py:335
  58.6 1.2 %collective-permute-done.18.refs_7_ = bf16[80,128]{1,0:T(8,128)(2,1)S(1)} collective-permute-done((bf16[80,128]{1,0:T(8,128)(2,1)S(1)}, bf16[80,128]{1,0:T(8,128)(2,1)S(1)}, u32[]{:S(2)}, u32[]{:S(2)}) %collective-permute-start.18) | collective-permute-done | bytes 20512 | tf_op jit(solution)/shard_map/ppermute | solution.py:335
  59.8 0.9 %collective-permute-done.17.refs_6_ = bf16[80,128]{1,0:T(8,128)(2,1)S(1)} collective-permute-done((bf16[80,128]{1,0:T(8,128)(2,1)S(1)}, bf16[80,128]{1,0:T(8,128)(2,1)S(1)}, u32[]{:S(2)}, u32[]{:S(2)}) %collective-permute-start.17) | collective-permute-done | bytes 20512 | tf_op jit(solution)/shard_map/ppermute | solution.py:335
  60.7 0.4 collective-permute-done.16.refs_5_
  61.1 1.3 %unpack.1 = (f32[512,512]{1,0:T(8,128)}, f32[512,512]{1,0:T(8,128)}) custom-call(s32[1]{0:T(128)} %bitcast.run_ref, s32[1]{0:T(128)} %bitcast.1.grp_ref, bf16[1024,128]{1,0:T(8,128)(2,1)S(1)} %shard_map.90.half_in_ref, bf16[496,128]{1,0:T(8,128)(2,1)S(1)} %shard_map.89.refs_0_, bf16[496,128]{1,0:T(8,128)(2,1)S(1)} %collective-permute-done.12.refs_1_, ...), custom_call_target="tpu_custom_call" | custom-call | tf_op jit(solution)/shard_map/unpack/pallas_call | solution.py:473
  62.4 0.0 collective-permute-done.15.refs_0_
  62.4 0.8 %place.1 = f32[512,512]{1,0:T(8,128)} custom-call(s32[1]{0:T(128)} %bitcast.run_ref, s32[1]{0:T(128)} %bitcast.1.grp_ref, bf16[1024,128]{1,0:T(8,128)(2,1)S(1)} %collective-permute-done.15.refs_0_, f32[512,512]{1,0:T(8,128)} %get-tuple-element.48.refs_1_), custom_call_target="tpu_custom_call", output_to_operand_aliasing={{}: (3, {})} | custom-call | tf_op jit(solution)/shard_map/place/pallas_call | solution.py:487
  (10 shorter events, 0.1 us)
Async XLA Ops:
  0.6 13.6 %collective-permute-start.1 = (bf16[256,512]{1,0:T(8,128)(2,1)}, bf16[256,512]{1,0:T(8,128)(2,1)S(1)}, u32[]{:S(2)}, u32[]{:S(2)}) collective-permute-start(bf16[256,512]{1,0:T(8,128)(2,1)} %bitcast.12), channel_id=1, source_target_pairs={{1,2},{3,4},{5,6},{7,8},{9,10},{11,12},{13,14},{15,0},{2,1},{4,3},... | collective-permute-start | bytes 786440 | tf_op jit(solution)/shard_map/ppermute | solution.py:364
  7.7 9.4 %collective-permute-start = (bf16[256,512]{1,0:T(8,128)(2,1)}, bf16[256,512]{1,0:T(8,128)(2,1)S(1)}, u32[]{:S(2)}, u32[]{:S(2)}) collective-permute-start(bf16[256,512]{1,0:T(8,128)(2,1)} %bitcast.13), channel_id=1, source_target_pairs={{0,1},{2,3},{4,5},{6,7},{8,9},{10,11},{12,13},{14,15},{1,0},{3,2},... | collective-permute-start | bytes 786440 | tf_op jit(solution)/shard_map/ppermute | solution.py:365
  7.7 2.5 %copy-start.2 = (bf16[1,256,512]{2,1,0:T(8,128)(2,1)S(1)}, bf16[1,256,512]{2,1,0:T(8,128)(2,1)}, u32[]{:S(2)}) copy-start(bf16[1,256,512]{2,1,0:T(8,128)(2,1)} %param.8) | copy-start | bytes 786436
  10.1 0.7 %copy-start.3 = (s32[1,2,4]{2,1,0:T(2,128)S(1)}, s32[1,2,4]{2,1,0:T(2,128)}, u32[]{:S(2)}) copy-start(s32[1,2,4]{2,1,0:T(2,128)} %param.10) | copy-start | bytes 100
  10.1 0.7 %copy-start.4 = (s32[1,2]{1,0:T(1,128)S(1)}, s32[1,2]{1,0:T(1,128)}, u32[]{:S(2)}) copy-start(s32[1,2]{1,0:T(1,128)} %live_ref.1) | copy-start | bytes 28
  10.8 6.2 %copy-start = (bf16[1,256,512]{2,1,0:T(8,128)(2,1)S(1)}, bf16[1,256,512]{2,1,0:T(8,128)(2,1)}, u32[]{:S(2)}) copy-start(bf16[1,256,512]{2,1,0:T(8,128)(2,1)} %param.7) | copy-start | bytes 786436
  10.8 6.2 %copy-start.1 = (bf16[512,512]{1,0:T(8,128)(2,1)S(1)}, bf16[512,512]{1,0:T(8,128)(2,1)}, u32[]{:S(2)}) copy-start(bf16[512,512]{1,0:T(8,128)(2,1)} %w_ref.1) | copy-start | bytes 1572868
  19.0 11.2 %collective-permute-start.2 = (bf16[256,512]{1,0:T(8,128)(2,1)S(1)}, bf16[256,512]{1,0:T(8,128)(2,1)S(1)}, u32[]{:S(2)}, u32[]{:S(2)}) collective-permute-start(bf16[256,512]{1,0:T(8,128)(2,1)S(1)} %bitcast.17), channel_id=1, source_target_pairs={{0,16},{16,0},{1,17},{17,1},{2,18},{18,2},{3,19},{19,3},{4,20},{20... | collective-permute-start | bytes 786440 | tf_op jit(solution)/shard_map/ppermute | solution.py:433
  19.1 4.9 %collective-permute-start.3 = (bf16[320,128]{1,0:T(8,128)(2,1)S(1)}, bf16[320,128]{1,0:T(8,128)(2,1)S(1)}, u32[]{:S(2)}, u32[]{:S(2)}) collective-permute-start(bf16[320,128]{1,0:T(8,128)(2,1)S(1)} %get-tuple-element.39), channel_id=1, source_target_pairs={{0,4},{1,5},{2,6},{3,7},{4,0},{5,1},{6,2},{7,3},{8,12},{9,13},{10,... | collective-permute-start | bytes 245768 | tf_op jit(solution)/shard_map/ppermute | solution.py:335
  20.7 9.5 %collective-permute-start.4 = (bf16[320,128]{1,0:T(8,128)(2,1)S(1)}, bf16[320,128]{1,0:T(8,128)(2,1)S(1)}, u32[]{:S(2)}, u32[]{:S(2)}) collective-permute-start(bf16[320,128]{1,0:T(8,128)(2,1)S(1)} %get-tuple-element.40), channel_id=1, source_target_pairs={{0,8},{1,9},{2,10},{3,11},{4,12},{5,13},{6,14},{7,15},{8,0},{9,1},... | collective-permute-start | bytes 245768 | tf_op jit(solution)/shard_map/ppermute | solution.py:335
  23.3 6.9 %collective-permute-start.5 = (bf16[320,128]{1,0:T(8,128)(2,1)S(1)}, bf16[320,128]{1,0:T(8,128)(2,1)S(1)}, u32[]{:S(2)}, u32[]{:S(2)}) collective-permute-start(bf16[320,128]{1,0:T(8,128)(2,1)S(1)} %get-tuple-element.41), channel_id=1, source_target_pairs={{0,12},{1,13},{2,14},{3,15},{4,8},{5,9},{6,10},{7,11},{8,4},{9,5},... | collective-permute-start | bytes 245768 | tf_op jit(solution)/shard_map/ppermute | solution.py:335
  30.4 5.4 %collective-permute-start.6 = (bf16[336,128]{1,0:T(8,128)(2,1)S(1)}, bf16[336,128]{1,0:T(8,128)(2,1)S(1)}, u32[]{:S(2)}, u32[]{:S(2)}) collective-permute-start(bf16[336,128]{1,0:T(8,128)(2,1)S(1)} %get-tuple-element.43), channel_id=1, source_target_pairs={{0,1},{1,0},{2,3},{3,2},{4,5},{5,4},{6,7},{7,6},{8,9},{9,8},{10,11... | collective-permute-start | bytes 258056 | tf_op jit(solution)/shard_map/ppermute | solution.py:335
  32.3 4.5 %collective-permute-start.7 = (bf16[336,128]{1,0:T(8,128)(2,1)S(1)}, bf16[336,128]{1,0:T(8,128)(2,1)S(1)}, u32[]{:S(2)}, u32[]{:S(2)}) collective-permute-start(bf16[336,128]{1,0:T(8,128)(2,1)S(1)} %get-tuple-element.44), channel_id=1, source_target_pairs={{0,2},{1,3},{2,0},{3,1},{4,6},{5,7},{6,4},{7,5},{8,10},{9,11},{10,... | collective-permute-start | bytes 258056 | tf_op jit(solution)/shard_map/ppermute | solution.py:335
  32.4 5.4 %collective-permute-start.8 = (bf16[336,128]{1,0:T(8,128)(2,1)S(1)}, bf16[336,128]{1,0:T(8,128)(2,1)S(1)}, u32[]{:S(2)}, u32[]{:S(2)}) collective-permute-start(bf16[336,128]{1,0:T(8,128)(2,1)S(1)} %get-tuple-element.45), channel_id=1, source_target_pairs={{0,3},{1,2},{2,1},{3,0},{4,7},{5,6},{6,5},{7,4},{8,11},{9,10},{10,... | collective-permute-start | bytes 258056 | tf_op jit(solution)/shard_map/ppermute | solution.py:335
  37.9 7.2 %collective-permute-start.11 = (bf16[336,128]{1,0:T(8,128)(2,1)S(1)}, bf16[336,128]{1,0:T(8,128)(2,1)S(1)}, u32[]{:S(2)}, u32[]{:S(2)}) collective-permute-start(bf16[336,128]{1,0:T(8,128)(2,1)S(1)} %get-tuple-element.46.refs_0_), channel_id=1, source_target_pairs={{0,12},{1,13},{2,14},{3,15},{4,8},{5,9},{6,10},{7,11},{8,4},{9,5},... | collective-permute-start | bytes 258056 | tf_op jit(solution)/shard_map/ppermute | solution.py:335
  40.7 6.3 %collective-permute-start.10 = (bf16[336,128]{1,0:T(8,128)(2,1)S(1)}, bf16[336,128]{1,0:T(8,128)(2,1)S(1)}, u32[]{:S(2)}, u32[]{:S(2)}) collective-permute-start(bf16[336,128]{1,0:T(8,128)(2,1)S(1)} %get-tuple-element.46.refs_0_), channel_id=1, source_target_pairs={{0,8},{1,9},{2,10},{3,11},{4,12},{5,13},{6,14},{7,15},{8,0},{9,1},... | collective-permute-start | bytes 258056 | tf_op jit(solution)/shard_map/ppermute | solution.py:335
  41.5 5.5 %collective-permute-start.9 = (bf16[336,128]{1,0:T(8,128)(2,1)S(1)}, bf16[336,128]{1,0:T(8,128)(2,1)S(1)}, u32[]{:S(2)}, u32[]{:S(2)}) collective-permute-start(bf16[336,128]{1,0:T(8,128)(2,1)S(1)} %get-tuple-element.46.refs_0_), channel_id=1, source_target_pairs={{0,4},{1,5},{2,6},{3,7},{4,0},{5,1},{6,2},{7,3},{8,12},{9,13},{10,... | collective-permute-start | bytes 258056 | tf_op jit(solution)/shard_map/ppermute | solution.py:335
  47.0 6.0 %collective-permute-start.14 = (bf16[496,128]{1,0:T(8,128)(2,1)S(1)}, bf16[496,128]{1,0:T(8,128)(2,1)S(1)}, u32[]{:S(2)}, u32[]{:S(2)}) collective-permute-start(bf16[496,128]{1,0:T(8,128)(2,1)S(1)} %shard_map.89.refs_0_), channel_id=1, source_target_pairs={{0,3},{1,2},{2,1},{3,0},{4,7},{5,6},{6,5},{7,4},{8,11},{9,10},{10,... | collective-permute-start | bytes 380936 | tf_op jit(solution)/shard_map/ppermute | solution.py:335
  48.6 5.7 %collective-permute-start.13 = (bf16[496,128]{1,0:T(8,128)(2,1)S(1)}, bf16[496,128]{1,0:T(8,128)(2,1)S(1)}, u32[]{:S(2)}, u32[]{:S(2)}) collective-permute-start(bf16[496,128]{1,0:T(8,128)(2,1)S(1)} %shard_map.89.refs_0_), channel_id=1, source_target_pairs={{0,2},{1,3},{2,0},{3,1},{4,6},{5,7},{6,4},{7,5},{8,10},{9,11},{10,... | collective-permute-start | bytes 380936 | tf_op jit(solution)/shard_map/ppermute | solution.py:335
  50.0 4.9 %collective-permute-start.12 = (bf16[496,128]{1,0:T(8,128)(2,1)S(1)}, bf16[496,128]{1,0:T(8,128)(2,1)S(1)}, u32[]{:S(2)}, u32[]{:S(2)}) collective-permute-start(bf16[496,128]{1,0:T(8,128)(2,1)S(1)} %shard_map.89.refs_0_), channel_id=1, source_target_pairs={{0,1},{1,0},{2,3},{3,2},{4,5},{5,4},{6,7},{7,6},{8,9},{9,8},{10,11... | collective-permute-start | bytes 380936 | tf_op jit(solution)/shard_map/ppermute | solution.py:335
  54.9 7.5 %collective-permute-start.15 = (bf16[1024,128]{1,0:T(8,128)(2,1)S(1)}, bf16[1024,128]{1,0:T(8,128)(2,1)S(1)}, u32[]{:S(2)}, u32[]{:S(2)}) collective-permute-start(bf16[1024,128]{1,0:T(8,128)(2,1)S(1)} %shard_map.90.half_in_ref), channel_id=1, source_target_pairs={{0,16},{16,0},{1,17},{17,1},{2,18},{18,2},{3,19},{19,3},{4,20},{20... | collective-permute-start | bytes 786440 | tf_op jit(solution)/shard_map/ppermute | solution.py:469
  55.0 4.8 %collective-permute-start.18 = (bf16[80,128]{1,0:T(8,128)(2,1)S(1)}, bf16[80,128]{1,0:T(8,128)(2,1)S(1)}, u32[]{:S(2)}, u32[]{:S(2)}) collective-permute-start(bf16[80,128]{1,0:T(8,128)(2,1)S(1)} %get-tuple-element.47.refs_4_), channel_id=1, source_target_pairs={{0,3},{1,2},{2,1},{3,0},{4,7},{5,6},{6,5},{7,4},{8,11},{9,10},{10,... | collective-permute-start | bytes 61448 | tf_op jit(solution)/shard_map/ppermute | solution.py:335
  56.9 3.8 %collective-permute-start.17 = (bf16[80,128]{1,0:T(8,128)(2,1)S(1)}, bf16[80,128]{1,0:T(8,128)(2,1)S(1)}, u32[]{:S(2)}, u32[]{:S(2)}) collective-permute-start(bf16[80,128]{1,0:T(8,128)(2,1)S(1)} %get-tuple-element.47.refs_4_), channel_id=1, source_target_pairs={{0,2},{1,3},{2,0},{3,1},{4,6},{5,7},{6,4},{7,5},{8,10},{9,11},{10,... | collective-permute-start | bytes 61448 | tf_op jit(solution)/shard_map/ppermute | solution.py:335
  57.3 3.8 %collective-permute-start.16 = (bf16[80,128]{1,0:T(8,128)(2,1)S(1)}, bf16[80,128]{1,0:T(8,128)(2,1)S(1)}, u32[]{:S(2)}, u32[]{:S(2)}) collective-permute-start(bf16[80,128]{1,0:T(8,128)(2,1)S(1)} %get-tuple-element.47.refs_4_), channel_id=1, source_target_pairs={{0,1},{1,0},{2,3},{3,2},{4,5},{5,4},{6,7},{7,6},{8,9},{9,8},{10,11... | collective-permute-start | bytes 61448 | tf_op jit(solution)/shard_map/ppermute | solution.py:335
